TPU v7x, 32 devices: a whole 2x2x4 slice. The times are simulated.
32 devices in a mesh: energy: 8 (over z, x), slab: 4 (over y, core).
Axes of the slice: x: 2, y: 2, z: 4, core: 2. Of those that a mesh axis runs over, the one named last changes fastest.
Arguments:
- onsite: float32 [4, 256], P('slab'), may hold values from -1 to 1
- hopping: float32 [4, 256, 256], P('slab'), may hold values from -0.12 to 0.12
- coupling: float32 [4, 256], P('slab'), may hold values from 0.4 to 0.8
- boundary_green: float32 [2, 4, 16, 256, 256], P(None, 'slab', 'energy'), may hold values from -0.09 to 0.09
- damping: float32 [4, 16], P('slab', 'energy'), may hold values from 1.5 to 6
- occupation: float32 [4, 16], P('slab', 'energy'), may hold values from 0 to 1
- tile_map: int32 [4, 128, 128], P('slab'), may hold values from 0 to 255
- prev_potential: float32 [4, 128, 128], P('slab'), may hold values from -6 to 6
Outputs:
- lesser_diag: float32 [4, 16, 256], P('slab', 'energy')
- potential: float32 [4, 128, 128], P('slab', 'energy')
All inputs are finite; a program needn't handle non-finite values.
Results may differ from a plain program's by a relative error of at most 0.0003.
Values sent between devices are 32-bit elements; how exact they have to be, the bound alone decides.
No kernel may reach another device: no remote copies, remote signals or barrier semaphores. Data moves between devices by JAX's collectives and lax.ppermute only.
A program may use at most 64 MiB of HBM per device.

v0:
```python
import functools

import jax
import jax.numpy as jnp
from jax import lax
from jax.experimental import pallas as pl
from jax.experimental.pallas import tpu as pltpu
from jax.sharding import PartitionSpec as P

SHIFT = 2
SWEEPS = 2
PHONON = 0.5
CHARGE = 2.0
ANISO = 0.05
SCREEN = 0.05
MAIN_DIAGONAL = 2.0 + 4.0 * ANISO + SCREEN
LANES = 128
SUBLANES = 8
HALO = 4
VMEM_BYTES = 48 * 1024 * 1024

f32 = jnp.float32
bf16 = jnp.bfloat16
DEVICES = ("energy", "slab")


def parts(matrix):
    high = matrix.astype(bf16)
    return high, (matrix - high.astype(f32)).astype(bf16)


def left_of(matrix):
    real, imag = parts(matrix[0]), parts(matrix[1])
    return [jnp.concatenate([r, i], axis=1) for r, i in zip(real, imag)]


def right_of(matrix):
    real, imag = parts(matrix[0]), parts(matrix[1])
    return [
        jnp.concatenate(
            [jnp.concatenate([r, i], axis=1), jnp.concatenate([-i, r], axis=1)], axis=0
        )
        for r, i in zip(real, imag)
    ]


def right_adjoint_of(matrix):
    real, imag = parts(matrix[0]), parts(matrix[1])
    return [
        jnp.concatenate(
            [jnp.concatenate([r, i], axis=1), jnp.concatenate([-i, r], axis=1)], axis=0
        )
        for r, i in zip(real, imag)
    ]


def product(left, right, transposed=False):
    contract = (((1,), (1 if transposed else 0,)), ((), ()))

    def dot(a, b):
        return lax.dot_general(a, b, contract, preferred_element_type=f32)

    out = dot(left[0], right[0]) + dot(left[1], right[0]) + dot(left[0], right[1])
    size = out.shape[1] // 2
    return out[:, :size], out[:, size:]


def add(*matrices):
    return sum(m[0] for m in matrices), sum(m[1] for m in matrices)


def as_column(row):
    size = row.shape[1]
    return jnp.broadcast_to(row, (SUBLANES, size)).T[:, 0:1]


def start_of(energy, onsite, damping):
    real = energy - onsite
    modulus = real * real + damping * damping
    present = damping > 0.0
    modulus = jnp.where(present, modulus, 1.0)
    return jnp.where(present, real / modulus, 0.0), jnp.where(present, -damping / modulus, 0.0)


def scale(matrix, factor):
    return (
        matrix[0] * factor[0] - matrix[1] * factor[1],
        matrix[0] * factor[1] + matrix[1] * factor[0],
    )


def invert(coupled, row, column):
    b1 = scale(coupled, row)
    b1_left = left_of(b1)
    b2 = product(b1_left, right_of(b1))
    b2_right = right_of(b2)
    b4 = product(left_of(b2), b2_right)
    b3 = product(b1_left, b2_right)
    t = add(b1, b2, b3)
    rest = product(left_of(t), right_of(b4))
    size = b1[0].shape[0]
    unit = (
        lax.broadcasted_iota(jnp.int32, (size, size), 0)
        == lax.broadcasted_iota(jnp.int32, (size, size), 1)
    ).astype(f32)
    total = add(t, b4, rest)
    return scale((unit + total[0], total[1]), column)


class Element:
    def __init__(self, message_ref, hopping_ref, onsite_ref, chain, total_energies):
        size = hopping_ref.shape[-1]
        parity = lax.rem(lax.axis_index("energy"), SHIFT)
        index = (SHIFT * chain + parity).astype(f32)
        energy = -2.0 + (4.0 / total_energies) * (index + 0.5)
        self.sigma = (message_ref[0, 0:size, :], message_ref[1, 0:size, :])
        damping = message_ref[0, size : size + 1, :]
        self.occupation = message_ref[0, size + 1 : size + 2, :]
        onsite = onsite_ref[...]
        self.row = start_of(energy, onsite, damping)
        self.column = tuple(as_column(part) for part in self.row)
        self.hopping = hopping_ref[0]

    def lesser_source(self):
        real, imag = self.sigma
        return -self.occupation * (real - real.T), -self.occupation * (imag + imag.T)

    def green(self, phonon=None):
        coupled = (self.hopping + self.sigma[0], self.sigma[1])
        if phonon is not None:
            coupled = add(coupled, phonon)
        return invert(coupled, self.row, self.column)

    def green_and_lesser(self):
        green = self.green()
        mixed = product(left_of(green), right_of(self.lesser_source()))
        lesser = product(left_of(mixed), right_adjoint_of(green), transposed=True)
        return green, lesser

    def lesser_row(self, greens, lessers):
        half = tuple(PHONON * part for part in add(*greens))
        green = self.green(half)
        source = add(self.lesser_source(), tuple(PHONON * part for part in add(*lessers)))
        mixed = product(left_of(green), right_of(source))
        column = jnp.sum(mixed[1] * green[0] - mixed[0] * green[1], axis=1, keepdims=True)
        return jnp.broadcast_to(column, (column.shape[0], LANES)).T[0:1, :]


def chain_places():
    here = lax.axis_index("energy")
    odd = lax.rem(here, 2)
    step = 1 - 2 * odd
    return {"own": here, "pair": here + step, "early": here + 2 * step, "late": here - step}


def vmem():
    return pl.BlockSpec(memory_space=pltpu.VMEM)


def smem():
    return pl.BlockSpec(memory_space=pltpu.SMEM)


def call(kernel, operands, specs, shapes, products=0, **options):
    several = isinstance(shapes, list)
    listed = shapes if several else [shapes]
    size = listed[0].shape[-1] if listed else 0
    bytes_moved = sum(x.size * 4 for x in operands) + sum(x.size * 4 for x in listed)
    return pl.pallas_call(
        kernel,
        out_shape=shapes,
        in_specs=specs,
        out_specs=[vmem() for _ in listed] if several else vmem(),
        compiler_params=pltpu.CompilerParams(vmem_limit_bytes=VMEM_BYTES),
        cost_estimate=pl.CostEstimate(
            flops=products * 24 * size**3, transcendentals=0, bytes_accessed=bytes_moved
        ),
        **options,
    )(*operands)


def split_blocks(boundary_green, coupling, parity):
    planes, _, _, rows, columns = boundary_green.shape

    def kernel(parity_ref, block_ref, coupling_ref, right_ref, left_ref):
        row = coupling_ref[...]
        block = block_ref[0, 0, 0]
        left_ref[0] = block
        right_ref[0] = block * row * as_column(row)

    shape = jax.ShapeDtypeStruct((planes, rows, columns), f32)
    out = pl.BlockSpec((1, rows, columns), lambda i, p: (i, 0, 0))
    return pl.pallas_call(
        kernel,
        out_shape=[shape, shape],
        grid_spec=pltpu.PrefetchScalarGridSpec(
            num_scalar_prefetch=1,
            grid=(planes,),
            in_specs=[
                pl.BlockSpec((1, 1, 1, rows, columns), lambda i, p: (i, 0, p[0], 0, 0)),
                pl.BlockSpec((1, columns), lambda i, p: (0, 0)),
            ],
            out_specs=[out, out],
        ),
    )(parity, boundary_green, coupling)


def self_energy_message(from_left, from_right, coupling, damping, occupation, own):
    planes, rows, columns = from_left.shape

    def kernel(left_ref, right_ref, coupling_ref, damping_ref, occupation_ref, out_ref):
        parity = lax.rem(lax.axis_index("energy"), SHIFT)
        parity = parity if own else 1 - parity
        row = coupling_ref[...]
        weight = row * as_column(row)
        for plane in range(planes):
            out_ref[plane, 0:rows, :] = left_ref[plane] + weight * right_ref[plane]
            which = lax.broadcasted_iota(jnp.int32, (SUBLANES, columns), 0)
            out_ref[plane, rows : rows + SUBLANES, :] = jnp.where(
                which == 0, damping_ref[0, parity], occupation_ref[0, parity]
            )

    return call(
        kernel,
        (from_left, from_right, coupling, damping, occupation),
        [vmem(), vmem(), vmem(), smem(), smem()],
        jax.ShapeDtypeStruct((planes, rows + SUBLANES, columns), f32),
    )


def green_and_lesser(message, hopping, onsite, place, total_energies):
    def kernel(message_ref, hopping_ref, onsite_ref, green_ref, lesser_ref):
        element = Element(
            message_ref, hopping_ref, onsite_ref, chain_places()[place], total_energies
        )
        green, lesser = element.green_and_lesser()
        for plane in range(2):
            green_ref[plane] = green[plane]
            lesser_ref[plane] = lesser[plane]

    size = hopping.shape[-1]
    shape = jax.ShapeDtypeStruct((2, size, size), f32)
    return call(
        kernel, (message, hopping, onsite), [vmem()] * 3, [shape, shape], products=6
    )


def second_pass(outer, inner, green, lesser, hopping, onsite, places, total_energies, other=None):
    size = hopping.shape[-1]
    count = lax.axis_size("energy") * lax.axis_size("slab")

    def kernel(outer_ref, inner_ref, green_ref, lesser_ref, hopping_ref, onsite_ref, *refs):
        chains = chain_places()
        beyond = Element(outer_ref, hopping_ref, onsite_ref, chains[places[0]], total_energies)
        here = Element(inner_ref, hopping_ref, onsite_ref, chains[places[1]], total_energies)
        beyond_green, beyond_lesser = beyond.green_and_lesser()
        row = here.lesser_row(
            [beyond_green, (green_ref[0], green_ref[1])],
            [beyond_lesser, (lesser_ref[0], lesser_ref[1])],
        )
        if other is None:
            refs[0][...] = row
        else:
            other_row = refs[0][...]
            odd = lax.rem(lax.axis_index("energy"), 2) == 1
            first = jnp.where(odd, other_row, row)
            second = jnp.where(odd, row, other_row)
            both = jnp.concatenate([first, second], axis=0)
            refs[1][...] = jnp.broadcast_to(both[None], refs[1].shape)

    operands = [outer, inner, green, lesser, hopping, onsite]
    if other is None:
        shape = jax.ShapeDtypeStruct((1, size), f32)
    else:
        operands.append(other)
        shape = jax.ShapeDtypeStruct((count, 2, size), f32)
    return call(kernel, operands, [vmem()] * len(operands), shape, products=11)


def grid_rows(tile_map, potential):
    rows = tile_map.shape[1] // lax.axis_size("energy")
    first = lax.axis_index("energy") * rows
    both = jnp.stack([tile_map[0].astype(f32), potential[0]])
    both = jnp.pad(both, ((0, 0), (HALO, HALO), (0, 0)))
    return lax.dynamic_slice_in_dim(both, first, rows + 2 * HALO, axis=1)


def relax(diagonals, turns, orbitals, total_energies, grid_total):
    energy_devices, slabs = diagonals.shape[:2]
    rows, columns = turns[0].shape[1:]
    rows_here = rows - 2 * HALO

    def kernel(diagonal_ref, *refs):
        turn_refs = refs[:slabs]
        lesser_ref, potential_ref, grid_ref = refs[slabs:]
        here, slab = lax.axis_index("energy"), lax.axis_index("slab")
        odd = lax.rem(here, 2)
        for parity in range(2):
            pair = diagonal_ref[here - odd + parity, slab]
            lesser_ref[0, parity : parity + 1, :] = jnp.where(odd == 1, pair[1:2], pair[0:1])
        for turn in range(slabs):
            grid_ref[lax.rem(slab - turn + slabs, slabs)] = turn_refs[turn][...]
        grid_row = (
            lax.broadcasted_iota(jnp.int32, (rows, columns), 0) + here * rows_here - HALO
        )
        inside = (grid_row >= 0) & (grid_row < grid_total)
        column = lax.broadcasted_iota(jnp.int32, (rows, columns), 1)
        sources, potentials = [], []
        for at in range(slabs):
            pair = diagonal_ref[0, at]
            for device in range(1, energy_devices):
                pair = pair + diagonal_ref[device, at]
            density = (4.0 / total_energies) * (pair[0:1] + pair[1:2])
            index = grid_ref[at, 0].astype(jnp.int32)
            found = jnp.zeros((rows, columns), f32)
            for low in range(0, orbitals, LANES):
                table = jnp.broadcast_to(density[:, low : low + LANES], (rows, LANES))
                inner = jnp.clip(index - low, 0, LANES - 1)
                value = jnp.take_along_axis(table, inner, axis=1)
                found = jnp.where((index >= low) & (index < low + LANES), value, found)
            sources.append(CHARGE * found)
            potentials.append(grid_ref[at, 1])
        pivots = [MAIN_DIAGONAL]
        for at in range(1, slabs):
            pivots.append(MAIN_DIAGONAL - 1.0 / pivots[-1])
        for sweep in range(SWEEPS):
            eliminated = []
            for at in range(slabs):
                p = potentials[at]
                beside = (
                    pltpu.roll(p, 1, 0)
                    + pltpu.roll(p, rows - 1, 0)
                    + jnp.where(column == 0, 0.0, pltpu.roll(p, 1, 1))
                    + jnp.where(column == columns - 1, 0.0, pltpu.roll(p, columns - 1, 1))
                )
                right = sources[at] + ANISO * beside
                if at:
                    right = right + (1.0 / pivots[at - 1]) * eliminated[-1]
                eliminated.append(right)
            after = None
            for at in reversed(range(slabs)):
                value = eliminated[at] if after is None else eliminated[at] + after
                after = value * (1.0 / pivots[at])
                potentials[at] = jnp.where(inside, after, 0.0)
        for at in range(slabs):
            grid_ref[at, 0] = potentials[at]
        potential_ref[0] = grid_ref[slab, 0, HALO : HALO + rows_here, :]

    return call(
        kernel,
        (diagonals, *turns),
        [vmem()] * (1 + slabs),
        [
            jax.ShapeDtypeStruct((1, 2, orbitals), f32),
            jax.ShapeDtypeStruct((1, rows_here, columns), f32),
        ],
        scratch_shapes=[pltpu.VMEM((slabs, 2, rows, columns), f32)],
    )


def per_device(
    onsite, hopping, coupling, boundary_green, damping, occupation, tile_map, prev_potential
):
    energy_devices, slabs = lax.axis_size("energy"), lax.axis_size("slab")
    orbitals = onsite.shape[1]
    assert boundary_green.shape[2] == SHIFT and energy_devices % 2 == 0
    total_energies = SHIFT * energy_devices
    odd = lax.rem(lax.axis_index("energy"), 2)

    up = [(i, i + 1) for i in range(slabs - 1)]
    down = [(i + 1, i) for i in range(slabs - 1)]
    last = energy_devices - 1
    pair = [(i, i ^ 1) for i in range(energy_devices)]
    near = [(i, i + 1 if i % 2 else i - 1) for i in range(1, last)]
    far = [(i, i + 2) for i in range(1, last, 2) if i + 2 <= last]
    far += [(i, i - 2) for i in range(2, energy_devices, 2)]

    def exchange(parity, own):
        right, left = split_blocks(boundary_green, coupling, parity[None])
        from_left = lax.ppermute(right, "slab", up)
        from_right = lax.ppermute(left, "slab", down)
        return self_energy_message(from_left, from_right, coupling, damping, occupation, own)

    other = exchange(1 - odd, False)
    mine = exchange(odd, True)
    turns = [grid_rows(tile_map, prev_potential)]
    for turn in range(1, slabs):
        ring = [(i, (i + turn) % slabs) for i in range(slabs)]
        turns.append(lax.ppermute(turns[0], "slab", ring))

    paired = lax.ppermute(other, "energy", pair)
    early = lax.ppermute(mine, "energy", far)
    late = lax.ppermute(other, "energy", near)

    common = (hopping, onsite)
    own_green, own_lesser = green_and_lesser(mine, *common, "own", total_energies)
    pair_green, pair_lesser = green_and_lesser(paired, *common, "pair", total_energies)
    pair_row = second_pass(
        early, paired, own_green, own_lesser, *common, ("early", "pair"), total_energies
    )
    rows = second_pass(
        late, mine, pair_green, pair_lesser, *common, ("late", "own"), total_energies, pair_row
    )
    diagonals = lax.all_to_all(rows, DEVICES, 0, 0)
    diagonals = diagonals.reshape(energy_devices, slabs, 2, orbitals)
    lesser, potential = relax(diagonals, turns, orbitals, total_energies, tile_map.shape[1])
    return lesser, potential


def solution(mesh):
    in_specs = (
        P("slab", None),
        P("slab", None, None),
        P("slab", None),
        P(None, "slab", "energy", None, None),
        P("slab", "energy"),
        P("slab", "energy"),
        P("slab", None, None),
        P("slab", None, None),
    )
    out_specs = (P("slab", "energy", None), P("slab", "energy", None))
    return jax.shard_map(
        per_device, mesh=mesh, in_specs=in_specs, out_specs=out_specs, check_vma=False
    )
```

profile of v0, /device:TPU:0, one launch (start us, length us, event | category | flops | bytes accessed | tf_op | source)
XLA Modules:
  0.0 67.9 jit_solution(9543101906591662992)
XLA Ops:
  0.6 2.2 %shard_map.95 = (f32[2,256,256]{2,1,0:T(8,128)}, f32[2,256,256]{2,1,0:T(8,128)}) custom-call(s32[1]{0:T(128)} %bitcast.parity_ref, f32[2,1,2,256,256]{4,3,2,1,0:T(8,128)} %block_ref.3, f32[1,256]{1,0:T(1,128)} %coupling_ref.7), custom_call_target="tpu_custom_call" | custom-call | tf_op jit(solution)/shard_map/pallas_call | solution.py:193
  2.9 2.4 %collective-permute-start = (f32[2,256,256]{2,1,0:T(8,128)}, f32[2,256,256]{2,1,0:T(8,128)S(1)}, u32[]{:S(2)}, u32[]{:S(2)}) collective-permute-start(f32[2,256,256]{2,1,0:T(8,128)} %get-tuple-element.10), channel_id=1, source_target_pairs={{0,1},{1,2},{2,3},{4,5},{5,6},{6,7},{8,9},{9,10},{10,11},{12,13},{... | collective-permute-start | bytes 1572872 | tf_op jit(solution)/shard_map/ppermute | solution.py:380
  5.3 1.3 %collective-permute-start.1 = (f32[2,256,256]{2,1,0:T(8,128)}, f32[2,256,256]{2,1,0:T(8,128)S(1)}, u32[]{:S(2)}, u32[]{:S(2)}) collective-permute-start(f32[2,256,256]{2,1,0:T(8,128)} %get-tuple-element.11), channel_id=1, source_target_pairs={{1,0},{2,1},{3,2},{5,4},{6,5},{7,6},{9,8},{10,9},{11,10},{13,12},{... | collective-permute-start | bytes 1572872 | tf_op jit(solution)/shard_map/ppermute | solution.py:381
  6.6 2.2 %shard_map.97 = (f32[2,256,256]{2,1,0:T(8,128)}, f32[2,256,256]{2,1,0:T(8,128)}) custom-call(s32[1]{0:T(128)} %bitcast.1.parity_ref, f32[2,1,2,256,256]{4,3,2,1,0:T(8,128)} %block_ref.3, f32[1,256]{1,0:T(1,128)} %coupling_ref.7), custom_call_target="tpu_custom_call" | custom-call | tf_op jit(solution)/shard_map/pallas_call | solution.py:193
  8.8 0.0 copy-start.2
  8.8 0.0 copy-start
  8.8 0.0 copy-start.1
  8.8 5.3 %collective-permute-start.3 = (f32[2,256,256]{2,1,0:T(8,128)}, f32[2,256,256]{2,1,0:T(8,128)S(1)}, u32[]{:S(2)}, u32[]{:S(2)}) collective-permute-start(f32[2,256,256]{2,1,0:T(8,128)} %get-tuple-element.12), channel_id=1, source_target_pairs={{0,1},{1,2},{2,3},{4,5},{5,6},{6,7},{8,9},{9,10},{10,11},{12,13},{... | collective-permute-start | bytes 1572872 | tf_op jit(solution)/shard_map/ppermute | solution.py:380
  14.1 1.3 %collective-permute-start.4 = (f32[2,256,256]{2,1,0:T(8,128)}, f32[2,256,256]{2,1,0:T(8,128)S(1)}, u32[]{:S(2)}, u32[]{:S(2)}) collective-permute-start(f32[2,256,256]{2,1,0:T(8,128)} %get-tuple-element.13), channel_id=1, source_target_pairs={{1,0},{2,1},{3,2},{5,4},{6,5},{7,6},{9,8},{10,9},{11,10},{13,12},{... | collective-permute-start | bytes 1572872 | tf_op jit(solution)/shard_map/ppermute | solution.py:381
  15.4 0.0 collective-permute-done.left_ref
  15.4 0.0 collective-permute-done.1.right_ref
  15.4 0.0 copy-done.2
  15.4 0.0 copy-done
  15.4 0.0 copy-done.1
  15.4 0.8 %shard_map.96 = f32[2,264,256]{2,1,0:T(8,128)S(1)} custom-call(f32[2,256,256]{2,1,0:T(8,128)S(1)} %collective-permute-done.left_ref, f32[2,256,256]{2,1,0:T(8,128)S(1)} %collective-permute-done.1.right_ref, f32[1,256]{1,0:T(1,128)S(1)} %copy-done, f32[1,2]{1,0:T(1,128)S(1)} %copy-done.1, f32[1,2]{1,0:T(1,128)S(1)} %copy-done.2), custom_call_target="tpu_custom_call" | custom-call | bytes 1590288 | tf_op jit(solution)/shard_map/pallas_call | solution.py:169
  16.2 0.0 copy-start.5
  16.3 0.0 copy-start.3
  16.3 1.6 %collective-permute-start.5 = (f32[2,264,256]{2,1,0:T(8,128)S(1)}, f32[2,264,256]{2,1,0:T(8,128)S(1)}, u32[]{:S(2)}, u32[]{:S(2)}) collective-permute-start(f32[2,264,256]{2,1,0:T(8,128)S(1)} %shard_map.96), channel_id=1, source_target_pairs={{0,4},{4,0},{8,12},{12,8},{16,20},{20,16},{24,28},{28,24},{1,5},{5... | collective-permute-start | bytes 1622024 | tf_op jit(solution)/shard_map/ppermute | solution.py:391
  17.8 0.0 collective-permute-done.3.left_ref
  17.8 1.5 %collective-permute-done.4.right_ref = f32[2,256,256]{2,1,0:T(8,128)S(1)} collective-permute-done((f32[2,256,256]{2,1,0:T(8,128)}, f32[2,256,256]{2,1,0:T(8,128)S(1)}, u32[]{:S(2)}, u32[]{:S(2)}) %collective-permute-start.4) | collective-permute-done | bytes 524320 | tf_op jit(solution)/shard_map/ppermute | solution.py:381
  19.3 0.8 %shard_map.98.message_ref.inner_ref = f32[2,264,256]{2,1,0:T(8,128)S(1)} custom-call(f32[2,256,256]{2,1,0:T(8,128)S(1)} %collective-permute-done.3.left_ref, f32[2,256,256]{2,1,0:T(8,128)S(1)} %collective-permute-done.4.right_ref, f32[1,256]{1,0:T(1,128)S(1)} %copy-done, f32[1,2]{1,0:T(1,128)S(1)} %copy-done.1, f32[1,2]{1,0:T(1,128)S(1)} %copy-done.2), custom_call_target="tpu_custom_call" | custom-call | bytes 1590288 | tf_op jit(solution)/shard_map/pallas_call | solution.py:169
  20.1 1.3 %collective-permute-start.6 = (f32[2,264,256]{2,1,0:T(8,128)S(1)}, f32[2,264,256]{2,1,0:T(8,128)S(1)}, u32[]{:S(2)}, u32[]{:S(2)}) collective-permute-start(f32[2,264,256]{2,1,0:T(8,128)S(1)} %shard_map.98.message_ref.inner_ref), channel_id=1, source_target_pairs={{4,12},{12,20},{20,28},{8,0},{16,8},{24,16},{5,13},{13,21},{21,29}... | collective-permute-start | bytes 1622024 | tf_op jit(solution)/shard_map/ppermute | solution.py:392
  21.4 0.0 copy-done.5
  21.4 0.0 copy-start.4
  21.5 0.7 %collective-permute-start.2 = (f32[2,264,256]{2,1,0:T(8,128)S(1)}, f32[2,264,256]{2,1,0:T(8,128)S(1)}, u32[]{:S(2)}, u32[]{:S(2)}) collective-permute-start(f32[2,264,256]{2,1,0:T(8,128)S(1)} %shard_map.96), channel_id=1, source_target_pairs={{4,8},{8,4},{12,16},{16,12},{20,24},{24,20},{5,9},{9,5},{13,17},{1... | collective-permute-start | bytes 1622024 | tf_op jit(solution)/shard_map/ppermute | solution.py:393
  22.2 0.0 copy-done.3
  22.2 0.0 copy-done.4
  22.2 3.1 %shard_map.100 = (f32[2,256,256]{2,1,0:T(8,128)S(1)}, f32[2,256,256]{2,1,0:T(8,128)S(1)}) custom-call(f32[2,264,256]{2,1,0:T(8,128)S(1)} %shard_map.98.message_ref.inner_ref, f32[1,256,256]{2,1,0:T(8,128)S(1)} %copy-done.3, f32[1,256]{1,0:T(1,128)S(1)} %copy-done.4), custom_call_target="tpu_custom_call" | custom-call | flops 2415919104 | bytes 1852416 | tf_op jit(solution)/shard_map/pallas_call | solution.py:169
  25.3 3.9 %collective-permute-done.5.message_ref.inner_ref = f32[2,264,256]{2,1,0:T(8,128)S(1)} collective-permute-done((f32[2,264,256]{2,1,0:T(8,128)S(1)}, f32[2,264,256]{2,1,0:T(8,128)S(1)}, u32[]{:S(2)}, u32[]{:S(2)}) %collective-permute-start.5) | collective-permute-done | bytes 540704 | tf_op jit(solution)/shard_map/ppermute | solution.py:391
  29.3 3.1 %shard_map.99 = (f32[2,256,256]{2,1,0:T(8,128)S(1)}, f32[2,256,256]{2,1,0:T(8,128)S(1)}) custom-call(f32[2,264,256]{2,1,0:T(8,128)S(1)} %collective-permute-done.5.message_ref.inner_ref, f32[1,256,256]{2,1,0:T(8,128)S(1)} %copy-done.3, f32[1,256]{1,0:T(1,128)S(1)} %copy-done.4), custom_call_target="tpu_custom_call" | custom-call | flops 2415919104 | bytes 1852416 | tf_op jit(solution)/shard_map/pallas_call | solution.py:169
  32.4 0.0 collective-permute-done.6.outer_ref
  32.4 5.8 %shard_map.101.refs_0_ = f32[1,256]{1,0:T(1,128)S(1)} custom-call(f32[2,264,256]{2,1,0:T(8,128)S(1)} %collective-permute-done.6.outer_ref, f32[2,264,256]{2,1,0:T(8,128)S(1)} %collective-permute-done.5.message_ref.inner_ref, f32[2,256,256]{2,1,0:T(8,128)S(1)} %get-tuple-element.16.green_ref, f32[2,256,256]{2,1,0:T(8,128)S(1)} %get-tuple-element.17.lesser_ref, ...), custom_call_target="tpu_custom_call" | custom-call | flops 4429185024 | bytes 2394112 | tf_op jit(solution)/shard_map/pallas_call | solution.py:169
  38.2 0.0 collective-permute-done.2.outer_ref
  38.2 6.5 %shard_map.102 = f32[32,2,256]{2,1,0:T(2,128)} custom-call(f32[2,264,256]{2,1,0:T(8,128)S(1)} %collective-permute-done.2.outer_ref, f32[2,264,256]{2,1,0:T(8,128)S(1)} %shard_map.98.message_ref.inner_ref, f32[2,256,256]{2,1,0:T(8,128)S(1)} %get-tuple-element.14.green_ref, f32[2,256,256]{2,1,0:T(8,128)S(1)} %get-tuple-element.15.lesser_ref, ...), custom_call_target="tpu_custom_call" | custom-call | flops 4429185024 | bytes 2459648 | tf_op jit(solution)/shard_map/pallas_call | solution.py:169
  44.7 0.0 copy-start.6
  44.7 14.9 %all-to-all-start = ((f32[32,2,256]{2,1,0:T(2,128)}), f32[32,2,256]{2,1,0:T(2,128)S(1)}, u32[]{:S(2)}, u32[]{:S(2)}) async-start(f32[32,2,256]{2,1,0:T(2,128)} %shard_map.102), calls=%async_computation | async-start | bytes 131072 | tf_op jit(solution)/shard_map/all_to_all | solution.py:404
  59.6 0.0 copy-done.6
  59.6 0.3 collective-permute-start.7
  59.9 1.7 %collective-permute-start.8 = (f32[2,24,128]{2,1,0:T(8,128)S(1)}, f32[2,24,128]{2,1,0:T(8,128)S(1)}, u32[]{:S(2)}, u32[]{:S(2)}) collective-permute-start(f32[2,24,128]{2,1,0:T(8,128)S(1)} %fusion.1.refs_0_), channel_id=1, source_target_pairs={{0,2},{1,3},{2,0},{3,1},{4,6},{5,7},{6,4},{7,5},{8,10},{9,11},{10,... | collective-permute-start | bytes 73736 | tf_op jit(solution)/shard_map/ppermute | solution.py:389
  61.6 1.3 %collective-permute-start.9 = (f32[2,24,128]{2,1,0:T(8,128)S(1)}, f32[2,24,128]{2,1,0:T(8,128)S(1)}, u32[]{:S(2)}, u32[]{:S(2)}) collective-permute-start(f32[2,24,128]{2,1,0:T(8,128)S(1)} %fusion.1.refs_0_), channel_id=1, source_target_pairs={{0,3},{1,0},{2,1},{3,2},{4,7},{5,4},{6,5},{7,6},{8,11},{9,8},{10,9... | collective-permute-start | bytes 73736 | tf_op jit(solution)/shard_map/ppermute | solution.py:389
  62.9 0.0 collective-permute-done.7.refs_1_
  62.9 0.8 %collective-permute-done.8.refs_2_ = f32[2,24,128]{2,1,0:T(8,128)S(1)} collective-permute-done((f32[2,24,128]{2,1,0:T(8,128)S(1)}, f32[2,24,128]{2,1,0:T(8,128)S(1)}, u32[]{:S(2)}, u32[]{:S(2)}) %collective-permute-start.8) | collective-permute-done | bytes 24608 | tf_op jit(solution)/shard_map/ppermute | solution.py:389
  63.8 0.7 collective-permute-done.9.refs_3_
  64.4 2.5 %all-to-all-done = f32[32,2,256]{2,1,0:T(2,128)S(1)} async-done(((f32[32,2,256]{2,1,0:T(2,128)}), f32[32,2,256]{2,1,0:T(2,128)S(1)}, u32[]{:S(2)}, u32[]{:S(2)}) %all-to-all-start) | async-done | bytes 65568 | tf_op jit(solution)/shard_map/all_to_all | solution.py:404
  67.0 0.9 %shard_map.103 = (f32[1,2,256]{2,1,0:T(2,128)}, f32[1,16,128]{2,1,0:T(8,128)}) custom-call(f32[8,4,2,256]{3,2,1,0:T(2,128)S(1)} %bitcast.3, f32[2,24,128]{2,1,0:T(8,128)S(1)} %fusion.1.refs_0_, f32[2,24,128]{2,1,0:T(8,128)S(1)} %collective-permute-done.7.refs_1_, f32[2,24,128]{2,1,0:T(8,128)S(1)} %collective-permute-done.8.refs_2_, ...), custom_call_target="tpu_custom_call" | custom-call | bytes 174080 | tf_op jit(solution)/shard_map/pallas_call | solution.py:169
  (2 shorter events, 0.0 us)
Async XLA Ops:
  2.9 12.5 %collective-permute-start = (f32[2,256,256]{2,1,0:T(8,128)}, f32[2,256,256]{2,1,0:T(8,128)S(1)}, u32[]{:S(2)}, u32[]{:S(2)}) collective-permute-start(f32[2,256,256]{2,1,0:T(8,128)} %get-tuple-element.10), channel_id=1, source_target_pairs={{0,1},{1,2},{2,3},{4,5},{5,6},{6,7},{8,9},{9,10},{10,11},{12,13},{... | collective-permute-start | bytes 1572872 | tf_op jit(solution)/shard_map/ppermute | solution.py:380
  5.3 10.1 %collective-permute-start.1 = (f32[2,256,256]{2,1,0:T(8,128)}, f32[2,256,256]{2,1,0:T(8,128)S(1)}, u32[]{:S(2)}, u32[]{:S(2)}) collective-permute-start(f32[2,256,256]{2,1,0:T(8,128)} %get-tuple-element.11), channel_id=1, source_target_pairs={{1,0},{2,1},{3,2},{5,4},{6,5},{7,6},{9,8},{10,9},{11,10},{13,12},{... | collective-permute-start | bytes 1572872 | tf_op jit(solution)/shard_map/ppermute | solution.py:381
  8.8 6.6 %copy-start.2 = (f32[1,2]{1,0:T(1,128)S(1)}, f32[1,2]{1,0:T(1,128)}, u32[]{:S(2)}) copy-start(f32[1,2]{1,0:T(1,128)} %occupation_ref.3) | copy-start | bytes 28
  8.8 6.7 %copy-start = (f32[1,256]{1,0:T(1,128)S(1)}, f32[1,256]{1,0:T(1,128)}, u32[]{:S(2)}) copy-start(f32[1,256]{1,0:T(1,128)} %coupling_ref.7) | copy-start | bytes 3076
  8.8 6.7 %copy-start.1 = (f32[1,2]{1,0:T(1,128)S(1)}, f32[1,2]{1,0:T(1,128)}, u32[]{:S(2)}) copy-start(f32[1,2]{1,0:T(1,128)} %damping_ref.3) | copy-start | bytes 28
  8.8 9.0 %collective-permute-start.3 = (f32[2,256,256]{2,1,0:T(8,128)}, f32[2,256,256]{2,1,0:T(8,128)S(1)}, u32[]{:S(2)}, u32[]{:S(2)}) collective-permute-start(f32[2,256,256]{2,1,0:T(8,128)} %get-tuple-element.12), channel_id=1, source_target_pairs={{0,1},{1,2},{2,3},{4,5},{5,6},{6,7},{8,9},{9,10},{10,11},{12,13},{... | collective-permute-start | bytes 1572872 | tf_op jit(solution)/shard_map/ppermute | solution.py:380
  14.1 5.2 %collective-permute-start.4 = (f32[2,256,256]{2,1,0:T(8,128)}, f32[2,256,256]{2,1,0:T(8,128)S(1)}, u32[]{:S(2)}, u32[]{:S(2)}) collective-permute-start(f32[2,256,256]{2,1,0:T(8,128)} %get-tuple-element.13), channel_id=1, source_target_pairs={{1,0},{2,1},{3,2},{5,4},{6,5},{7,6},{9,8},{10,9},{11,10},{13,12},{... | collective-permute-start | bytes 1572872 | tf_op jit(solution)/shard_map/ppermute | solution.py:381
  16.2 5.2 %copy-start.5 = (s32[1,128,128]{2,1,0:T(8,128)S(1)}, s32[1,128,128]{2,1,0:T(8,128)}, u32[]{:S(2)}) copy-start(s32[1,128,128]{2,1,0:T(8,128)} %param.14) | copy-start | bytes 196612
  16.3 5.9 %copy-start.3 = (f32[1,256,256]{2,1,0:T(8,128)S(1)}, f32[1,256,256]{2,1,0:T(8,128)}, u32[]{:S(2)}) copy-start(f32[1,256,256]{2,1,0:T(8,128)} %hopping_ref.7) | copy-start | bytes 786436
  16.3 13.0 %collective-permute-start.5 = (f32[2,264,256]{2,1,0:T(8,128)S(1)}, f32[2,264,256]{2,1,0:T(8,128)S(1)}, u32[]{:S(2)}, u32[]{:S(2)}) collective-permute-start(f32[2,264,256]{2,1,0:T(8,128)S(1)} %shard_map.96), channel_id=1, source_target_pairs={{0,4},{4,0},{8,12},{12,8},{16,20},{20,16},{24,28},{28,24},{1,5},{5... | collective-permute-start | bytes 1622024 | tf_op jit(solution)/shard_map/ppermute | solution.py:391
  20.1 12.3 %collective-permute-start.6 = (f32[2,264,256]{2,1,0:T(8,128)S(1)}, f32[2,264,256]{2,1,0:T(8,128)S(1)}, u32[]{:S(2)}, u32[]{:S(2)}) collective-permute-start(f32[2,264,256]{2,1,0:T(8,128)S(1)} %shard_map.98.message_ref.inner_ref), channel_id=1, source_target_pairs={{4,12},{12,20},{20,28},{8,0},{16,8},{24,16},{5,13},{13,21},{21,29}... | collective-permute-start | bytes 1622024 | tf_op jit(solution)/shard_map/ppermute | solution.py:392
  21.4 0.7 %copy-start.4 = (f32[1,256]{1,0:T(1,128)S(1)}, f32[1,256]{1,0:T(1,128)}, u32[]{:S(2)}) copy-start(f32[1,256]{1,0:T(1,128)} %onsite_ref.7) | copy-start | bytes 3076
  21.5 16.7 %collective-permute-start.2 = (f32[2,264,256]{2,1,0:T(8,128)S(1)}, f32[2,264,256]{2,1,0:T(8,128)S(1)}, u32[]{:S(2)}, u32[]{:S(2)}) collective-permute-start(f32[2,264,256]{2,1,0:T(8,128)S(1)} %shard_map.96), channel_id=1, source_target_pairs={{4,8},{8,4},{12,16},{16,12},{20,24},{24,20},{5,9},{9,5},{13,17},{1... | collective-permute-start | bytes 1622024 | tf_op jit(solution)/shard_map/ppermute | solution.py:393
  44.7 14.9 %copy-start.6 = (f32[1,128,128]{2,1,0:T(8,128)S(1)}, f32[1,128,128]{2,1,0:T(8,128)}, u32[]{:S(2)}) copy-start(f32[1,128,128]{2,1,0:T(8,128)} %param.15) | copy-start | bytes 196612
  44.7 22.3 %all-to-all-start = ((f32[32,2,256]{2,1,0:T(2,128)}), f32[32,2,256]{2,1,0:T(2,128)S(1)}, u32[]{:S(2)}, u32[]{:S(2)}) async-start(f32[32,2,256]{2,1,0:T(2,128)} %shard_map.102), calls=%async_computation | async-start | bytes 131072 | tf_op jit(solution)/shard_map/all_to_all | solution.py:404
  59.6 3.3 %collective-permute-start.7 = (f32[2,24,128]{2,1,0:T(8,128)S(1)}, f32[2,24,128]{2,1,0:T(8,128)S(1)}, u32[]{:S(2)}, u32[]{:S(2)}) collective-permute-start(f32[2,24,128]{2,1,0:T(8,128)S(1)} %fusion.1.refs_0_), channel_id=1, source_target_pairs={{0,1},{1,2},{2,3},{3,0},{4,5},{5,6},{6,7},{7,4},{8,9},{9,10},{10,1... | collective-permute-start | bytes 73736 | tf_op jit(solution)/shard_map/ppermute | solution.py:389
  59.9 3.8 %collective-permute-start.8 = (f32[2,24,128]{2,1,0:T(8,128)S(1)}, f32[2,24,128]{2,1,0:T(8,128)S(1)}, u32[]{:S(2)}, u32[]{:S(2)}) collective-permute-start(f32[2,24,128]{2,1,0:T(8,128)S(1)} %fusion.1.refs_0_), channel_id=1, source_target_pairs={{0,2},{1,3},{2,0},{3,1},{4,6},{5,7},{6,4},{7,5},{8,10},{9,11},{10,... | collective-permute-start | bytes 73736 | tf_op jit(solution)/shard_map/ppermute | solution.py:389
  61.6 2.9 %collective-permute-start.9 = (f32[2,24,128]{2,1,0:T(8,128)S(1)}, f32[2,24,128]{2,1,0:T(8,128)S(1)}, u32[]{:S(2)}, u32[]{:S(2)}) collective-permute-start(f32[2,24,128]{2,1,0:T(8,128)S(1)} %fusion.1.refs_0_), channel_id=1, source_target_pairs={{0,3},{1,0},{2,1},{3,2},{4,7},{5,4},{6,5},{7,6},{8,11},{9,8},{10,9... | collective-permute-start | bytes 73736 | tf_op jit(solution)/shard_map/ppermute | solution.py:389
where the time goes:
time: 68.2 us; the launch traced here: 67.9 us
  starting transfers between devices  32 us (47%)
  Pallas kernels  25.5 us (37%)
  waiting for transfers between devices  9.49 us (14%)
  between operations  0.87 us (1%)
    pallas_call x7, Pallas kernels, call(): pl.pallas_call(kernel, out_shape=shapes, in_specs=specs, out_specs=[vmem(...  21 us
    all_to_all x1, starting transfers between devices, per_device(): diagonals = lax.all_to_all(rows, DEVICES, 0, 0)  14.9 us
    ppermute x2, starting transfers between devices, exchange(): from_left = lax.ppermute(right, 'slab', up)  7.67 us
    pallas_call x2, Pallas kernels, split_blocks(): pl.pallas_call(kernel, out_shape=[shape, shape], grid_spec=pltpu.Prefetch...  4.44 us
    ppermute x1, waiting for transfers between devices, per_device(): paired = lax.ppermute(other, 'energy', pair)  3.93 us
    ppermute x3, starting transfers between devices, per_device(): turns.append(lax.ppermute(turns[0], 'slab', ring))  3.3 us
    ppermute x2, starting transfers between devices, exchange(): from_right = lax.ppermute(left, 'slab', down)  2.58 us
    all_to_all x1, waiting for transfers between devices, per_device(): diagonals = lax.all_to_all(rows, DEVICES, 0, 0)  2.55 us
  transfers between devices with their start and end apart: 11, of which 5 were waited for; matrix products, arithmetic and copies ran while one was open for 0% of the time, Pallas kernels for 23%

commit v1 on v0

--- a/solution.py
+++ b/solution.py
@@ -29,40 +29,31 @@
     return high, (matrix - high.astype(f32)).astype(bf16)
 
 
-def left_of(matrix):
-    real, imag = parts(matrix[0]), parts(matrix[1])
-    return [jnp.concatenate([r, i], axis=1) for r, i in zip(real, imag)]
-
-
-def right_of(matrix):
-    real, imag = parts(matrix[0]), parts(matrix[1])
-    return [
-        jnp.concatenate(
-            [jnp.concatenate([r, i], axis=1), jnp.concatenate([-i, r], axis=1)], axis=0
-        )
-        for r, i in zip(real, imag)
+def dot(left, right, transposed=False):
+    contract = (((1,), (1 if transposed else 0,)), ((), ()))
+    out = [
+        lax.dot_general(left[i], right[j], contract, preferred_element_type=f32)
+        for i, j in ((0, 0), (1, 0), (0, 1))
     ]
-
-
-def right_adjoint_of(matrix):
-    real, imag = parts(matrix[0]), parts(matrix[1])
-    return [
-        jnp.concatenate(
-            [jnp.concatenate([r, i], axis=1), jnp.concatenate([-i, r], axis=1)], axis=0
-        )
-        for r, i in zip(real, imag)
-    ]
-
-
-def product(left, right, transposed=False):
-    contract = (((1,), (1 if transposed else 0,)), ((), ()))
-
-    def dot(a, b):
-        return lax.dot_general(a, b, contract, preferred_element_type=f32)
-
-    out = dot(left[0], right[0]) + dot(left[1], right[0]) + dot(left[0], right[1])
-    size = out.shape[1] // 2
-    return out[:, :size], out[:, size:]
+    return out[0] + out[1] + out[2]
+
+
+def factor(matrix):
+    return parts(matrix[0]), parts(matrix[1]), parts(matrix[0] + matrix[1])
+
+
+def adjoint_factor(matrix):
+    return parts(matrix[0]), parts(matrix[1]), parts(matrix[0] - matrix[1])
+
+
+def product(left, right):
+    real, imag, both = (dot(a, b) for a, b in zip(left, right))
+    return real - imag, both - real - imag
+
+
+def adjoint_product(left, right):
+    real, imag, both = (dot(a, b, transposed=True) for a, b in zip(left, right))
+    return real + imag, both - real + imag
 
 
 def add(*matrices):
@@ -91,13 +82,13 @@
 
 def invert(coupled, row, column):
     b1 = scale(coupled, row)
-    b1_left = left_of(b1)
-    b2 = product(b1_left, right_of(b1))
-    b2_right = right_of(b2)
-    b4 = product(left_of(b2), b2_right)
-    b3 = product(b1_left, b2_right)
+    b1_factor = factor(b1)
+    b2 = product(b1_factor, b1_factor)
+    b2_factor = factor(b2)
+    b4 = product(b2_factor, b2_factor)
+    b3 = product(b1_factor, b2_factor)
     t = add(b1, b2, b3)
-    rest = product(left_of(t), right_of(b4))
+    rest = product(factor(t), factor(b4))
     size = b1[0].shape[0]
     unit = (
         lax.broadcasted_iota(jnp.int32, (size, size), 0)
@@ -133,16 +124,18 @@
 
     def green_and_lesser(self):
         green = self.green()
-        mixed = product(left_of(green), right_of(self.lesser_source()))
-        lesser = product(left_of(mixed), right_adjoint_of(green), transposed=True)
-        return green, lesser
+        mixed = product(factor(green), factor(self.lesser_source()))
+        return green, adjoint_product(factor(mixed), adjoint_factor(green))
 
     def lesser_row(self, greens, lessers):
         half = tuple(PHONON * part for part in add(*greens))
         green = self.green(half)
         source = add(self.lesser_source(), tuple(PHONON * part for part in add(*lessers)))
-        mixed = product(left_of(green), right_of(source))
-        column = jnp.sum(mixed[1] * green[0] - mixed[0] * green[1], axis=1, keepdims=True)
+        real, imag = parts(green[0]), parts(green[1])
+        source_real, source_imag = parts(source[0]), parts(source[1])
+        terms = green[0] * dot(real, source_imag) + green[1] * dot(imag, source_imag)
+        terms = terms - 2.0 * green[1] * dot(real, source_real)
+        column = jnp.sum(terms, axis=1, keepdims=True)
         return jnp.broadcast_to(column, (column.shape[0], LANES)).T[0:1, :]
 
 
@@ -173,59 +166,83 @@
         out_specs=[vmem() for _ in listed] if several else vmem(),
         compiler_params=pltpu.CompilerParams(vmem_limit_bytes=VMEM_BYTES),
         cost_estimate=pl.CostEstimate(
-            flops=products * 24 * size**3, transcendentals=0, bytes_accessed=bytes_moved
+            flops=0, transcendentals=0, bytes_accessed=0
         ),
         **options,
     )(*operands)
 
 
-def split_blocks(boundary_green, coupling, parity):
+def block_messages(boundary_green, coupling, damping, occupation):
     planes, _, _, rows, columns = boundary_green.shape
 
-    def kernel(parity_ref, block_ref, coupling_ref, right_ref, left_ref):
-        row = coupling_ref[...]
-        block = block_ref[0, 0, 0]
-        left_ref[0] = block
-        right_ref[0] = block * row * as_column(row)
-
-    shape = jax.ShapeDtypeStruct((planes, rows, columns), f32)
-    out = pl.BlockSpec((1, rows, columns), lambda i, p: (i, 0, 0))
-    return pl.pallas_call(
-        kernel,
-        out_shape=[shape, shape],
-        grid_spec=pltpu.PrefetchScalarGridSpec(
-            num_scalar_prefetch=1,
-            grid=(planes,),
-            in_specs=[
-                pl.BlockSpec((1, 1, 1, rows, columns), lambda i, p: (i, 0, p[0], 0, 0)),
-                pl.BlockSpec((1, columns), lambda i, p: (0, 0)),
-            ],
-            out_specs=[out, out],
-        ),
-    )(parity, boundary_green, coupling)
-
-
-def self_energy_message(from_left, from_right, coupling, damping, occupation, own):
-    planes, rows, columns = from_left.shape
-
-    def kernel(left_ref, right_ref, coupling_ref, damping_ref, occupation_ref, out_ref):
+    def kernel(block_ref, coupling_ref, *refs):
+        level_refs, other_ref, own_ref, held_refs, sems = refs[:2], refs[2], refs[3], refs[4:6], refs[6]
         parity = lax.rem(lax.axis_index("energy"), SHIFT)
-        parity = parity if own else 1 - parity
-        row = coupling_ref[...]
-        weight = row * as_column(row)
-        for plane in range(planes):
-            out_ref[plane, 0:rows, :] = left_ref[plane] + weight * right_ref[plane]
-            which = lax.broadcasted_iota(jnp.int32, (SUBLANES, columns), 0)
-            out_ref[plane, rows : rows + SUBLANES, :] = jnp.where(
-                which == 0, damping_ref[0, parity], occupation_ref[0, parity]
-            )
-
+        moves = []
+        for which, out_ref in ((1 - parity, other_ref), (parity, own_ref)):
+            for plane in range(planes):
+                moves.append(
+                    (block_ref.at[plane, 0, which], out_ref.at[plane, pl.ds(0, rows)])
+                )
+        moves.append((coupling_ref, own_ref.at[0, pl.ds(rows, 1)]))
+        moves += list(zip(level_refs, held_refs))
+        copies = [
+            pltpu.make_async_copy(source, target, sems.at[at])
+            for at, (source, target) in enumerate(moves)
+        ]
+        for copy in copies:
+            copy.start()
+        for copy in copies:
+            copy.wait()
+        levels = [
+            jnp.where(parity == 0, held_ref[0:1, 1:2], held_ref[0:1, 0:1]) for held_ref in held_refs
+        ]
+        which = lax.broadcasted_iota(jnp.int32, (SUBLANES, columns), 0)
+        other_ref[0, rows:, :] = jnp.where(which == 0, levels[0], levels[1])
+
+    operands = (boundary_green, coupling, damping, occupation)
+    shape = jax.ShapeDtypeStruct((planes, rows + SUBLANES, columns), f32)
     return call(
         kernel,
-        (from_left, from_right, coupling, damping, occupation),
-        [vmem(), vmem(), vmem(), smem(), smem()],
-        jax.ShapeDtypeStruct((planes, rows + SUBLANES, columns), f32),
-    )
+        [pltpu.with_memory_space_constraint(x, pltpu.HBM) for x in operands],
+        [pl.BlockSpec(memory_space=pltpu.HBM)] * 4,
+        [shape, shape],
+        scratch_shapes=[
+            pltpu.VMEM(damping.shape, f32),
+            pltpu.VMEM(damping.shape, f32),
+            pltpu.SemaphoreType.DMA((2 * planes + 3,)),
+        ],
+    )
+
+
+def self_energy(outer, inner, coupling, coupled, damping, occupation, given=None):
+    planes, height, columns = outer.shape
+    rows = height - SUBLANES
+
+    def kernel(outer_ref, inner_ref, coupling_ref, *refs):
+        out_ref = refs[-1]
+        even = lax.rem(lax.axis_index("slab"), 2) == 0
+        weights = []
+        for at, before in enumerate((even, jnp.logical_not(even))):
+            row = jnp.where(before, refs[at][0, rows : rows + 1, :], coupling_ref[...])
+            weights.append(row * as_column(row))
+        refs = refs[2:]
+        if given is None:
+            parity = lax.rem(lax.axis_index("energy"), SHIFT)
+            which = lax.broadcasted_iota(jnp.int32, (SUBLANES, columns), 0)
+            extra = jnp.where(which == 0, refs[0][0, parity], refs[1][0, parity])
+        else:
+            extra = refs[0][0, rows:, :]
+        for plane in range(planes):
+            out_ref[plane, 0:rows, :] = (
+                weights[0] * outer_ref[plane, 0:rows, :] + weights[1] * inner_ref[plane, 0:rows, :]
+            )
+            out_ref[plane, rows:, :] = extra
+
+    operands = [outer, inner, coupling, *coupled]
+    operands += [damping, occupation] if given is None else [given]
+    specs = [vmem()] * 5 + ([smem(), smem()] if given is None else [vmem()])
+    return call(kernel, operands, specs, jax.ShapeDtypeStruct(outer.shape, f32))
 
 
 def green_and_lesser(message, hopping, onsite, place, total_energies):
@@ -365,36 +382,37 @@
     orbitals = onsite.shape[1]
     assert boundary_green.shape[2] == SHIFT and energy_devices % 2 == 0
     total_energies = SHIFT * energy_devices
-    odd = lax.rem(lax.axis_index("energy"), 2)
-
-    up = [(i, i + 1) for i in range(slabs - 1)]
-    down = [(i + 1, i) for i in range(slabs - 1)]
+
+    swaps = [
+        [pair for i in range(low, slabs - 1, 2) for pair in ((i, i + 1), (i + 1, i))]
+        for low in (1, 0)
+    ]
     last = energy_devices - 1
     pair = [(i, i ^ 1) for i in range(energy_devices)]
-    near = [(i, i + 1 if i % 2 else i - 1) for i in range(1, last)]
     far = [(i, i + 2) for i in range(1, last, 2) if i + 2 <= last]
     far += [(i, i - 2) for i in range(2, energy_devices, 2)]
-
-    def exchange(parity, own):
-        right, left = split_blocks(boundary_green, coupling, parity[None])
-        from_left = lax.ppermute(right, "slab", up)
-        from_right = lax.ppermute(left, "slab", down)
-        return self_energy_message(from_left, from_right, coupling, damping, occupation, own)
-
-    other = exchange(1 - odd, False)
-    mine = exchange(odd, True)
-    turns = [grid_rows(tile_map, prev_potential)]
+    near = [(to, i) for i, to in far]
+
+    common = (hopping, onsite)
+    other, own = block_messages(boundary_green, coupling, damping, occupation)
+    crossed = lax.ppermute(other, "energy", pair)
+    own_sides = [lax.ppermute(own, "slab", way) for way in swaps]
+    mine = self_energy(*own_sides, coupling, own_sides, damping, occupation)
+    early = lax.ppermute(mine, "energy", far)
+    pair_sides = [lax.ppermute(crossed, "slab", way) for way in swaps]
+    paired = self_energy(*pair_sides, coupling, own_sides, damping, occupation, crossed)
+    late = lax.ppermute(paired, "energy", near)
+    mine_after, _ = lax.optimization_barrier((mine, paired))
+    own_green, own_lesser = green_and_lesser(mine_after, *common, "own", total_energies)
+    grid = grid_rows(tile_map, prev_potential)
+    own_green, grid = lax.optimization_barrier((own_green, grid))
+    turns = [grid]
     for turn in range(1, slabs):
         ring = [(i, (i + turn) % slabs) for i in range(slabs)]
         turns.append(lax.ppermute(turns[0], "slab", ring))
 
-    paired = lax.ppermute(other, "energy", pair)
-    early = lax.ppermute(mine, "energy", far)
-    late = lax.ppermute(other, "energy", near)
-
-    common = (hopping, onsite)
-    own_green, own_lesser = green_and_lesser(mine, *common, "own", total_energies)
     pair_green, pair_lesser = green_and_lesser(paired, *common, "pair", total_energies)
+    early, *turns = lax.optimization_barrier((early, *turns))
     pair_row = second_pass(
         early, paired, own_green, own_lesser, *common, ("early", "pair"), total_energies
     )

time: 68.2 us -> 63.4 us (0.930)
  blocking collectives: 0 us -> 11 us
  starting transfers between devices: 32 us -> 23.3 us
  Pallas kernels: 25.5 us -> 18.6 us
  waiting for transfers between devices: 9.49 us -> 8.69 us
    all_to_all x1 -> x0, starting transfers between devices: 14.9 us -> none  [per_device(): diagonals = lax.all_to_all(rows, DEVICES, 0, 0)]
    all_to_all x0 -> x1, blocking collectives: none -> 11 us  [per_device(): diagonals = lax.all_to_all(rows, DEVICES, 0, 0)]
    pallas_call x2 -> x0, Pallas kernels: 4.44 us -> none  [split_blocks(): pl.pallas_call(kernel, out_shape=[shape, shape], grid_spec=pltpu.Prefetch...]
    ppermute x3, starting transfers between devices: 3.3 us -> 6.69 us  [per_device(): turns.append(lax.ppermute(turns[0], 'slab', ring))]
    ppermute x6, waiting for transfers between devices: 5.42 us -> 8.68 us  [the longest x1 8.67 us: per_device(): crossed = lax.ppermute(other, 'energy', pair)]
    ppermute x6, starting transfers between devices: 12.5 us -> 15.2 us  [the longest x1 4.71 us: per_device(): late = lax.ppermute(paired, 'energy', near)]
    all_to_all x1 -> x0, waiting for transfers between devices: 2.55 us -> none  [per_device(): diagonals = lax.all_to_all(rows, DEVICES, 0, 0)]
    pallas_call x7 -> x8, Pallas kernels: 21 us -> 18.6 us  [call(): pl.pallas_call(kernel, out_shape=shapes, in_specs=specs, out_specs=[vmem(...]
  transfers between devices with their start and end apart: 11 -> 10, of which waited for: 5 -> 1; matrix products, arithmetic and copies ran while one was open for 0% -> 0% of each run, Pallas kernels for 23% -> 18%
where the time goes in v1:
time: 63.4 us; the launch traced here: 63.1 us
  starting transfers between devices  23.3 us (37%)
  Pallas kernels  18.6 us (29%)
  blocking collectives  11 us (17%)
  waiting for transfers between devices  8.69 us (14%)
  between operations  0.88 us (1%)
  local copies, waits for them, and re-layouts  0.67 us (1%)
    pallas_call x8, Pallas kernels, call(): pl.pallas_call(kernel, out_shape=shapes, in_specs=specs, out_specs=[vmem(...  18.6 us
    all_to_all x1, blocking collectives, per_device(): diagonals = lax.all_to_all(rows, DEVICES, 0, 0)  11 us
    ppermute x1, waiting for transfers between devices, per_device(): crossed = lax.ppermute(other, 'energy', pair)  8.67 us
    ppermute x3, starting transfers between devices, per_device(): turns.append(lax.ppermute(turns[0], 'slab', ring))  6.69 us
    ppermute x1, starting transfers between devices, per_device(): late = lax.ppermute(paired, 'energy', near)  4.71 us
    ppermute x2, starting transfers between devices, per_device(): pair_sides = [lax.ppermute(crossed, 'slab', way) for way in swaps]  3.85 us
    ppermute x2, starting transfers between devices, per_device(): own_sides = [lax.ppermute(own, 'slab', way) for way in swaps]  3.6 us
    ppermute x1, starting transfers between devices, per_device(): crossed = lax.ppermute(other, 'energy', pair)  3 us
  transfers between devices with their start and end apart: 10, of which 1 were waited for; matrix products, arithmetic and copies ran while one was open for 0% of the time, Pallas kernels for 18%

profile of v1, /device:TPU:0, one launch (start us, length us, event | category | flops | bytes accessed | tf_op | source)
XLA Modules:
  0.0 63.1 jit_solution(308808950274263402)
XLA Ops:
  0.6 1.4 %shard_map.95 = (f32[2,264,256]{2,1,0:T(8,128)S(1)}, f32[2,264,256]{2,1,0:T(8,128)S(1)}) custom-call(f32[2,1,2,256,256]{4,3,2,1,0:T(8,128)} %block_ref.1, f32[1,256]{1,0:T(1,128)} %coupling_ref.5, f32[1,2]{1,0:T(1,128)} %refs_2_.1, f32[1,2]{1,0:T(1,128)} %refs_3_.1), custom_call_target="tpu_custom_call" | custom-call | tf_op jit(solution)/shard_map/pallas_call | solution.py:162
  2.0 0.0 copy-start.4
  2.1 0.0 copy-start.2
  2.1 0.0 copy-start.3
  2.1 3.0 %collective-permute-start = (f32[2,264,256]{2,1,0:T(8,128)S(1)}, f32[2,264,256]{2,1,0:T(8,128)S(1)}, u32[]{:S(2)}, u32[]{:S(2)}) collective-permute-start(f32[2,264,256]{2,1,0:T(8,128)S(1)} %get-tuple-element.16), channel_id=1, source_target_pairs={{0,4},{4,0},{8,12},{12,8},{16,20},{20,16},{24,28},{28,24},{1,5},{5... | collective-permute-start | bytes 1622024 | tf_op jit(solution)/shard_map/ppermute | solution.py:398
  5.1 0.7 %collective-permute-start.3 = (f32[2,264,256]{2,1,0:T(8,128)S(1)}, f32[2,264,256]{2,1,0:T(8,128)S(1)}, u32[]{:S(2)}, u32[]{:S(2)}) collective-permute-start(f32[2,264,256]{2,1,0:T(8,128)S(1)} %get-tuple-element.17), channel_id=1, source_target_pairs={{1,2},{2,1},{5,6},{6,5},{9,10},{10,9},{13,14},{14,13},{17,18},{18,... | collective-permute-start | bytes 1622024 | tf_op jit(solution)/shard_map/ppermute | solution.py:399
  5.8 2.9 %collective-permute-start.4 = (f32[2,264,256]{2,1,0:T(8,128)S(1)}, f32[2,264,256]{2,1,0:T(8,128)S(1)}, u32[]{:S(2)}, u32[]{:S(2)}) collective-permute-start(f32[2,264,256]{2,1,0:T(8,128)S(1)} %get-tuple-element.17), channel_id=1, source_target_pairs={{0,1},{1,0},{2,3},{3,2},{4,5},{5,4},{6,7},{7,6},{8,9},{9,8},{10,11... | collective-permute-start | bytes 1622024 | tf_op jit(solution)/shard_map/ppermute | solution.py:399
  8.7 8.7 %collective-permute-done.refs_2_ = f32[2,264,256]{2,1,0:T(8,128)S(1)} collective-permute-done((f32[2,264,256]{2,1,0:T(8,128)S(1)}, f32[2,264,256]{2,1,0:T(8,128)S(1)}, u32[]{:S(2)}, u32[]{:S(2)}) %collective-permute-start) | collective-permute-done | bytes 540704 | tf_op jit(solution)/shard_map/ppermute | solution.py:398
  17.4 0.7 %collective-permute-start.1 = (f32[2,264,256]{2,1,0:T(8,128)S(1)}, f32[2,264,256]{2,1,0:T(8,128)S(1)}, u32[]{:S(2)}, u32[]{:S(2)}) collective-permute-start(f32[2,264,256]{2,1,0:T(8,128)S(1)} %collective-permute-done.refs_2_), channel_id=1, source_target_pairs={{1,2},{2,1},{5,6},{6,5},{9,10},{10,9},{13,14},{14,13},{17,18},{18,... | collective-permute-start | bytes 1622024 | tf_op jit(solution)/shard_map/ppermute | solution.py:402
  18.1 3.2 %collective-permute-start.2 = (f32[2,264,256]{2,1,0:T(8,128)S(1)}, f32[2,264,256]{2,1,0:T(8,128)S(1)}, u32[]{:S(2)}, u32[]{:S(2)}) collective-permute-start(f32[2,264,256]{2,1,0:T(8,128)S(1)} %collective-permute-done.refs_2_), channel_id=1, source_target_pairs={{0,1},{1,0},{2,3},{3,2},{4,5},{5,4},{6,7},{7,6},{8,9},{9,8},{10,11... | collective-permute-start | bytes 1622024 | tf_op jit(solution)/shard_map/ppermute | solution.py:402
  21.2 0.0 collective-permute-done.3.refs_0_.outer_ref
  21.2 0.0 collective-permute-done.4.refs_1_.inner_ref
  21.2 0.0 copy-done.4
  21.2 0.0 copy-done.2
  21.2 0.0 copy-done.3
  21.2 0.8 %shard_map.97.message_ref.inner_ref = f32[2,264,256]{2,1,0:T(8,128)S(1)} custom-call(f32[2,264,256]{2,1,0:T(8,128)S(1)} %collective-permute-done.3.refs_0_.outer_ref, f32[2,264,256]{2,1,0:T(8,128)S(1)} %collective-permute-done.4.refs_1_.inner_ref, f32[1,256]{1,0:T(1,128)S(1)} %copy-done.2, f32[2,264,256]{2,1,0:T(8,128)S(1)} %collective-permute-done.3.refs_0_.outer_ref, ...), custom_call_target="tpu_custom_call" | custom-call | tf_op jit(solution)/shard_map/pallas_call | solution.py:162
  22.1 0.0 copy-start.5
  22.1 1.4 %collective-permute-start.6 = (f32[2,264,256]{2,1,0:T(8,128)S(1)}, f32[2,264,256]{2,1,0:T(8,128)S(1)}, u32[]{:S(2)}, u32[]{:S(2)}) collective-permute-start(f32[2,264,256]{2,1,0:T(8,128)S(1)} %shard_map.97.message_ref.inner_ref), channel_id=1, source_target_pairs={{4,12},{12,20},{20,28},{8,0},{16,8},{24,16},{5,13},{13,21},{21,29}... | collective-permute-start | bytes 1622024 | tf_op jit(solution)/shard_map/ppermute | solution.py:401
  23.5 0.0 collective-permute-done.1.outer_ref
  23.5 0.0 collective-permute-done.2.inner_ref
  23.5 0.0 copy-start.6
  23.6 0.3 shard_map.96.message_ref.inner_ref
  23.8 0.0 copy-start
  23.9 4.7 %collective-permute-start.5 = (f32[2,264,256]{2,1,0:T(8,128)S(1)}, f32[2,264,256]{2,1,0:T(8,128)S(1)}, u32[]{:S(2)}, u32[]{:S(2)}) collective-permute-start(f32[2,264,256]{2,1,0:T(8,128)S(1)} %shard_map.96.message_ref.inner_ref), channel_id=1, source_target_pairs={{12,4},{20,12},{28,20},{0,8},{8,16},{16,24},{13,5},{21,13},{29,21}... | collective-permute-start | bytes 1622024 | tf_op jit(solution)/shard_map/ppermute | solution.py:404
  28.6 0.0 copy-done.5
  28.6 0.0 copy-done.6
  28.6 0.0 copy-start.1
  28.7 0.0 copy-done
  28.7 0.6 copy-done.1
  29.3 2.6 %shard_map.99 = (f32[2,256,256]{2,1,0:T(8,128)S(1)}, f32[2,256,256]{2,1,0:T(8,128)S(1)}) custom-call(f32[2,264,256]{2,1,0:T(8,128)S(1)} %shard_map.97.message_ref.inner_ref, f32[1,256,256]{2,1,0:T(8,128)S(1)} %copy-done, f32[1,256]{1,0:T(1,128)S(1)} %copy-done.1), custom_call_target="tpu_custom_call" | custom-call | tf_op jit(solution)/shard_map/pallas_call | solution.py:162
  31.9 3.6 %collective-permute-start.7 = (f32[2,24,128]{2,1,0:T(8,128)S(1)}, f32[2,24,128]{2,1,0:T(8,128)S(1)}, u32[]{:S(2)}, u32[]{:S(2)}) collective-permute-start(f32[2,24,128]{2,1,0:T(8,128)S(1)} %fusion.1.refs_0_), channel_id=1, source_target_pairs={{0,1},{1,2},{2,3},{3,0},{4,5},{5,6},{6,7},{7,4},{8,9},{9,10},{10,1... | collective-permute-start | bytes 73736 | tf_op jit(solution)/shard_map/ppermute | solution.py:412
  35.6 1.7 %collective-permute-start.8 = (f32[2,24,128]{2,1,0:T(8,128)S(1)}, f32[2,24,128]{2,1,0:T(8,128)S(1)}, u32[]{:S(2)}, u32[]{:S(2)}) collective-permute-start(f32[2,24,128]{2,1,0:T(8,128)S(1)} %fusion.1.refs_0_), channel_id=1, source_target_pairs={{0,2},{1,3},{2,0},{3,1},{4,6},{5,7},{6,4},{7,5},{8,10},{9,11},{10,... | collective-permute-start | bytes 73736 | tf_op jit(solution)/shard_map/ppermute | solution.py:412
  37.2 1.4 %collective-permute-start.9 = (f32[2,24,128]{2,1,0:T(8,128)S(1)}, f32[2,24,128]{2,1,0:T(8,128)S(1)}, u32[]{:S(2)}, u32[]{:S(2)}) collective-permute-start(f32[2,24,128]{2,1,0:T(8,128)S(1)} %fusion.1.refs_0_), channel_id=1, source_target_pairs={{0,3},{1,0},{2,1},{3,2},{4,7},{5,4},{6,5},{7,6},{8,11},{9,8},{10,9... | collective-permute-start | bytes 73736 | tf_op jit(solution)/shard_map/ppermute | solution.py:412
  38.6 2.6 %shard_map.98 = (f32[2,256,256]{2,1,0:T(8,128)S(1)}, f32[2,256,256]{2,1,0:T(8,128)S(1)}) custom-call(f32[2,264,256]{2,1,0:T(8,128)S(1)} %shard_map.96.message_ref.inner_ref, f32[1,256,256]{2,1,0:T(8,128)S(1)} %copy-done, f32[1,256]{1,0:T(1,128)S(1)} %copy-done.1), custom_call_target="tpu_custom_call" | custom-call | tf_op jit(solution)/shard_map/pallas_call | solution.py:162
  41.3 0.0 collective-permute-done.6.outer_ref
  41.3 0.0 collective-permute-done.7.refs_1_
  41.3 0.0 collective-permute-done.8.refs_2_
  41.3 0.0 collective-permute-done.9.refs_3_
  41.3 4.9 %shard_map.100.refs_0_ = f32[1,256]{1,0:T(1,128)S(1)} custom-call(f32[2,264,256]{2,1,0:T(8,128)S(1)} %collective-permute-done.6.outer_ref, f32[2,264,256]{2,1,0:T(8,128)S(1)} %shard_map.96.message_ref.inner_ref, f32[2,256,256]{2,1,0:T(8,128)S(1)} %get-tuple-element.24.green_ref, f32[2,256,256]{2,1,0:T(8,128)S(1)} %get-tuple-element.25.lesser_ref, ...), custom_call_target="tpu_custom_call" | custom-call | tf_op jit(solution)/shard_map/pallas_call | solution.py:162
  46.2 0.0 collective-permute-done.5.outer_ref
  46.3 5.0 %shard_map.101 = f32[32,2,256]{2,1,0:T(2,128)S(1)} custom-call(f32[2,264,256]{2,1,0:T(8,128)S(1)} %collective-permute-done.5.outer_ref, f32[2,264,256]{2,1,0:T(8,128)S(1)} %shard_map.97.message_ref.inner_ref, f32[2,256,256]{2,1,0:T(8,128)S(1)} %get-tuple-element.18.green_ref, f32[2,256,256]{2,1,0:T(8,128)S(1)} %get-tuple-element.19.lesser_ref, ...), custom_call_target="tpu_custom_call" | custom-call | tf_op jit(solution)/shard_map/pallas_call | solution.py:162
  51.3 11.0 %all_to_all.5 = f32[32,2,256]{2,1,0:T(2,128)S(1)} all-to-all(f32[32,2,256]{2,1,0:T(2,128)S(1)} %shard_map.101), channel_id=1, replica_groups=mesh['energy'=8,'slab'=4] {'energy','slab'}, dimensions={0} | all-to-all | bytes 131072 | tf_op jit(solution)/shard_map/all_to_all | solution.py:422
  62.2 0.9 %shard_map.102 = (f32[1,2,256]{2,1,0:T(2,128)}, f32[1,16,128]{2,1,0:T(8,128)}) custom-call(f32[8,4,2,256]{3,2,1,0:T(2,128)S(1)} %bitcast.1, f32[2,24,128]{2,1,0:T(8,128)S(1)} %fusion.1.refs_0_, f32[2,24,128]{2,1,0:T(8,128)S(1)} %collective-permute-done.7.refs_1_, f32[2,24,128]{2,1,0:T(8,128)S(1)} %collective-permute-done.8.refs_2_, ...), custom_call_target="tpu_custom_call" | custom-call | tf_op jit(solution)/shard_map/pallas_call | solution.py:162
  (2 shorter events, 0.0 us)
Async XLA Ops:
  2.0 19.2 %copy-start.4 = (f32[1,2]{1,0:T(1,128)S(1)}, f32[1,2]{1,0:T(1,128)}, u32[]{:S(2)}) copy-start(f32[1,2]{1,0:T(1,128)} %refs_3_.1) | copy-start | bytes 28
  2.1 19.2 %copy-start.2 = (f32[1,256]{1,0:T(1,128)S(1)}, f32[1,256]{1,0:T(1,128)}, u32[]{:S(2)}) copy-start(f32[1,256]{1,0:T(1,128)} %coupling_ref.5) | copy-start | bytes 3076
  2.1 19.2 %copy-start.3 = (f32[1,2]{1,0:T(1,128)S(1)}, f32[1,2]{1,0:T(1,128)}, u32[]{:S(2)}) copy-start(f32[1,2]{1,0:T(1,128)} %refs_2_.1) | copy-start | bytes 28
  2.1 15.3 %collective-permute-start = (f32[2,264,256]{2,1,0:T(8,128)S(1)}, f32[2,264,256]{2,1,0:T(8,128)S(1)}, u32[]{:S(2)}, u32[]{:S(2)}) collective-permute-start(f32[2,264,256]{2,1,0:T(8,128)S(1)} %get-tuple-element.16), channel_id=1, source_target_pairs={{0,4},{4,0},{8,12},{12,8},{16,20},{20,16},{24,28},{28,24},{1,5},{5... | collective-permute-start | bytes 1622024 | tf_op jit(solution)/shard_map/ppermute | solution.py:398
  5.1 16.1 %collective-permute-start.3 = (f32[2,264,256]{2,1,0:T(8,128)S(1)}, f32[2,264,256]{2,1,0:T(8,128)S(1)}, u32[]{:S(2)}, u32[]{:S(2)}) collective-permute-start(f32[2,264,256]{2,1,0:T(8,128)S(1)} %get-tuple-element.17), channel_id=1, source_target_pairs={{1,2},{2,1},{5,6},{6,5},{9,10},{10,9},{13,14},{14,13},{17,18},{18,... | collective-permute-start | bytes 1622024 | tf_op jit(solution)/shard_map/ppermute | solution.py:399
  5.8 15.4 %collective-permute-start.4 = (f32[2,264,256]{2,1,0:T(8,128)S(1)}, f32[2,264,256]{2,1,0:T(8,128)S(1)}, u32[]{:S(2)}, u32[]{:S(2)}) collective-permute-start(f32[2,264,256]{2,1,0:T(8,128)S(1)} %get-tuple-element.17), channel_id=1, source_target_pairs={{0,1},{1,0},{2,3},{3,2},{4,5},{5,4},{6,7},{7,6},{8,9},{9,8},{10,11... | collective-permute-start | bytes 1622024 | tf_op jit(solution)/shard_map/ppermute | solution.py:399
  17.4 6.2 %collective-permute-start.1 = (f32[2,264,256]{2,1,0:T(8,128)S(1)}, f32[2,264,256]{2,1,0:T(8,128)S(1)}, u32[]{:S(2)}, u32[]{:S(2)}) collective-permute-start(f32[2,264,256]{2,1,0:T(8,128)S(1)} %collective-permute-done.refs_2_), channel_id=1, source_target_pairs={{1,2},{2,1},{5,6},{6,5},{9,10},{10,9},{13,14},{14,13},{17,18},{18,... | collective-permute-start | bytes 1622024 | tf_op jit(solution)/shard_map/ppermute | solution.py:402
  18.1 5.5 %collective-permute-start.2 = (f32[2,264,256]{2,1,0:T(8,128)S(1)}, f32[2,264,256]{2,1,0:T(8,128)S(1)}, u32[]{:S(2)}, u32[]{:S(2)}) collective-permute-start(f32[2,264,256]{2,1,0:T(8,128)S(1)} %collective-permute-done.refs_2_), channel_id=1, source_target_pairs={{0,1},{1,0},{2,3},{3,2},{4,5},{5,4},{6,7},{7,6},{8,9},{9,8},{10,11... | collective-permute-start | bytes 1622024 | tf_op jit(solution)/shard_map/ppermute | solution.py:402
  22.1 6.5 %copy-start.5 = (s32[1,128,128]{2,1,0:T(8,128)S(1)}, s32[1,128,128]{2,1,0:T(8,128)}, u32[]{:S(2)}) copy-start(s32[1,128,128]{2,1,0:T(8,128)} %param.14) | copy-start | bytes 196612
  22.1 19.2 %collective-permute-start.6 = (f32[2,264,256]{2,1,0:T(8,128)S(1)}, f32[2,264,256]{2,1,0:T(8,128)S(1)}, u32[]{:S(2)}, u32[]{:S(2)}) collective-permute-start(f32[2,264,256]{2,1,0:T(8,128)S(1)} %shard_map.97.message_ref.inner_ref), channel_id=1, source_target_pairs={{4,12},{12,20},{20,28},{8,0},{16,8},{24,16},{5,13},{13,21},{21,29}... | collective-permute-start | bytes 1622024 | tf_op jit(solution)/shard_map/ppermute | solution.py:401
  23.5 5.1 %copy-start.6 = (f32[1,128,128]{2,1,0:T(8,128)S(1)}, f32[1,128,128]{2,1,0:T(8,128)}, u32[]{:S(2)}) copy-start(f32[1,128,128]{2,1,0:T(8,128)} %param.15) | copy-start | bytes 196612
  23.8 4.8 %copy-start = (f32[1,256,256]{2,1,0:T(8,128)S(1)}, f32[1,256,256]{2,1,0:T(8,128)}, u32[]{:S(2)}) copy-start(f32[1,256,256]{2,1,0:T(8,128)} %hopping_ref.7) | copy-start | bytes 786436
  23.9 22.4 %collective-permute-start.5 = (f32[2,264,256]{2,1,0:T(8,128)S(1)}, f32[2,264,256]{2,1,0:T(8,128)S(1)}, u32[]{:S(2)}, u32[]{:S(2)}) collective-permute-start(f32[2,264,256]{2,1,0:T(8,128)S(1)} %shard_map.96.message_ref.inner_ref), channel_id=1, source_target_pairs={{12,4},{20,12},{28,20},{0,8},{8,16},{16,24},{13,5},{21,13},{29,21}... | collective-permute-start | bytes 1622024 | tf_op jit(solution)/shard_map/ppermute | solution.py:404
  28.6 0.7 %copy-start.1 = (f32[1,256]{1,0:T(1,128)S(1)}, f32[1,256]{1,0:T(1,128)}, u32[]{:S(2)}) copy-start(f32[1,256]{1,0:T(1,128)} %onsite_ref.7) | copy-start | bytes 3076
  31.9 9.3 %collective-permute-start.7 = (f32[2,24,128]{2,1,0:T(8,128)S(1)}, f32[2,24,128]{2,1,0:T(8,128)S(1)}, u32[]{:S(2)}, u32[]{:S(2)}) collective-permute-start(f32[2,24,128]{2,1,0:T(8,128)S(1)} %fusion.1.refs_0_), channel_id=1, source_target_pairs={{0,1},{1,2},{2,3},{3,0},{4,5},{5,6},{6,7},{7,4},{8,9},{9,10},{10,1... | collective-permute-start | bytes 73736 | tf_op jit(solution)/shard_map/ppermute | solution.py:412
  35.6 5.7 %collective-permute-start.8 = (f32[2,24,128]{2,1,0:T(8,128)S(1)}, f32[2,24,128]{2,1,0:T(8,128)S(1)}, u32[]{:S(2)}, u32[]{:S(2)}) collective-permute-start(f32[2,24,128]{2,1,0:T(8,128)S(1)} %fusion.1.refs_0_), channel_id=1, source_target_pairs={{0,2},{1,3},{2,0},{3,1},{4,6},{5,7},{6,4},{7,5},{8,10},{9,11},{10,... | collective-permute-start | bytes 73736 | tf_op jit(solution)/shard_map/ppermute | solution.py:412
  37.2 4.1 %collective-permute-start.9 = (f32[2,24,128]{2,1,0:T(8,128)S(1)}, f32[2,24,128]{2,1,0:T(8,128)S(1)}, u32[]{:S(2)}, u32[]{:S(2)}) collective-permute-start(f32[2,24,128]{2,1,0:T(8,128)S(1)} %fusion.1.refs_0_), channel_id=1, source_target_pairs={{0,3},{1,0},{2,1},{3,2},{4,7},{5,4},{6,5},{7,6},{8,11},{9,8},{10,9... | collective-permute-start | bytes 73736 | tf_op jit(solution)/shard_map/ppermute | solution.py:412

commit v2 on v1

v2 whole, which is shorter than its diff:
```python
import functools

import jax
import jax.numpy as jnp
from jax import lax
from jax.experimental import pallas as pl
from jax.experimental.pallas import tpu as pltpu
from jax.sharding import PartitionSpec as P

SHIFT = 2
SWEEPS = 2
PHONON = 0.5
CHARGE = 2.0
ANISO = 0.05
SCREEN = 0.05
MAIN_DIAGONAL = 2.0 + 4.0 * ANISO + SCREEN
LANES = 128
SUBLANES = 8
VMEM_BYTES = 48 * 1024 * 1024

f32 = jnp.float32
bf16 = jnp.bfloat16
DEVICES = ("energy", "slab")


def parts(matrix):
    high = matrix.astype(bf16)
    return high, (matrix - high.astype(f32)).astype(bf16)


def dot(left, right, transposed=False):
    contract = (((1,), (1 if transposed else 0,)), ((), ()))
    out = [
        lax.dot_general(left[i], right[j], contract, preferred_element_type=f32)
        for i, j in ((0, 0), (1, 0), (0, 1))
    ]
    return out[0] + out[1] + out[2]


def factor(matrix):
    return parts(matrix[0]), parts(matrix[1]), parts(matrix[0] + matrix[1])


def adjoint_factor(matrix):
    return parts(matrix[0]), parts(matrix[1]), parts(matrix[0] - matrix[1])


def product(left, right):
    real, imag, both = (dot(a, b) for a, b in zip(left, right))
    return real - imag, both - real - imag


def adjoint_product(left, right):
    real, imag, both = (dot(a, b, transposed=True) for a, b in zip(left, right))
    return real + imag, both - real + imag


def add(*matrices):
    return sum(m[0] for m in matrices), sum(m[1] for m in matrices)


def as_column(row):
    size = row.shape[1]
    return jnp.broadcast_to(row, (SUBLANES, size)).T[:, 0:1]


def start_of(energy, onsite, damping):
    real = energy - onsite
    modulus = real * real + damping * damping
    present = damping > 0.0
    modulus = jnp.where(present, modulus, 1.0)
    return jnp.where(present, real / modulus, 0.0), jnp.where(present, -damping / modulus, 0.0)


def scale(matrix, factor):
    return (
        matrix[0] * factor[0] - matrix[1] * factor[1],
        matrix[0] * factor[1] + matrix[1] * factor[0],
    )


def invert(coupled, row, column):
    b1 = scale(coupled, row)
    b1_factor = factor(b1)
    b2 = product(b1_factor, b1_factor)
    b2_factor = factor(b2)
    b4 = product(b2_factor, b2_factor)
    b3 = product(b1_factor, b2_factor)
    t = add(b1, b2, b3)
    rest = product(factor(t), factor(b4))
    size = b1[0].shape[0]
    unit = (
        lax.broadcasted_iota(jnp.int32, (size, size), 0)
        == lax.broadcasted_iota(jnp.int32, (size, size), 1)
    ).astype(f32)
    total = add(t, b4, rest)
    return scale((unit + total[0], total[1]), column)


def halves(message_ref):
    height, columns = message_ref.shape
    return message_ref.at[pl.ds(columns, height - columns)], message_ref.at[pl.ds(0, columns)]


class Element:
    def __init__(self, message_refs, hopping_ref, onsite_ref, chain, total_energies):
        size = hopping_ref.shape[-1]
        parity = lax.rem(lax.axis_index("energy"), SHIFT)
        index = (SHIFT * chain + parity).astype(f32)
        energy = -2.0 + (4.0 / total_energies) * (index + 0.5)
        real_ref, imag_ref = message_refs if len(message_refs) == 2 else halves(message_refs[0])
        self.sigma = (real_ref[0:size, :], imag_ref[...])
        damping = real_ref[size : size + 1, :]
        self.occupation = real_ref[size + 1 : size + 2, :]
        onsite = onsite_ref[...]
        self.row = start_of(energy, onsite, damping)
        self.column = tuple(as_column(part) for part in self.row)
        self.hopping = hopping_ref[0]

    def lesser_source(self):
        real, imag = self.sigma
        return -self.occupation * (real - real.T), -self.occupation * (imag + imag.T)

    def green(self, phonon=None):
        coupled = (self.hopping + self.sigma[0], self.sigma[1])
        if phonon is not None:
            coupled = add(coupled, phonon)
        return invert(coupled, self.row, self.column)

    def green_and_lesser(self):
        green = self.green()
        mixed = product(factor(green), factor(self.lesser_source()))
        return green, adjoint_product(factor(mixed), adjoint_factor(green))

    def lesser_row(self, greens, lessers):
        half = tuple(PHONON * part for part in add(*greens))
        green = self.green(half)
        source = add(self.lesser_source(), tuple(PHONON * part for part in add(*lessers)))
        real, imag = parts(green[0]), parts(green[1])
        source_real, source_imag = parts(source[0]), parts(source[1])
        terms = green[0] * dot(real, source_imag) + green[1] * dot(imag, source_imag)
        terms = terms - 2.0 * green[1] * dot(real, source_real)
        column = jnp.sum(terms, axis=1, keepdims=True)
        return jnp.broadcast_to(column, (column.shape[0], LANES)).T[0:1, :]


def chain_places():
    here = lax.axis_index("energy")
    odd = lax.rem(here, 2)
    step = 1 - 2 * odd
    return {"own": here, "pair": here + step, "early": here + 2 * step, "late": here - step}


def vmem():
    return pl.BlockSpec(memory_space=pltpu.VMEM)


def smem():
    return pl.BlockSpec(memory_space=pltpu.SMEM)


def call(kernel, operands, specs, shapes, **options):
    several = isinstance(shapes, list)
    return pl.pallas_call(
        kernel,
        out_shape=shapes,
        in_specs=specs,
        out_specs=[vmem() for _ in shapes] if several else vmem(),
        compiler_params=pltpu.CompilerParams(vmem_limit_bytes=VMEM_BYTES),
        cost_estimate=pl.CostEstimate(flops=0, transcendentals=0, bytes_accessed=0),
        **options,
    )(*operands)


def block_messages(boundary_green, coupling, damping, occupation):
    _, _, _, rows, columns = boundary_green.shape

    def kernel(block_ref, coupling_ref, *refs):
        level_refs, (real_ref, imag_ref), own_refs = refs[:2], refs[2:4], refs[4:6]
        held_refs, sems = refs[6:8], refs[8]
        parity = lax.rem(lax.axis_index("energy"), SHIFT)
        moves = [
            (block_ref.at[0, 0, 1 - parity], real_ref.at[pl.ds(0, rows)]),
            *zip(level_refs, held_refs),
            (block_ref.at[1, 0, 1 - parity], imag_ref),
            (block_ref.at[0, 0, parity], own_refs[0].at[pl.ds(0, rows)]),
            (coupling_ref, own_refs[0].at[pl.ds(rows, 1)]),
            (block_ref.at[1, 0, parity], own_refs[1]),
        ]
        copies = [
            pltpu.make_async_copy(source, target, sems.at[at])
            for at, (source, target) in enumerate(moves)
        ]
        for copy in copies:
            copy.start()
        for copy in copies:
            copy.wait()
        levels = [
            jnp.where(parity == 0, held_ref[0:1, 1:2], held_ref[0:1, 0:1]) for held_ref in held_refs
        ]
        which = lax.broadcasted_iota(jnp.int32, (SUBLANES, columns), 0)
        real_ref[rows:, :] = jnp.where(which == 0, levels[0], levels[1])

    operands = (boundary_green, coupling, damping, occupation)
    return call(
        kernel,
        [pltpu.with_memory_space_constraint(x, pltpu.HBM) for x in operands],
        [pl.BlockSpec(memory_space=pltpu.HBM)] * 4,
        [
            jax.ShapeDtypeStruct((height, columns), f32)
            for height in (rows + SUBLANES, rows) * 2
        ],
        scratch_shapes=[
            pltpu.VMEM(damping.shape, f32),
            pltpu.VMEM(damping.shape, f32),
            pltpu.SemaphoreType.DMA((7,)),
        ],
    )


def slab_weights(coupling_ref, side_refs):
    even = lax.rem(lax.axis_index("slab"), 2) == 0
    below = coupling_ref.shape[1]
    weights = []
    for side_ref, before in zip(side_refs, (even, jnp.logical_not(even))):
        row = jnp.where(before, side_ref[below : below + 1, :], coupling_ref[...])
        weights.append(row * as_column(row))
    return weights


def own_self_energy(real_sides, imag_sides, coupling, damping, occupation):
    columns = coupling.shape[1]

    def kernel(*refs):
        real_refs, imag_refs = refs[:2], refs[2:4]
        coupling_ref, damping_ref, occupation_ref, out_ref = refs[4:]
        weights = slab_weights(coupling_ref, real_refs)
        rows = pl.ds(0, columns)
        for low, side_refs in ((0, imag_refs), (columns, real_refs)):
            outer, inner = (w * ref[rows, :] for w, ref in zip(weights, side_refs))
            out_ref[pl.ds(low, columns), :] = outer + inner
        parity = lax.rem(lax.axis_index("energy"), SHIFT)
        which = lax.broadcasted_iota(jnp.int32, (SUBLANES, columns), 0)
        out_ref[2 * columns :, :] = jnp.where(
            which == 0, damping_ref[0, parity], occupation_ref[0, parity]
        )

    return call(
        kernel,
        (*real_sides, *imag_sides, coupling, damping, occupation),
        [vmem()] * 5 + [smem()] * 2,
        jax.ShapeDtypeStruct((2 * columns + SUBLANES, columns), f32),
    )


def pair_self_energy(sides, coupling, own_sides, crossed):
    height, columns = crossed.shape

    def kernel(outer_ref, inner_ref, coupling_ref, own_outer_ref, own_inner_ref, crossed_ref, out_ref):
        outer_weight, inner_weight = slab_weights(coupling_ref, (own_outer_ref, own_inner_ref))
        rows = pl.ds(0, columns)
        out_ref[rows, :] = outer_weight * outer_ref[rows, :] + inner_weight * inner_ref[rows, :]
        if height > columns:
            out_ref[columns:, :] = crossed_ref[columns:, :]

    operands = (*sides, coupling, *own_sides, crossed)
    return call(kernel, operands, [vmem()] * 6, jax.ShapeDtypeStruct((height, columns), f32))


def green_and_lesser(message, hopping, onsite, place, total_energies):
    count = len(message)

    def kernel(*refs):
        hopping_ref, onsite_ref, green_ref, lesser_ref = refs[count:]
        element = Element(
            refs[:count], hopping_ref, onsite_ref, chain_places()[place], total_energies
        )
        green, lesser = element.green_and_lesser()
        for plane in range(2):
            green_ref[plane] = green[plane]
            lesser_ref[plane] = lesser[plane]

    size = hopping.shape[-1]
    shape = jax.ShapeDtypeStruct((2, size, size), f32)
    operands = (*message, hopping, onsite)
    return call(kernel, operands, [vmem()] * len(operands), [shape, shape])


def grid_share(rows_here, energy_devices):
    needed = rows_here + 2 * SWEEPS
    return needed, -(-2 * needed // energy_devices)


def pair_pass(early, paired, green, lesser, hopping, onsite, tile_map, potential, total_energies):
    size = hopping.shape[-1]
    energy_devices, slabs = lax.axis_size("energy"), lax.axis_size("slab")
    grid_total, columns = tile_map.shape[1:]
    rows_here = grid_total // energy_devices
    needed, share = grid_share(rows_here, energy_devices)
    padded = grid_total + 2 * SWEEPS

    def kernel(*refs):
        early_refs, paired_refs, refs = refs[:1], refs[1:3], refs[3:]
        green_ref, lesser_ref, hopping_ref, onsite_ref, tile_ref, potential_ref = refs[:6]
        parcel_ref, grid_ref = refs[6:]
        chains = chain_places()
        here = Element(paired_refs, hopping_ref, onsite_ref, chains["pair"], total_energies)
        beyond = Element(early_refs, hopping_ref, onsite_ref, chains["early"], total_energies)
        beyond_green, beyond_lesser = beyond.green_and_lesser()
        row = here.lesser_row(
            [beyond_green, (green_ref[0], green_ref[1])],
            [beyond_lesser, (lesser_ref[0], lesser_ref[1])],
        )
        border = jnp.zeros((SWEEPS, columns), f32)
        for at, plane in enumerate((potential_ref[0], tile_ref[0].astype(f32))):
            low = at * padded
            grid_ref[low : low + SWEEPS, :] = border
            grid_ref[low + SWEEPS : low + SWEEPS + grid_total, :] = plane
            grid_ref[low + SWEEPS + grid_total : low + padded, :] = border
        first = lax.axis_index("energy") * share
        for to in range(energy_devices):
            pieces = [row]
            for i in range(share):
                place = jnp.minimum(first + i, 2 * needed - 1)
                which = (place >= needed).astype(jnp.int32)
                source = which * (padded - needed) + place + to * rows_here
                pieces.append(grid_ref[pl.ds(source, 1), :])
            parcel = jnp.concatenate(pieces, axis=1)
            for slab in range(slabs):
                parcel_ref[to * slabs + slab, :, size:] = parcel

    operands = [early, *paired, green, lesser, hopping, onsite, tile_map, potential]
    parcels = (energy_devices * slabs, 1, 2 * size + share * columns)
    return call(
        kernel,
        operands,
        [vmem()] * len(operands),
        jax.ShapeDtypeStruct(parcels, f32),
        scratch_shapes=[pltpu.VMEM((2 * padded, columns), f32)],
    )


def own_pass(late, mine, green, lesser, hopping, onsite, parcels, total_energies):
    size = hopping.shape[-1]

    def kernel(*refs):
        late_refs, mine_refs, refs = refs[:2], refs[2:3], refs[3:]
        green_ref, lesser_ref, hopping_ref, onsite_ref, _, parcel_ref = refs
        chains = chain_places()
        here = Element(mine_refs, hopping_ref, onsite_ref, chains["own"], total_energies)
        beyond = Element(late_refs, hopping_ref, onsite_ref, chains["late"], total_energies)
        beyond_green, beyond_lesser = beyond.green_and_lesser()
        row = here.lesser_row(
            [beyond_green, (green_ref[0], green_ref[1])],
            [beyond_lesser, (lesser_ref[0], lesser_ref[1])],
        )
        for to in range(parcel_ref.shape[0]):
            parcel_ref[to, :, 0:size] = row

    operands = [*late, mine, green, lesser, hopping, onsite, parcels]
    return call(
        kernel,
        operands,
        [vmem()] * len(operands),
        jax.ShapeDtypeStruct(parcels.shape, f32),
        input_output_aliases={len(operands) - 1: 0},
    )


def relax(parcels, orbitals, total_energies, grid_total, columns):
    energy_devices, slabs = parcels.shape[:2]
    rows_here = grid_total // energy_devices
    needed, share = grid_share(rows_here, energy_devices)
    rows = -(-needed // SUBLANES) * SUBLANES

    def kernel(parcel_ref, lesser_ref, potential_ref, grid_ref):
        here, slab = lax.axis_index("energy"), lax.axis_index("slab")
        odd = lax.rem(here, 2)
        for parity in range(2):
            both = parcel_ref[here - odd + parity, slab, :, 0 : 2 * orbitals]
            lesser_ref[0, parity : parity + 1, :] = jnp.where(
                odd == parity, both[:, 0:orbitals], both[:, orbitals:]
            )
        empty = jnp.zeros((rows - needed, columns), f32)
        for at in range(slabs):
            for which in range(2):
                if rows > needed:
                    grid_ref[at, which, needed:, :] = empty
            for place in range(2 * needed):
                device, low = place // share, 2 * orbitals + place % share * columns
                row = place % needed
                grid_ref[at, place // needed, row : row + 1, :] = parcel_ref[
                    device, at, :, low : low + columns
                ]
        grid_row = (
            lax.broadcasted_iota(jnp.int32, (rows, columns), 0) + here * rows_here - SWEEPS
        )
        inside = (grid_row >= 0) & (grid_row < grid_total)
        column = lax.broadcasted_iota(jnp.int32, (rows, columns), 1)
        sources, potentials = [], []
        for at in range(slabs):
            both = parcel_ref[0, at, :, 0 : 2 * orbitals]
            for device in range(1, energy_devices):
                both = both + parcel_ref[device, at, :, 0 : 2 * orbitals]
            density = (4.0 / total_energies) * (both[:, 0:orbitals] + both[:, orbitals:])
            index = grid_ref[at, 1].astype(jnp.int32)
            found = jnp.zeros((rows, columns), f32)
            for low in range(0, orbitals, LANES):
                table = jnp.broadcast_to(density[:, low : low + LANES], (rows, LANES))
                within = jnp.clip(index - low, 0, LANES - 1)
                value = jnp.take_along_axis(table, within, axis=1)
                found = jnp.where((index >= low) & (index < low + LANES), value, found)
            sources.append(CHARGE * found)
            potentials.append(grid_ref[at, 0])
        pivots = [MAIN_DIAGONAL]
        for at in range(1, slabs):
            pivots.append(MAIN_DIAGONAL - 1.0 / pivots[-1])
        for sweep in range(SWEEPS):
            eliminated = []
            for at in range(slabs):
                p = potentials[at]
                beside = (
                    pltpu.roll(p, 1, 0)
                    + pltpu.roll(p, rows - 1, 0)
                    + jnp.where(column == 0, 0.0, pltpu.roll(p, 1, 1))
                    + jnp.where(column == columns - 1, 0.0, pltpu.roll(p, columns - 1, 1))
                )
                right = sources[at] + ANISO * beside
                if at:
                    right = right + (1.0 / pivots[at - 1]) * eliminated[-1]
                eliminated.append(right)
            after = None
            for at in reversed(range(slabs)):
                value = eliminated[at] if after is None else eliminated[at] + after
                after = value * (1.0 / pivots[at])
                potentials[at] = jnp.where(inside, after, 0.0)
        for at in range(slabs):
            grid_ref[at, 0] = potentials[at]
        potential_ref[0] = grid_ref[slab, 0, SWEEPS : SWEEPS + rows_here, :]

    return call(
        kernel,
        (parcels,),
        [vmem()],
        [
            jax.ShapeDtypeStruct((1, 2, orbitals), f32),
            jax.ShapeDtypeStruct((1, rows_here, columns), f32),
        ],
        scratch_shapes=[pltpu.VMEM((slabs, 2, rows, columns), f32)],
    )


def per_device(
    onsite, hopping, coupling, boundary_green, damping, occupation, tile_map, prev_potential
):
    energy_devices, slabs = lax.axis_size("energy"), lax.axis_size("slab")
    orbitals = onsite.shape[1]
    assert boundary_green.shape[2] == SHIFT and energy_devices % 2 == 0
    total_energies = SHIFT * energy_devices

    swaps = [
        [pair for i in range(low, slabs - 1, 2) for pair in ((i, i + 1), (i + 1, i))]
        for low in (1, 0)
    ]
    last = energy_devices - 1
    pair = [(i, i ^ 1) for i in range(energy_devices)]
    far = [(i, i + 2) for i in range(1, last, 2) if i + 2 <= last]
    far += [(i, i - 2) for i in range(2, energy_devices, 2)]
    near = [(to, i) for i, to in far]

    common = (hopping, onsite)
    blocks = block_messages(boundary_green, coupling, damping, occupation)
    crossed = [lax.ppermute(part, "energy", pair) for part in blocks[:2]]
    own_sides = [[lax.ppermute(part, "slab", way) for way in swaps] for part in blocks[2:]]
    mine = own_self_energy(*own_sides, coupling, damping, occupation)
    early = lax.ppermute(mine, "energy", far)
    own_green, own_lesser = green_and_lesser([mine], *common, "own", total_energies)
    paired, late = [], []
    for plane, part in enumerate(crossed):
        sides = [lax.ppermute(part, "slab", way) for way in swaps]
        if plane:
            part, own_green = lax.optimization_barrier((part, own_green))
        paired.append(pair_self_energy(sides, coupling, own_sides[0], part))
        late.append(lax.ppermute(paired[-1], "energy", near))
    pair_green, pair_lesser = green_and_lesser(paired, *common, "pair", total_energies)
    parcels = pair_pass(
        early, paired, own_green, own_lesser, *common, tile_map, prev_potential, total_energies
    )
    parcels = own_pass(late, mine, pair_green, pair_lesser, *common, parcels, total_energies)
    parcels = lax.all_to_all(parcels, DEVICES, 0, 0)
    parcels = parcels.reshape(energy_devices, slabs, *parcels.shape[1:])
    return relax(parcels, orbitals, total_energies, *tile_map.shape[1:])


def solution(mesh):
    in_specs = (
        P("slab", None),
        P("slab", None, None),
        P("slab", None),
        P(None, "slab", "energy", None, None),
        P("slab", "energy"),
        P("slab", "energy"),
        P("slab", None, None),
        P("slab", None, None),
    )
    out_specs = (P("slab", "energy", None), P("slab", "energy", None))
    return jax.shard_map(
        per_device, mesh=mesh, in_specs=in_specs, out_specs=out_specs, check_vma=False
    )
```

time: 63.4 us -> 59.6 us (0.940)
  waiting for transfers between devices: 8.69 us -> 2.08 us
  starting transfers between devices: 23.3 us -> 25.1 us
  blocking collectives: 11 us -> 11.9 us
    ppermute x9 -> x12, waiting for transfers between devices: 8.69 us -> 2.08 us  [the longest x2 2.05 us: per_device(): crossed = [lax.ppermute(part, 'energy', pair) for part in blocks[:2]]]
    ppermute x9 -> x12, starting transfers between devices: 21.9 us -> 23.7 us  [the longest x2 8.36 us: per_device(): late.append(lax.ppermute(paired[-1], 'energy', near))]
    all_to_all x1, blocking collectives: 11 us -> 11.9 us  [per_device(): parcels = lax.all_to_all(parcels, DEVICES, 0, 0)]
    unnamed x14, local copies, waits for them, and re-layouts: 0.67 us -> 0.04 us
    pallas_call x8 -> x9, Pallas kernels: 18.6 us -> 19.2 us  [call(): pl.pallas_call(kernel, out_shape=shapes, in_specs=specs, out_specs=[vmem(...]
  transfers between devices with their start and end apart: 10 -> 13, of which waited for: 1 -> 1; matrix products, arithmetic and copies ran while one was open for 0% -> 0% of each run, Pallas kernels for 18% -> 20%
where the time goes in v2:
time: 59.6 us; the launch traced here: 59.2 us
  starting transfers between devices  25.1 us (42%)
  Pallas kernels  19.2 us (32%)
  blocking collectives  11.9 us (20%)
  waiting for transfers between devices  2.08 us (3%)
  between operations  0.89 us (1%)
    pallas_call x9, Pallas kernels, call(): pl.pallas_call(kernel, out_shape=shapes, in_specs=specs, out_specs=[vmem(...  19.2 us
    all_to_all x1, blocking collectives, per_device(): parcels = lax.all_to_all(parcels, DEVICES, 0, 0)  11.9 us
    ppermute x2, starting transfers between devices, per_device(): late.append(lax.ppermute(paired[-1], 'energy', near))  8.36 us
    ppermute x4, starting transfers between devices, per_device(): sides = [lax.ppermute(part, 'slab', way) for way in swaps]  7.24 us
    ppermute x4, starting transfers between devices, per_device(): lax.ppermute(part, 'slab', way)  4.91 us
    ppermute x2, starting transfers between devices, per_device(): crossed = [lax.ppermute(part, 'energy', pair) for part in blocks[:2]]  3.16 us
    ppermute x2, waiting for transfers between devices, per_device(): crossed = [lax.ppermute(part, 'energy', pair) for part in blocks[:2]]  2.05 us
    ppermute x1, starting transfers between devices, per_device(): early = lax.ppermute(mine, 'energy', far)  1.42 us
  transfers between devices with their start and end apart: 13, of which 1 were waited for; matrix products, arithmetic and copies ran while one was open for 0% of the time, Pallas kernels for 20%

profile of v2, /device:TPU:0, one launch (start us, length us, event | category | flops | bytes accessed | tf_op | source)
XLA Modules:
  0.0 59.2 jit_solution(16272724098791575970)
XLA Ops:
  0.6 1.5 %shard_map.95 = (f32[264,256]{1,0:T(8,128)S(1)}, f32[256,256]{1,0:T(8,128)S(1)}, f32[264,256]{1,0:T(8,128)S(1)}, f32[256,256]{1,0:T(8,128)S(1)}) custom-call(f32[2,1,2,256,256]{4,3,2,1,0:T(8,128)} %block_ref.1, f32[1,256]{1,0:T(1,128)} %coupling_ref.5, f32[1,2]{1,0:T(1,128)} %refs_5_.3, f32[1,2]{1,0:T(1,128)} %refs_6_.3), custom_call_target="tpu_custom_call" | custom-call | tf_op jit(solution)/shard_map/pallas_call | solution.py:164
  2.1 0.5 collective-permute-start.10
  2.6 2.6 %collective-permute-start = (f32[264,256]{1,0:T(8,128)S(1)}, f32[264,256]{1,0:T(8,128)S(1)}, u32[]{:S(2)}, u32[]{:S(2)}) collective-permute-start(f32[264,256]{1,0:T(8,128)S(1)} %get-tuple-element.12), channel_id=1, source_target_pairs={{0,4},{4,0},{8,12},{12,8},{16,20},{20,16},{24,28},{28,24},{1,5},{5... | collective-permute-start | bytes 811016 | tf_op jit(solution)/shard_map/ppermute | solution.py:473
  5.2 0.0 copy-start.6
  5.2 0.0 copy-start.4
  5.2 0.0 copy-start.5
  5.2 0.8 %collective-permute-start.3 = (f32[264,256]{1,0:T(8,128)S(1)}, f32[264,256]{1,0:T(8,128)S(1)}, u32[]{:S(2)}, u32[]{:S(2)}) collective-permute-start(f32[264,256]{1,0:T(8,128)S(1)} %get-tuple-element.13), channel_id=1, source_target_pairs={{1,2},{2,1},{5,6},{6,5},{9,10},{10,9},{13,14},{14,13},{17,18},{18,... | collective-permute-start | bytes 811016 | tf_op jit(solution)/shard_map/ppermute | solution.py:474
  6.0 2.9 %collective-permute-start.4 = (f32[264,256]{1,0:T(8,128)S(1)}, f32[264,256]{1,0:T(8,128)S(1)}, u32[]{:S(2)}, u32[]{:S(2)}) collective-permute-start(f32[264,256]{1,0:T(8,128)S(1)} %get-tuple-element.13), channel_id=1, source_target_pairs={{0,1},{1,0},{2,3},{3,2},{4,5},{5,4},{6,7},{7,6},{8,9},{9,8},{10,11... | collective-permute-start | bytes 811016 | tf_op jit(solution)/shard_map/ppermute | solution.py:474
  8.9 0.7 %collective-permute-start.9 = (f32[256,256]{1,0:T(8,128)S(1)}, f32[256,256]{1,0:T(8,128)S(1)}, u32[]{:S(2)}, u32[]{:S(2)}) collective-permute-start(f32[256,256]{1,0:T(8,128)S(1)} %get-tuple-element.15), channel_id=1, source_target_pairs={{1,2},{2,1},{5,6},{6,5},{9,10},{10,9},{13,14},{14,13},{17,18},{18,... | collective-permute-start | bytes 786440 | tf_op jit(solution)/shard_map/ppermute | solution.py:474
  9.6 0.0 collective-permute-done.10.refs_3_
  9.6 0.6 %collective-permute-start.6 = (f32[256,256]{1,0:T(8,128)S(1)}, f32[256,256]{1,0:T(8,128)S(1)}, u32[]{:S(2)}, u32[]{:S(2)}) collective-permute-start(f32[256,256]{1,0:T(8,128)S(1)} %get-tuple-element.14), channel_id=1, source_target_pairs={{0,4},{4,0},{8,12},{12,8},{16,20},{20,16},{24,28},{28,24},{1,5},{5... | collective-permute-start | bytes 786440 | tf_op jit(solution)/shard_map/ppermute | solution.py:473
  10.2 2.0 %collective-permute-done.crossed_ref = f32[264,256]{1,0:T(8,128)S(1)} collective-permute-done((f32[264,256]{1,0:T(8,128)S(1)}, f32[264,256]{1,0:T(8,128)S(1)}, u32[]{:S(2)}, u32[]{:S(2)}) %collective-permute-start) | collective-permute-done | bytes 270368 | tf_op jit(solution)/shard_map/ppermute | solution.py:473
  12.2 0.7 %collective-permute-start.1 = (f32[264,256]{1,0:T(8,128)S(1)}, f32[264,256]{1,0:T(8,128)S(1)}, u32[]{:S(2)}, u32[]{:S(2)}) collective-permute-start(f32[264,256]{1,0:T(8,128)S(1)} %collective-permute-done.crossed_ref), channel_id=1, source_target_pairs={{1,2},{2,1},{5,6},{6,5},{9,10},{10,9},{13,14},{14,13},{17,18},{18,... | collective-permute-start | bytes 811016 | tf_op jit(solution)/shard_map/ppermute | solution.py:480
  12.9 0.0 collective-permute-done.9.refs_2_
  12.9 4.0 %collective-permute-start.2 = (f32[264,256]{1,0:T(8,128)S(1)}, f32[264,256]{1,0:T(8,128)S(1)}, u32[]{:S(2)}, u32[]{:S(2)}) collective-permute-start(f32[264,256]{1,0:T(8,128)S(1)} %collective-permute-done.crossed_ref), channel_id=1, source_target_pairs={{0,1},{1,0},{2,3},{3,2},{4,5},{5,4},{6,7},{7,6},{8,9},{9,8},{10,11... | collective-permute-start | bytes 811016 | tf_op jit(solution)/shard_map/ppermute | solution.py:480
  16.9 0.0 collective-permute-done.3.own_outer_ref.refs_0_
  16.9 0.0 collective-permute-done.4.own_inner_ref.refs_1_
  16.9 0.0 copy-done.6
  16.9 0.0 copy-done.4
  16.9 0.0 copy-done.5
  16.9 0.8 %shard_map.97.refs_0_.refs_2_ = f32[520,256]{1,0:T(8,128)S(1)} custom-call(f32[264,256]{1,0:T(8,128)S(1)} %collective-permute-done.3.own_outer_ref.refs_0_, f32[264,256]{1,0:T(8,128)S(1)} %collective-permute-done.4.own_inner_ref.refs_1_, f32[256,256]{1,0:T(8,128)S(1)} %collective-permute-done.9.refs_2_, f32[256,256]{1,0:T(8,128)S(1)} %collective-permute-done.10.refs_3_, ...), custom_call_target="tpu_custom_call" | custom-call | tf_op jit(solution)/shard_map/pallas_call | solution.py:164
  17.8 0.0 copy-start
  17.8 0.0 copy-start.3
  17.8 1.4 %collective-permute-start.12 = (f32[520,256]{1,0:T(8,128)S(1)}, f32[520,256]{1,0:T(8,128)S(1)}, u32[]{:S(2)}, u32[]{:S(2)}) collective-permute-start(f32[520,256]{1,0:T(8,128)S(1)} %shard_map.97.refs_0_.refs_2_), channel_id=1, source_target_pairs={{4,12},{12,20},{20,28},{8,0},{16,8},{24,16},{5,13},{13,21},{21,29}... | collective-permute-start | bytes 1597448 | tf_op jit(solution)/shard_map/ppermute | solution.py:476
  19.2 0.0 collective-permute-done.6.crossed_ref
  19.2 0.7 %collective-permute-start.7 = (f32[256,256]{1,0:T(8,128)S(1)}, f32[256,256]{1,0:T(8,128)S(1)}, u32[]{:S(2)}, u32[]{:S(2)}) collective-permute-start(f32[256,256]{1,0:T(8,128)S(1)} %collective-permute-done.6.crossed_ref), channel_id=1, source_target_pairs={{1,2},{2,1},{5,6},{6,5},{9,10},{10,9},{13,14},{14,13},{17,18},{18,... | collective-permute-start | bytes 786440 | tf_op jit(solution)/shard_map/ppermute | solution.py:480
  19.9 1.9 %collective-permute-start.8 = (f32[256,256]{1,0:T(8,128)S(1)}, f32[256,256]{1,0:T(8,128)S(1)}, u32[]{:S(2)}, u32[]{:S(2)}) collective-permute-start(f32[256,256]{1,0:T(8,128)S(1)} %collective-permute-done.6.crossed_ref), channel_id=1, source_target_pairs={{0,1},{1,0},{2,3},{3,2},{4,5},{5,4},{6,7},{7,6},{8,9},{9,8},{10,11... | collective-permute-start | bytes 786440 | tf_op jit(solution)/shard_map/ppermute | solution.py:480
  21.8 0.0 collective-permute-done.1.outer_ref
  21.9 0.0 collective-permute-done.2.inner_ref
  21.9 0.3 shard_map.96.refs_0_.refs_1_
  22.1 4.6 %collective-permute-start.5 = (f32[264,256]{1,0:T(8,128)S(1)}, f32[264,256]{1,0:T(8,128)S(1)}, u32[]{:S(2)}, u32[]{:S(2)}) collective-permute-start(f32[264,256]{1,0:T(8,128)S(1)} %shard_map.96.refs_0_.refs_1_), channel_id=1, source_target_pairs={{12,4},{20,12},{28,20},{0,8},{8,16},{16,24},{13,5},{21,13},{29,21}... | collective-permute-start | bytes 811016 | tf_op jit(solution)/shard_map/ppermute | solution.py:484
  26.7 0.0 copy-done
  26.7 0.0 copy-done.3
  26.7 2.7 %shard_map.98 = (f32[2,256,256]{2,1,0:T(8,128)S(1)}, f32[2,256,256]{2,1,0:T(8,128)S(1)}) custom-call(f32[520,256]{1,0:T(8,128)S(1)} %shard_map.97.refs_0_.refs_2_, f32[1,256,256]{2,1,0:T(8,128)S(1)} %copy-done, f32[1,256]{1,0:T(1,128)S(1)} %copy-done.3), custom_call_target="tpu_custom_call" | custom-call | tf_op jit(solution)/shard_map/pallas_call | solution.py:164
  29.4 0.0 collective-permute-done.7.outer_ref
  29.4 0.0 collective-permute-done.8.inner_ref
  29.4 0.3 shard_map.99.refs_1_.refs_2_
  29.7 0.0 copy-start.1
  29.7 0.0 copy-start.2
  29.7 3.8 %collective-permute-start.11 = (f32[256,256]{1,0:T(8,128)S(1)}, f32[256,256]{1,0:T(8,128)S(1)}, u32[]{:S(2)}, u32[]{:S(2)}) collective-permute-start(f32[256,256]{1,0:T(8,128)S(1)} %shard_map.99.refs_1_.refs_2_), channel_id=1, source_target_pairs={{12,4},{20,12},{28,20},{0,8},{8,16},{16,24},{13,5},{21,13},{29,21}... | collective-permute-start | bytes 786440 | tf_op jit(solution)/shard_map/ppermute | solution.py:484
  33.5 2.7 %shard_map.100 = (f32[2,256,256]{2,1,0:T(8,128)S(1)}, f32[2,256,256]{2,1,0:T(8,128)S(1)}) custom-call(f32[264,256]{1,0:T(8,128)S(1)} %shard_map.96.refs_0_.refs_1_, f32[256,256]{1,0:T(8,128)S(1)} %shard_map.99.refs_1_.refs_2_, f32[1,256,256]{2,1,0:T(8,128)S(1)} %copy-done, f32[1,256]{1,0:T(1,128)S(1)} %copy-done.3), custom_call_target="tpu_custom_call" | custom-call | tf_op jit(solution)/shard_map/pallas_call | solution.py:164
  36.2 0.0 collective-permute-done.12.refs_0_
  36.2 0.0 copy-done.1
  36.2 0.0 copy-done.2
  36.2 5.1 %shard_map.101.refs_7_ = f32[32,1,1152]{2,1,0:T(1,128)S(1)} custom-call(f32[520,256]{1,0:T(8,128)S(1)} %collective-permute-done.12.refs_0_, f32[264,256]{1,0:T(8,128)S(1)} %shard_map.96.refs_0_.refs_1_, f32[256,256]{1,0:T(8,128)S(1)} %shard_map.99.refs_1_.refs_2_, f32[2,256,256]{2,1,0:T(8,128)S(1)} %get-tuple-element.20.refs_3_, ...), custom_call_target="tpu_custom_call" | custom-call | tf_op jit(solution)/shard_map/pallas_call | solution.py:164
  41.3 0.0 collective-permute-done.11.refs_1_
  41.3 0.0 collective-permute-done.5.refs_0_
  41.3 5.1 %shard_map.102 = f32[32,1,1152]{2,1,0:T(1,128)S(1)} custom-call(f32[264,256]{1,0:T(8,128)S(1)} %collective-permute-done.5.refs_0_, f32[256,256]{1,0:T(8,128)S(1)} %collective-permute-done.11.refs_1_, f32[520,256]{1,0:T(8,128)S(1)} %shard_map.97.refs_0_.refs_2_, f32[2,256,256]{2,1,0:T(8,128)S(1)} %get-tuple-element.18.refs_3_, ...), custom_call_target="tpu_custom_call", output_to_operand_aliasing={{}: (7, {})} | custom-call | tf_op jit(solution)/shard_map/pallas_call | solution.py:164
  46.4 11.9 %all_to_all.5 = f32[32,1,1152]{2,1,0:T(1,128)S(1)} all-to-all(f32[32,1,1152]{2,1,0:T(1,128)S(1)} %shard_map.102), channel_id=1, replica_groups=mesh['energy'=8,'slab'=4] {'energy','slab'}, dimensions={0} | all-to-all | bytes 294912 | tf_op jit(solution)/shard_map/all_to_all | solution.py:490
  58.3 0.9 %shard_map.103 = (f32[1,2,256]{2,1,0:T(2,128)}, f32[1,16,128]{2,1,0:T(8,128)}) custom-call(f32[8,4,1,1152]{3,2,1,0:T(1,128)S(1)} %bitcast.1), custom_call_target="tpu_custom_call" | custom-call | tf_op jit(solution)/shard_map/pallas_call | solution.py:164
Async XLA Ops:
  2.1 7.5 %collective-permute-start.10 = (f32[256,256]{1,0:T(8,128)S(1)}, f32[256,256]{1,0:T(8,128)S(1)}, u32[]{:S(2)}, u32[]{:S(2)}) collective-permute-start(f32[256,256]{1,0:T(8,128)S(1)} %get-tuple-element.15), channel_id=1, source_target_pairs={{0,1},{1,0},{2,3},{3,2},{4,5},{5,4},{6,7},{7,6},{8,9},{9,8},{10,11... | collective-permute-start | bytes 786440 | tf_op jit(solution)/shard_map/ppermute | solution.py:474
  2.6 9.6 %collective-permute-start = (f32[264,256]{1,0:T(8,128)S(1)}, f32[264,256]{1,0:T(8,128)S(1)}, u32[]{:S(2)}, u32[]{:S(2)}) collective-permute-start(f32[264,256]{1,0:T(8,128)S(1)} %get-tuple-element.12), channel_id=1, source_target_pairs={{0,4},{4,0},{8,12},{12,8},{16,20},{20,16},{24,28},{28,24},{1,5},{5... | collective-permute-start | bytes 811016 | tf_op jit(solution)/shard_map/ppermute | solution.py:473
  5.2 11.8 %copy-start.6 = (f32[1,2]{1,0:T(1,128)S(1)}, f32[1,2]{1,0:T(1,128)}, u32[]{:S(2)}) copy-start(f32[1,2]{1,0:T(1,128)} %refs_6_.3) | copy-start | bytes 28
  5.2 11.8 %copy-start.4 = (f32[1,256]{1,0:T(1,128)S(1)}, f32[1,256]{1,0:T(1,128)}, u32[]{:S(2)}) copy-start(f32[1,256]{1,0:T(1,128)} %coupling_ref.5) | copy-start | bytes 3076
  5.2 11.8 %copy-start.5 = (f32[1,2]{1,0:T(1,128)S(1)}, f32[1,2]{1,0:T(1,128)}, u32[]{:S(2)}) copy-start(f32[1,2]{1,0:T(1,128)} %refs_5_.3) | copy-start | bytes 28
  5.2 11.7 %collective-permute-start.3 = (f32[264,256]{1,0:T(8,128)S(1)}, f32[264,256]{1,0:T(8,128)S(1)}, u32[]{:S(2)}, u32[]{:S(2)}) collective-permute-start(f32[264,256]{1,0:T(8,128)S(1)} %get-tuple-element.13), channel_id=1, source_target_pairs={{1,2},{2,1},{5,6},{6,5},{9,10},{10,9},{13,14},{14,13},{17,18},{18,... | collective-permute-start | bytes 811016 | tf_op jit(solution)/shard_map/ppermute | solution.py:474
  6.0 10.9 %collective-permute-start.4 = (f32[264,256]{1,0:T(8,128)S(1)}, f32[264,256]{1,0:T(8,128)S(1)}, u32[]{:S(2)}, u32[]{:S(2)}) collective-permute-start(f32[264,256]{1,0:T(8,128)S(1)} %get-tuple-element.13), channel_id=1, source_target_pairs={{0,1},{1,0},{2,3},{3,2},{4,5},{5,4},{6,7},{7,6},{8,9},{9,8},{10,11... | collective-permute-start | bytes 811016 | tf_op jit(solution)/shard_map/ppermute | solution.py:474
  8.9 4.0 %collective-permute-start.9 = (f32[256,256]{1,0:T(8,128)S(1)}, f32[256,256]{1,0:T(8,128)S(1)}, u32[]{:S(2)}, u32[]{:S(2)}) collective-permute-start(f32[256,256]{1,0:T(8,128)S(1)} %get-tuple-element.15), channel_id=1, source_target_pairs={{1,2},{2,1},{5,6},{6,5},{9,10},{10,9},{13,14},{14,13},{17,18},{18,... | collective-permute-start | bytes 786440 | tf_op jit(solution)/shard_map/ppermute | solution.py:474
  9.6 9.6 %collective-permute-start.6 = (f32[256,256]{1,0:T(8,128)S(1)}, f32[256,256]{1,0:T(8,128)S(1)}, u32[]{:S(2)}, u32[]{:S(2)}) collective-permute-start(f32[256,256]{1,0:T(8,128)S(1)} %get-tuple-element.14), channel_id=1, source_target_pairs={{0,4},{4,0},{8,12},{12,8},{16,20},{20,16},{24,28},{28,24},{1,5},{5... | collective-permute-start | bytes 786440 | tf_op jit(solution)/shard_map/ppermute | solution.py:473
  12.2 9.6 %collective-permute-start.1 = (f32[264,256]{1,0:T(8,128)S(1)}, f32[264,256]{1,0:T(8,128)S(1)}, u32[]{:S(2)}, u32[]{:S(2)}) collective-permute-start(f32[264,256]{1,0:T(8,128)S(1)} %collective-permute-done.crossed_ref), channel_id=1, source_target_pairs={{1,2},{2,1},{5,6},{6,5},{9,10},{10,9},{13,14},{14,13},{17,18},{18,... | collective-permute-start | bytes 811016 | tf_op jit(solution)/shard_map/ppermute | solution.py:480
  12.9 8.9 %collective-permute-start.2 = (f32[264,256]{1,0:T(8,128)S(1)}, f32[264,256]{1,0:T(8,128)S(1)}, u32[]{:S(2)}, u32[]{:S(2)}) collective-permute-start(f32[264,256]{1,0:T(8,128)S(1)} %collective-permute-done.crossed_ref), channel_id=1, source_target_pairs={{0,1},{1,0},{2,3},{3,2},{4,5},{5,4},{6,7},{7,6},{8,9},{9,8},{10,11... | collective-permute-start | bytes 811016 | tf_op jit(solution)/shard_map/ppermute | solution.py:480
  17.8 8.9 %copy-start = (f32[1,256,256]{2,1,0:T(8,128)S(1)}, f32[1,256,256]{2,1,0:T(8,128)}, u32[]{:S(2)}) copy-start(f32[1,256,256]{2,1,0:T(8,128)} %refs_5_.5) | copy-start | bytes 786436
  17.8 8.9 %copy-start.3 = (f32[1,256]{1,0:T(1,128)S(1)}, f32[1,256]{1,0:T(1,128)}, u32[]{:S(2)}) copy-start(f32[1,256]{1,0:T(1,128)} %refs_6_.5) | copy-start | bytes 3076
  17.8 18.4 %collective-permute-start.12 = (f32[520,256]{1,0:T(8,128)S(1)}, f32[520,256]{1,0:T(8,128)S(1)}, u32[]{:S(2)}, u32[]{:S(2)}) collective-permute-start(f32[520,256]{1,0:T(8,128)S(1)} %shard_map.97.refs_0_.refs_2_), channel_id=1, source_target_pairs={{4,12},{12,20},{20,28},{8,0},{16,8},{24,16},{5,13},{13,21},{21,29}... | collective-permute-start | bytes 1597448 | tf_op jit(solution)/shard_map/ppermute | solution.py:476
  19.2 10.2 %collective-permute-start.7 = (f32[256,256]{1,0:T(8,128)S(1)}, f32[256,256]{1,0:T(8,128)S(1)}, u32[]{:S(2)}, u32[]{:S(2)}) collective-permute-start(f32[256,256]{1,0:T(8,128)S(1)} %collective-permute-done.6.crossed_ref), channel_id=1, source_target_pairs={{1,2},{2,1},{5,6},{6,5},{9,10},{10,9},{13,14},{14,13},{17,18},{18,... | collective-permute-start | bytes 786440 | tf_op jit(solution)/shard_map/ppermute | solution.py:480
  19.9 9.5 %collective-permute-start.8 = (f32[256,256]{1,0:T(8,128)S(1)}, f32[256,256]{1,0:T(8,128)S(1)}, u32[]{:S(2)}, u32[]{:S(2)}) collective-permute-start(f32[256,256]{1,0:T(8,128)S(1)} %collective-permute-done.6.crossed_ref), channel_id=1, source_target_pairs={{0,1},{1,0},{2,3},{3,2},{4,5},{5,4},{6,7},{7,6},{8,9},{9,8},{10,11... | collective-permute-start | bytes 786440 | tf_op jit(solution)/shard_map/ppermute | solution.py:480
  22.1 19.2 %collective-permute-start.5 = (f32[264,256]{1,0:T(8,128)S(1)}, f32[264,256]{1,0:T(8,128)S(1)}, u32[]{:S(2)}, u32[]{:S(2)}) collective-permute-start(f32[264,256]{1,0:T(8,128)S(1)} %shard_map.96.refs_0_.refs_1_), channel_id=1, source_target_pairs={{12,4},{20,12},{28,20},{0,8},{8,16},{16,24},{13,5},{21,13},{29,21}... | collective-permute-start | bytes 811016 | tf_op jit(solution)/shard_map/ppermute | solution.py:484
  29.7 6.5 %copy-start.1 = (s32[1,128,128]{2,1,0:T(8,128)S(1)}, s32[1,128,128]{2,1,0:T(8,128)}, u32[]{:S(2)}) copy-start(s32[1,128,128]{2,1,0:T(8,128)} %refs_7_.1) | copy-start | bytes 196612
  29.7 6.5 %copy-start.2 = (f32[1,128,128]{2,1,0:T(8,128)S(1)}, f32[1,128,128]{2,1,0:T(8,128)}, u32[]{:S(2)}) copy-start(f32[1,128,128]{2,1,0:T(8,128)} %refs_8_.1) | copy-start | bytes 196612
  29.7 11.6 %collective-permute-start.11 = (f32[256,256]{1,0:T(8,128)S(1)}, f32[256,256]{1,0:T(8,128)S(1)}, u32[]{:S(2)}, u32[]{:S(2)}) collective-permute-start(f32[256,256]{1,0:T(8,128)S(1)} %shard_map.99.refs_1_.refs_2_), channel_id=1, source_target_pairs={{12,4},{20,12},{28,20},{0,8},{8,16},{16,24},{13,5},{21,13},{29,21}... | collective-permute-start | bytes 786440 | tf_op jit(solution)/shard_map/ppermute | solution.py:484

commit v3 on v2

--- a/solution.py
+++ b/solution.py
@@ -16,6 +16,7 @@
 MAIN_DIAGONAL = 2.0 + 4.0 * ANISO + SCREEN
 LANES = 128
 SUBLANES = 8
+CROSS_ROWS = 8
 VMEM_BYTES = 48 * 1024 * 1024
 
 f32 = jnp.float32
@@ -30,11 +31,13 @@
 
 def dot(left, right, transposed=False):
     contract = (((1,), (1 if transposed else 0,)), ((), ()))
-    out = [
-        lax.dot_general(left[i], right[j], contract, preferred_element_type=f32)
-        for i, j in ((0, 0), (1, 0), (0, 1))
-    ]
-    return out[0] + out[1] + out[2]
+
+    def multiply(a, b):
+        return lax.dot_general(a, b, contract, preferred_element_type=f32)
+
+    size = left[0].shape[0]
+    both = multiply(jnp.concatenate(left, axis=0), right[0])
+    return both[:size] + both[size:] + multiply(left[0], right[1])
 
 
 def factor(matrix):
@@ -155,10 +158,6 @@
     return pl.BlockSpec(memory_space=pltpu.VMEM)
 
 
-def smem():
-    return pl.BlockSpec(memory_space=pltpu.SMEM)
-
-
 def call(kernel, operands, specs, shapes, **options):
     several = isinstance(shapes, list)
     return pl.pallas_call(
@@ -177,12 +176,12 @@
 
     def kernel(block_ref, coupling_ref, *refs):
         level_refs, (real_ref, imag_ref), own_refs = refs[:2], refs[2:4], refs[4:6]
-        held_refs, sems = refs[6:8], refs[8]
+        own_levels_ref, held_refs, sems = refs[6], refs[7:9], refs[9]
         parity = lax.rem(lax.axis_index("energy"), SHIFT)
         moves = [
             (block_ref.at[0, 0, 1 - parity], real_ref.at[pl.ds(0, rows)]),
             *zip(level_refs, held_refs),
-            (block_ref.at[1, 0, 1 - parity], imag_ref),
+            (block_ref.at[1, 0, 1 - parity], imag_ref.at[pl.ds(0, rows)]),
             (block_ref.at[0, 0, parity], own_refs[0].at[pl.ds(0, rows)]),
             (coupling_ref, own_refs[0].at[pl.ds(rows, 1)]),
             (block_ref.at[1, 0, parity], own_refs[1]),
@@ -195,11 +194,14 @@
             copy.start()
         for copy in copies:
             copy.wait()
+        damping_here, occupation_here = (held_ref[...] for held_ref in held_refs)
+        which = lax.broadcasted_iota(jnp.int32, (SUBLANES, columns), 0)
         levels = [
-            jnp.where(parity == 0, held_ref[0:1, 1:2], held_ref[0:1, 0:1]) for held_ref in held_refs
+            jnp.where(which == 0, damping_here[:, at : at + 1], occupation_here[:, at : at + 1])
+            for at in range(SHIFT)
         ]
-        which = lax.broadcasted_iota(jnp.int32, (SUBLANES, columns), 0)
-        real_ref[rows:, :] = jnp.where(which == 0, levels[0], levels[1])
+        real_ref[rows : rows + SUBLANES, :] = jnp.where(parity == 0, levels[1], levels[0])
+        own_levels_ref[...] = jnp.where(parity == 0, levels[0], levels[1])
 
     operands = (boundary_green, coupling, damping, occupation)
     return call(
@@ -208,7 +210,7 @@
         [pl.BlockSpec(memory_space=pltpu.HBM)] * 4,
         [
             jax.ShapeDtypeStruct((height, columns), f32)
-            for height in (rows + SUBLANES, rows) * 2
+            for height in (rows + CROSS_ROWS, rows + CROSS_ROWS, rows + SUBLANES, rows, SUBLANES)
         ],
         scratch_shapes=[
             pltpu.VMEM(damping.shape, f32),
@@ -228,40 +230,37 @@
     return weights
 
 
-def own_self_energy(real_sides, imag_sides, coupling, damping, occupation):
+def own_self_energy(real_sides, imag_sides, coupling, levels):
     columns = coupling.shape[1]
 
     def kernel(*refs):
         real_refs, imag_refs = refs[:2], refs[2:4]
-        coupling_ref, damping_ref, occupation_ref, out_ref = refs[4:]
+        coupling_ref, levels_ref, out_ref = refs[4:]
         weights = slab_weights(coupling_ref, real_refs)
         rows = pl.ds(0, columns)
         for low, side_refs in ((0, imag_refs), (columns, real_refs)):
             outer, inner = (w * ref[rows, :] for w, ref in zip(weights, side_refs))
             out_ref[pl.ds(low, columns), :] = outer + inner
-        parity = lax.rem(lax.axis_index("energy"), SHIFT)
-        which = lax.broadcasted_iota(jnp.int32, (SUBLANES, columns), 0)
-        out_ref[2 * columns :, :] = jnp.where(
-            which == 0, damping_ref[0, parity], occupation_ref[0, parity]
-        )
+        out_ref[2 * columns :, :] = levels_ref[...]
 
     return call(
         kernel,
-        (*real_sides, *imag_sides, coupling, damping, occupation),
-        [vmem()] * 5 + [smem()] * 2,
+        (*real_sides, *imag_sides, coupling, levels),
+        [vmem()] * 6,
         jax.ShapeDtypeStruct((2 * columns + SUBLANES, columns), f32),
     )
 
 
-def pair_self_energy(sides, coupling, own_sides, crossed):
-    height, columns = crossed.shape
+def pair_self_energy(sides, coupling, own_sides, crossed, extra):
+    columns = crossed.shape[1]
+    height = columns + extra
 
     def kernel(outer_ref, inner_ref, coupling_ref, own_outer_ref, own_inner_ref, crossed_ref, out_ref):
         outer_weight, inner_weight = slab_weights(coupling_ref, (own_outer_ref, own_inner_ref))
         rows = pl.ds(0, columns)
         out_ref[rows, :] = outer_weight * outer_ref[rows, :] + inner_weight * inner_ref[rows, :]
-        if height > columns:
-            out_ref[columns:, :] = crossed_ref[columns:, :]
+        if extra:
+            out_ref[columns:, :] = crossed_ref[columns:height, :]
 
     operands = (*sides, coupling, *own_sides, crossed)
     return call(kernel, operands, [vmem()] * 6, jax.ShapeDtypeStruct((height, columns), f32))
@@ -297,12 +296,14 @@
     grid_total, columns = tile_map.shape[1:]
     rows_here = grid_total // energy_devices
     needed, share = grid_share(rows_here, energy_devices)
-    padded = grid_total + 2 * SWEEPS
+    rows = -(-needed // SUBLANES) * SUBLANES
+    padded = grid_total + SUBLANES
+    length = max(share * columns, size)
 
     def kernel(*refs):
         early_refs, paired_refs, refs = refs[:1], refs[1:3], refs[3:]
         green_ref, lesser_ref, hopping_ref, onsite_ref, tile_ref, potential_ref = refs[:6]
-        parcel_ref, grid_ref = refs[6:]
+        parcel_ref, row_ref, local_ref, grid_ref = refs[6:]
         chains = chain_places()
         here = Element(paired_refs, hopping_ref, onsite_ref, chains["pair"], total_energies)
         beyond = Element(early_refs, hopping_ref, onsite_ref, chains["early"], total_energies)
@@ -311,41 +312,58 @@
             [beyond_green, (green_ref[0], green_ref[1])],
             [beyond_lesser, (lesser_ref[0], lesser_ref[1])],
         )
-        border = jnp.zeros((SWEEPS, columns), f32)
+        row_ref[...] = row
+        at_energy, at_slab = lax.axis_index("energy"), lax.axis_index("slab")
+        border = jnp.zeros((SUBLANES, columns), f32)
         for at, plane in enumerate((potential_ref[0], tile_ref[0].astype(f32))):
             low = at * padded
-            grid_ref[low : low + SWEEPS, :] = border
+            grid_ref[low : low + SUBLANES, :] = border
+            grid_ref[low + padded - SUBLANES : low + padded, :] = border
             grid_ref[low + SWEEPS : low + SWEEPS + grid_total, :] = plane
-            grid_ref[low + SWEEPS + grid_total : low + padded, :] = border
-        first = lax.axis_index("energy") * share
+        for at in range(2):
+            low = pl.multiple_of(at * padded + at_energy * rows_here, SUBLANES)
+            local_ref[at] = grid_ref[pl.ds(low, rows), :]
+        first = at_energy * share
+
+        def filled(pieces):
+            piece = jnp.concatenate(pieces, axis=1)
+            short = length - piece.shape[1]
+            if short:
+                piece = jnp.concatenate([piece, jnp.zeros((1, short), f32)], axis=1)
+            return piece
+
+        same = filled([row])
         for to in range(energy_devices):
-            pieces = [row]
+            pieces = []
             for i in range(share):
                 place = jnp.minimum(first + i, 2 * needed - 1)
                 which = (place >= needed).astype(jnp.int32)
                 source = which * (padded - needed) + place + to * rows_here
                 pieces.append(grid_ref[pl.ds(source, 1), :])
-            parcel = jnp.concatenate(pieces, axis=1)
+            other = filled(pieces)
             for slab in range(slabs):
-                parcel_ref[to * slabs + slab, :, size:] = parcel
+                parcel_ref[to * slabs + slab, :, size:] = jnp.where(at_slab == slab, same, other)
 
     operands = [early, *paired, green, lesser, hopping, onsite, tile_map, potential]
-    parcels = (energy_devices * slabs, 1, 2 * size + share * columns)
     return call(
         kernel,
         operands,
         [vmem()] * len(operands),
-        jax.ShapeDtypeStruct(parcels, f32),
+        [
+            jax.ShapeDtypeStruct((energy_devices * slabs, 1, size + length), f32),
+            jax.ShapeDtypeStruct((1, size), f32),
+            jax.ShapeDtypeStruct((2, rows, columns), f32),
+        ],
         scratch_shapes=[pltpu.VMEM((2 * padded, columns), f32)],
     )
 
 
-def own_pass(late, mine, green, lesser, hopping, onsite, parcels, total_energies):
+def own_pass(late, mine, green, lesser, hopping, onsite, parcels, other_row, total_energies):
     size = hopping.shape[-1]
 
     def kernel(*refs):
         late_refs, mine_refs, refs = refs[:2], refs[2:3], refs[3:]
-        green_ref, lesser_ref, hopping_ref, onsite_ref, _, parcel_ref = refs
+        green_ref, lesser_ref, hopping_ref, onsite_ref, other_ref, _, parcel_ref, row_ref = refs
         chains = chain_places()
         here = Element(mine_refs, hopping_ref, onsite_ref, chains["own"], total_energies)
         beyond = Element(late_refs, hopping_ref, onsite_ref, chains["late"], total_energies)
@@ -354,32 +372,37 @@
             [beyond_green, (green_ref[0], green_ref[1])],
             [beyond_lesser, (lesser_ref[0], lesser_ref[1])],
         )
+        row_ref[...] = row
+        both = row + other_ref[...]
         for to in range(parcel_ref.shape[0]):
-            parcel_ref[to, :, 0:size] = row
-
-    operands = [*late, mine, green, lesser, hopping, onsite, parcels]
+            parcel_ref[to, :, 0:size] = both
+
+    operands = [*late, mine, green, lesser, hopping, onsite, other_row, parcels]
     return call(
         kernel,
         operands,
         [vmem()] * len(operands),
-        jax.ShapeDtypeStruct(parcels.shape, f32),
+        [
+            jax.ShapeDtypeStruct(parcels.shape, f32),
+            jax.ShapeDtypeStruct(other_row.shape, f32),
+        ],
         input_output_aliases={len(operands) - 1: 0},
     )
 
 
-def relax(parcels, orbitals, total_energies, grid_total, columns):
+def relax(parcels, own_row, local, orbitals, total_energies, grid_total, columns):
     energy_devices, slabs = parcels.shape[:2]
     rows_here = grid_total // energy_devices
     needed, share = grid_share(rows_here, energy_devices)
-    rows = -(-needed // SUBLANES) * SUBLANES
-
-    def kernel(parcel_ref, lesser_ref, potential_ref, grid_ref):
+    rows = local.shape[1]
+
+    def kernel(parcel_ref, own_ref, local_ref, lesser_ref, potential_ref, grid_ref):
         here, slab = lax.axis_index("energy"), lax.axis_index("slab")
         odd = lax.rem(here, 2)
+        pair_row = parcel_ref[here + 1 - 2 * odd, slab, :, orbitals : 2 * orbitals]
         for parity in range(2):
-            both = parcel_ref[here - odd + parity, slab, :, 0 : 2 * orbitals]
             lesser_ref[0, parity : parity + 1, :] = jnp.where(
-                odd == parity, both[:, 0:orbitals], both[:, orbitals:]
+                odd == parity, own_ref[...], pair_row
             )
         empty = jnp.zeros((rows - needed, columns), f32)
         for at in range(slabs):
@@ -387,11 +410,12 @@
                 if rows > needed:
                     grid_ref[at, which, needed:, :] = empty
             for place in range(2 * needed):
-                device, low = place // share, 2 * orbitals + place % share * columns
+                device, low = place // share, orbitals + place % share * columns
                 row = place % needed
                 grid_ref[at, place // needed, row : row + 1, :] = parcel_ref[
                     device, at, :, low : low + columns
                 ]
+        grid_ref[slab] = local_ref[...]
         grid_row = (
             lax.broadcasted_iota(jnp.int32, (rows, columns), 0) + here * rows_here - SWEEPS
         )
@@ -399,10 +423,10 @@
         column = lax.broadcasted_iota(jnp.int32, (rows, columns), 1)
         sources, potentials = [], []
         for at in range(slabs):
-            both = parcel_ref[0, at, :, 0 : 2 * orbitals]
+            total = parcel_ref[0, at, :, 0:orbitals]
             for device in range(1, energy_devices):
-                both = both + parcel_ref[device, at, :, 0 : 2 * orbitals]
-            density = (4.0 / total_energies) * (both[:, 0:orbitals] + both[:, orbitals:])
+                total = total + parcel_ref[device, at, :, 0:orbitals]
+            density = (4.0 / total_energies) * total
             index = grid_ref[at, 1].astype(jnp.int32)
             found = jnp.zeros((rows, columns), f32)
             for low in range(0, orbitals, LANES):
@@ -440,8 +464,8 @@
 
     return call(
         kernel,
-        (parcels,),
-        [vmem()],
+        (parcels, own_row, local),
+        [vmem()] * 3,
         [
             jax.ShapeDtypeStruct((1, 2, orbitals), f32),
             jax.ShapeDtypeStruct((1, rows_here, columns), f32),
@@ -471,8 +495,8 @@
     common = (hopping, onsite)
     blocks = block_messages(boundary_green, coupling, damping, occupation)
     crossed = [lax.ppermute(part, "energy", pair) for part in blocks[:2]]
-    own_sides = [[lax.ppermute(part, "slab", way) for way in swaps] for part in blocks[2:]]
-    mine = own_self_energy(*own_sides, coupling, damping, occupation)
+    own_sides = [[lax.ppermute(part, "slab", way) for way in swaps] for part in blocks[2:4]]
+    mine = own_self_energy(*own_sides, coupling, blocks[4])
     early = lax.ppermute(mine, "energy", far)
     own_green, own_lesser = green_and_lesser([mine], *common, "own", total_energies)
     paired, late = [], []
@@ -480,16 +504,19 @@
         sides = [lax.ppermute(part, "slab", way) for way in swaps]
         if plane:
             part, own_green = lax.optimization_barrier((part, own_green))
-        paired.append(pair_self_energy(sides, coupling, own_sides[0], part))
+        extra = 0 if plane else SUBLANES
+        paired.append(pair_self_energy(sides, coupling, own_sides[0], part, extra))
         late.append(lax.ppermute(paired[-1], "energy", near))
     pair_green, pair_lesser = green_and_lesser(paired, *common, "pair", total_energies)
-    parcels = pair_pass(
+    parcels, pair_row, local = pair_pass(
         early, paired, own_green, own_lesser, *common, tile_map, prev_potential, total_energies
     )
-    parcels = own_pass(late, mine, pair_green, pair_lesser, *common, parcels, total_energies)
+    parcels, own_row = own_pass(
+        late, mine, pair_green, pair_lesser, *common, parcels, pair_row, total_energies
+    )
     parcels = lax.all_to_all(parcels, DEVICES, 0, 0)
     parcels = parcels.reshape(energy_devices, slabs, *parcels.shape[1:])
-    return relax(parcels, orbitals, total_energies, *tile_map.shape[1:])
+    return relax(parcels, own_row, local, orbitals, total_energies, *tile_map.shape[1:])
 
 
 def solution(mesh):

time: 59.6 us -> 58.6 us (0.983)
  Pallas kernels: 19.2 us -> 18.1 us
  starting transfers between devices: 25.1 us -> 24.5 us
    pallas_call x9, Pallas kernels: 19.2 us -> 18.1 us  [call(): pl.pallas_call(kernel, out_shape=shapes, in_specs=specs, out_specs=[vmem(...]
    ppermute x2, starting transfers between devices: 8.36 us -> 7.59 us  [per_device(): late.append(lax.ppermute(paired[-1], 'energy', near))]
  transfers between devices with their start and end apart: 13 -> 13, of which waited for: 1 -> 1; matrix products, arithmetic and copies ran while one was open for 0% -> 0% of each run, Pallas kernels for 20% -> 19%
where the time goes in v3:
time: 58.6 us; the launch traced here: 58.2 us
  starting transfers between devices  24.5 us (42%)
  Pallas kernels  18.1 us (31%)
  blocking collectives  12.1 us (21%)
  waiting for transfers between devices  2.54 us (4%)
  between operations  0.87 us (1%)
    pallas_call x9, Pallas kernels, call(): pl.pallas_call(kernel, out_shape=shapes, in_specs=specs, out_specs=[vmem(...  18.1 us
    all_to_all x1, blocking collectives, per_device(): parcels = lax.all_to_all(parcels, DEVICES, 0, 0)  12.1 us
    ppermute x4, starting transfers between devices, per_device(): sides = [lax.ppermute(part, 'slab', way) for way in swaps]  7.61 us
    ppermute x2, starting transfers between devices, per_device(): late.append(lax.ppermute(paired[-1], 'energy', near))  7.59 us
    ppermute x4, starting transfers between devices, per_device(): lax.ppermute(part, 'slab', way)  4.78 us
    ppermute x2, starting transfers between devices, per_device(): crossed = [lax.ppermute(part, 'energy', pair) for part in blocks[:2]]  3.1 us
    ppermute x2, waiting for transfers between devices, per_device(): crossed = [lax.ppermute(part, 'energy', pair) for part in blocks[:2]]  2.52 us
    ppermute x1, starting transfers between devices, per_device(): early = lax.ppermute(mine, 'energy', far)  1.42 us
  transfers between devices with their start and end apart: 13, of which 1 were waited for; matrix products, arithmetic and copies ran while one was open for 0% of the time, Pallas kernels for 19%

profile of v3, /device:TPU:0, one launch (start us, length us, event | category | flops | bytes accessed | tf_op | source)
XLA Modules:
  0.0 58.2 jit_solution(9012489590671885213)
XLA Ops:
  0.6 1.4 %shard_map.95 = (f32[264,256]{1,0:T(8,128)S(1)}, f32[264,256]{1,0:T(8,128)S(1)}, f32[264,256]{1,0:T(8,128)S(1)}, f32[256,256]{1,0:T(8,128)S(1)}, f32[8,256]{1,0:T(8,128)S(1)}) custom-call(f32[2,1,2,256,256]{4,3,2,1,0:T(8,128)} %block_ref.1, f32[1,256]{1,0:T(1,128)} %coupling_ref.5, f32[1,2]{1,0:T(1,128)} %refs_0_.1, f32[1,2]{1,0:T(1,128)} %refs_1_.2), custom_call_target="tpu_custom_call" | custom-call | tf_op jit(solution)/shard_map/pallas_call | solution.py:163
  2.0 0.5 collective-permute-start.10
  2.5 2.6 %collective-permute-start = (f32[264,256]{1,0:T(8,128)S(1)}, f32[264,256]{1,0:T(8,128)S(1)}, u32[]{:S(2)}, u32[]{:S(2)}) collective-permute-start(f32[264,256]{1,0:T(8,128)S(1)} %get-tuple-element.18), channel_id=1, source_target_pairs={{0,4},{4,0},{8,12},{12,8},{16,20},{20,16},{24,28},{28,24},{1,5},{5... | collective-permute-start | bytes 811016 | tf_op jit(solution)/shard_map/ppermute | solution.py:497
  5.1 0.7 %collective-permute-start.3 = (f32[264,256]{1,0:T(8,128)S(1)}, f32[264,256]{1,0:T(8,128)S(1)}, u32[]{:S(2)}, u32[]{:S(2)}) collective-permute-start(f32[264,256]{1,0:T(8,128)S(1)} %get-tuple-element.19), channel_id=1, source_target_pairs={{1,2},{2,1},{5,6},{6,5},{9,10},{10,9},{13,14},{14,13},{17,18},{18,... | collective-permute-start | bytes 811016 | tf_op jit(solution)/shard_map/ppermute | solution.py:498
  5.8 2.9 %collective-permute-start.4 = (f32[264,256]{1,0:T(8,128)S(1)}, f32[264,256]{1,0:T(8,128)S(1)}, u32[]{:S(2)}, u32[]{:S(2)}) collective-permute-start(f32[264,256]{1,0:T(8,128)S(1)} %get-tuple-element.19), channel_id=1, source_target_pairs={{0,1},{1,0},{2,3},{3,2},{4,5},{5,4},{6,7},{7,6},{8,9},{9,8},{10,11... | collective-permute-start | bytes 811016 | tf_op jit(solution)/shard_map/ppermute | solution.py:498
  8.7 0.0 copy-start.4
  8.7 0.5 collective-permute-start.6
  9.2 0.0 collective-permute-done.10.refs_3_
  9.2 0.7 %collective-permute-start.9 = (f32[256,256]{1,0:T(8,128)S(1)}, f32[256,256]{1,0:T(8,128)S(1)}, u32[]{:S(2)}, u32[]{:S(2)}) collective-permute-start(f32[256,256]{1,0:T(8,128)S(1)} %get-tuple-element.21), channel_id=1, source_target_pairs={{1,2},{2,1},{5,6},{6,5},{9,10},{10,9},{13,14},{14,13},{17,18},{18,... | collective-permute-start | bytes 786440 | tf_op jit(solution)/shard_map/ppermute | solution.py:498
  9.9 2.5 %collective-permute-done.crossed_ref = f32[264,256]{1,0:T(8,128)S(1)} collective-permute-done((f32[264,256]{1,0:T(8,128)S(1)}, f32[264,256]{1,0:T(8,128)S(1)}, u32[]{:S(2)}, u32[]{:S(2)}) %collective-permute-start) | collective-permute-done | bytes 270368 | tf_op jit(solution)/shard_map/ppermute | solution.py:497
  12.4 0.7 %collective-permute-start.1 = (f32[264,256]{1,0:T(8,128)S(1)}, f32[264,256]{1,0:T(8,128)S(1)}, u32[]{:S(2)}, u32[]{:S(2)}) collective-permute-start(f32[264,256]{1,0:T(8,128)S(1)} %collective-permute-done.crossed_ref), channel_id=1, source_target_pairs={{1,2},{2,1},{5,6},{6,5},{9,10},{10,9},{13,14},{14,13},{17,18},{18,... | collective-permute-start | bytes 811016 | tf_op jit(solution)/shard_map/ppermute | solution.py:504
  13.1 0.0 collective-permute-done.9.refs_2_
  13.1 3.9 %collective-permute-start.2 = (f32[264,256]{1,0:T(8,128)S(1)}, f32[264,256]{1,0:T(8,128)S(1)}, u32[]{:S(2)}, u32[]{:S(2)}) collective-permute-start(f32[264,256]{1,0:T(8,128)S(1)} %collective-permute-done.crossed_ref), channel_id=1, source_target_pairs={{0,1},{1,0},{2,3},{3,2},{4,5},{5,4},{6,7},{7,6},{8,9},{9,8},{10,11... | collective-permute-start | bytes 811016 | tf_op jit(solution)/shard_map/ppermute | solution.py:504
  17.0 0.0 collective-permute-done.3.own_outer_ref.refs_0_
  17.0 0.0 collective-permute-done.4.own_inner_ref.refs_1_
  17.0 0.0 copy-done.4
  17.0 0.3 shard_map.97.refs_0_.refs_2_
  17.3 0.0 copy-start
  17.3 0.0 copy-start.3
  17.4 1.4 %collective-permute-start.12 = (f32[520,256]{1,0:T(8,128)S(1)}, f32[520,256]{1,0:T(8,128)S(1)}, u32[]{:S(2)}, u32[]{:S(2)}) collective-permute-start(f32[520,256]{1,0:T(8,128)S(1)} %shard_map.97.refs_0_.refs_2_), channel_id=1, source_target_pairs={{4,12},{12,20},{20,28},{8,0},{16,8},{24,16},{5,13},{13,21},{21,29}... | collective-permute-start | bytes 1597448 | tf_op jit(solution)/shard_map/ppermute | solution.py:500
  18.8 0.0 collective-permute-done.6.crossed_ref
  18.8 0.7 %collective-permute-start.7 = (f32[264,256]{1,0:T(8,128)S(1)}, f32[264,256]{1,0:T(8,128)S(1)}, u32[]{:S(2)}, u32[]{:S(2)}) collective-permute-start(f32[264,256]{1,0:T(8,128)S(1)} %collective-permute-done.6.crossed_ref), channel_id=1, source_target_pairs={{1,2},{2,1},{5,6},{6,5},{9,10},{10,9},{13,14},{14,13},{17,18},{18,... | collective-permute-start | bytes 811016 | tf_op jit(solution)/shard_map/ppermute | solution.py:504
  19.5 2.4 %collective-permute-start.8 = (f32[264,256]{1,0:T(8,128)S(1)}, f32[264,256]{1,0:T(8,128)S(1)}, u32[]{:S(2)}, u32[]{:S(2)}) collective-permute-start(f32[264,256]{1,0:T(8,128)S(1)} %collective-permute-done.6.crossed_ref), channel_id=1, source_target_pairs={{0,1},{1,0},{2,3},{3,2},{4,5},{5,4},{6,7},{7,6},{8,9},{9,8},{10,11... | collective-permute-start | bytes 811016 | tf_op jit(solution)/shard_map/ppermute | solution.py:504
  21.8 0.0 collective-permute-done.1.outer_ref
  21.8 0.0 collective-permute-done.2.inner_ref
  21.8 0.3 shard_map.96.refs_0_.refs_1_
  22.1 3.8 %collective-permute-start.5 = (f32[264,256]{1,0:T(8,128)S(1)}, f32[264,256]{1,0:T(8,128)S(1)}, u32[]{:S(2)}, u32[]{:S(2)}) collective-permute-start(f32[264,256]{1,0:T(8,128)S(1)} %shard_map.96.refs_0_.refs_1_), channel_id=1, source_target_pairs={{12,4},{20,12},{28,20},{0,8},{8,16},{16,24},{13,5},{21,13},{29,21}... | collective-permute-start | bytes 811016 | tf_op jit(solution)/shard_map/ppermute | solution.py:509
  25.9 0.0 copy-done
  25.9 0.0 copy-done.3
  25.9 2.6 %shard_map.98 = (f32[2,256,256]{2,1,0:T(8,128)S(1)}, f32[2,256,256]{2,1,0:T(8,128)S(1)}) custom-call(f32[520,256]{1,0:T(8,128)S(1)} %shard_map.97.refs_0_.refs_2_, f32[1,256,256]{2,1,0:T(8,128)S(1)} %copy-done, f32[1,256]{1,0:T(1,128)S(1)} %copy-done.3), custom_call_target="tpu_custom_call" | custom-call | tf_op jit(solution)/shard_map/pallas_call | solution.py:163
  28.5 0.0 collective-permute-done.7.outer_ref
  28.5 0.0 collective-permute-done.8.inner_ref
  28.5 0.3 shard_map.99.refs_1_.refs_2_
  28.8 0.0 copy-start.1
  28.8 0.0 copy-start.2
  28.8 3.8 %collective-permute-start.11 = (f32[256,256]{1,0:T(8,128)S(1)}, f32[256,256]{1,0:T(8,128)S(1)}, u32[]{:S(2)}, u32[]{:S(2)}) collective-permute-start(f32[256,256]{1,0:T(8,128)S(1)} %shard_map.99.refs_1_.refs_2_), channel_id=1, source_target_pairs={{12,4},{20,12},{28,20},{0,8},{8,16},{16,24},{13,5},{21,13},{29,21}... | collective-permute-start | bytes 786440 | tf_op jit(solution)/shard_map/ppermute | solution.py:509
  32.6 2.6 %shard_map.100 = (f32[2,256,256]{2,1,0:T(8,128)S(1)}, f32[2,256,256]{2,1,0:T(8,128)S(1)}) custom-call(f32[264,256]{1,0:T(8,128)S(1)} %shard_map.96.refs_0_.refs_1_, f32[256,256]{1,0:T(8,128)S(1)} %shard_map.99.refs_1_.refs_2_, f32[1,256,256]{2,1,0:T(8,128)S(1)} %copy-done, f32[1,256]{1,0:T(1,128)S(1)} %copy-done.3), custom_call_target="tpu_custom_call" | custom-call | tf_op jit(solution)/shard_map/pallas_call | solution.py:163
  35.2 0.0 collective-permute-done.12.refs_0_
  35.2 0.0 copy-done.1
  35.2 0.0 copy-done.2
  35.3 5.0 %shard_map.101 = (f32[32,1,896]{2,1,0:T(1,128)S(1)}, f32[1,256]{1,0:T(1,128)S(1)}, f32[2,24,128]{2,1,0:T(8,128)S(1)}) custom-call(f32[520,256]{1,0:T(8,128)S(1)} %collective-permute-done.12.refs_0_, f32[264,256]{1,0:T(8,128)S(1)} %shard_map.96.refs_0_.refs_1_, f32[256,256]{1,0:T(8,128)S(1)} %shard_map.99.refs_1_.refs_2_, ...), custom_call_target="tpu_custom_call" | custom-call | tf_op jit(solution)/shard_map/pallas_call | solution.py:163
  40.2 0.0 collective-permute-done.11.refs_1_
  40.2 0.0 collective-permute-done.5.refs_0_
  40.3 4.9 %shard_map.102 = (f32[32,1,896]{2,1,0:T(1,128)S(1)}, f32[1,256]{1,0:T(1,128)S(1)}) custom-call(f32[264,256]{1,0:T(8,128)S(1)} %collective-permute-done.5.refs_0_, f32[256,256]{1,0:T(8,128)S(1)} %collective-permute-done.11.refs_1_, f32[520,256]{1,0:T(8,128)S(1)} %shard_map.97.refs_0_.refs_2_, ...), custom_call_target="tpu_custom_call", output_to_operand_aliasing={{0}: (8, {})} | custom-call | tf_op jit(solution)/shard_map/pallas_call | solution.py:163
  45.2 12.1 %all_to_all.5 = f32[32,1,896]{2,1,0:T(1,128)S(1)} all-to-all(f32[32,1,896]{2,1,0:T(1,128)S(1)} %get-tuple-element.31), channel_id=1, replica_groups=mesh['energy'=8,'slab'=4] {'energy','slab'}, dimensions={0} | all-to-all | bytes 229376 | tf_op jit(solution)/shard_map/all_to_all | solution.py:517
  57.3 0.9 %shard_map.103 = (f32[1,2,256]{2,1,0:T(2,128)}, f32[1,16,128]{2,1,0:T(8,128)}) custom-call(f32[8,4,1,896]{3,2,1,0:T(1,128)S(1)} %bitcast.1, f32[1,256]{1,0:T(1,128)S(1)} %get-tuple-element.32.own_ref, f32[2,24,128]{2,1,0:T(8,128)S(1)} %get-tuple-element.33.local_ref), custom_call_target="tpu_custom_call" | custom-call | tf_op jit(solution)/shard_map/pallas_call | solution.py:163
Async XLA Ops:
  2.0 7.2 %collective-permute-start.10 = (f32[256,256]{1,0:T(8,128)S(1)}, f32[256,256]{1,0:T(8,128)S(1)}, u32[]{:S(2)}, u32[]{:S(2)}) collective-permute-start(f32[256,256]{1,0:T(8,128)S(1)} %get-tuple-element.21), channel_id=1, source_target_pairs={{0,1},{1,0},{2,3},{3,2},{4,5},{5,4},{6,7},{7,6},{8,9},{9,8},{10,11... | collective-permute-start | bytes 786440 | tf_op jit(solution)/shard_map/ppermute | solution.py:498
  2.5 9.9 %collective-permute-start = (f32[264,256]{1,0:T(8,128)S(1)}, f32[264,256]{1,0:T(8,128)S(1)}, u32[]{:S(2)}, u32[]{:S(2)}) collective-permute-start(f32[264,256]{1,0:T(8,128)S(1)} %get-tuple-element.18), channel_id=1, source_target_pairs={{0,4},{4,0},{8,12},{12,8},{16,20},{20,16},{24,28},{28,24},{1,5},{5... | collective-permute-start | bytes 811016 | tf_op jit(solution)/shard_map/ppermute | solution.py:497
  5.1 11.9 %collective-permute-start.3 = (f32[264,256]{1,0:T(8,128)S(1)}, f32[264,256]{1,0:T(8,128)S(1)}, u32[]{:S(2)}, u32[]{:S(2)}) collective-permute-start(f32[264,256]{1,0:T(8,128)S(1)} %get-tuple-element.19), channel_id=1, source_target_pairs={{1,2},{2,1},{5,6},{6,5},{9,10},{10,9},{13,14},{14,13},{17,18},{18,... | collective-permute-start | bytes 811016 | tf_op jit(solution)/shard_map/ppermute | solution.py:498
  5.8 11.3 %collective-permute-start.4 = (f32[264,256]{1,0:T(8,128)S(1)}, f32[264,256]{1,0:T(8,128)S(1)}, u32[]{:S(2)}, u32[]{:S(2)}) collective-permute-start(f32[264,256]{1,0:T(8,128)S(1)} %get-tuple-element.19), channel_id=1, source_target_pairs={{0,1},{1,0},{2,3},{3,2},{4,5},{5,4},{6,7},{7,6},{8,9},{9,8},{10,11... | collective-permute-start | bytes 811016 | tf_op jit(solution)/shard_map/ppermute | solution.py:498
  8.7 8.3 %copy-start.4 = (f32[1,256]{1,0:T(1,128)S(1)}, f32[1,256]{1,0:T(1,128)}, u32[]{:S(2)}) copy-start(f32[1,256]{1,0:T(1,128)} %coupling_ref.5) | copy-start | bytes 3076
  8.7 10.1 %collective-permute-start.6 = (f32[264,256]{1,0:T(8,128)S(1)}, f32[264,256]{1,0:T(8,128)S(1)}, u32[]{:S(2)}, u32[]{:S(2)}) collective-permute-start(f32[264,256]{1,0:T(8,128)S(1)} %get-tuple-element.20), channel_id=1, source_target_pairs={{0,4},{4,0},{8,12},{12,8},{16,20},{20,16},{24,28},{28,24},{1,5},{5... | collective-permute-start | bytes 811016 | tf_op jit(solution)/shard_map/ppermute | solution.py:497
  9.2 3.9 %collective-permute-start.9 = (f32[256,256]{1,0:T(8,128)S(1)}, f32[256,256]{1,0:T(8,128)S(1)}, u32[]{:S(2)}, u32[]{:S(2)}) collective-permute-start(f32[256,256]{1,0:T(8,128)S(1)} %get-tuple-element.21), channel_id=1, source_target_pairs={{1,2},{2,1},{5,6},{6,5},{9,10},{10,9},{13,14},{14,13},{17,18},{18,... | collective-permute-start | bytes 786440 | tf_op jit(solution)/shard_map/ppermute | solution.py:498
  12.4 9.4 %collective-permute-start.1 = (f32[264,256]{1,0:T(8,128)S(1)}, f32[264,256]{1,0:T(8,128)S(1)}, u32[]{:S(2)}, u32[]{:S(2)}) collective-permute-start(f32[264,256]{1,0:T(8,128)S(1)} %collective-permute-done.crossed_ref), channel_id=1, source_target_pairs={{1,2},{2,1},{5,6},{6,5},{9,10},{10,9},{13,14},{14,13},{17,18},{18,... | collective-permute-start | bytes 811016 | tf_op jit(solution)/shard_map/ppermute | solution.py:504
  13.1 8.7 %collective-permute-start.2 = (f32[264,256]{1,0:T(8,128)S(1)}, f32[264,256]{1,0:T(8,128)S(1)}, u32[]{:S(2)}, u32[]{:S(2)}) collective-permute-start(f32[264,256]{1,0:T(8,128)S(1)} %collective-permute-done.crossed_ref), channel_id=1, source_target_pairs={{0,1},{1,0},{2,3},{3,2},{4,5},{5,4},{6,7},{7,6},{8,9},{9,8},{10,11... | collective-permute-start | bytes 811016 | tf_op jit(solution)/shard_map/ppermute | solution.py:504
  17.3 8.6 %copy-start = (f32[1,256,256]{2,1,0:T(8,128)S(1)}, f32[1,256,256]{2,1,0:T(8,128)}, u32[]{:S(2)}) copy-start(f32[1,256,256]{2,1,0:T(8,128)} %refs_5_.3) | copy-start | bytes 786436
  17.3 8.6 %copy-start.3 = (f32[1,256]{1,0:T(1,128)S(1)}, f32[1,256]{1,0:T(1,128)}, u32[]{:S(2)}) copy-start(f32[1,256]{1,0:T(1,128)} %refs_6_.3) | copy-start | bytes 3076
  17.4 17.9 %collective-permute-start.12 = (f32[520,256]{1,0:T(8,128)S(1)}, f32[520,256]{1,0:T(8,128)S(1)}, u32[]{:S(2)}, u32[]{:S(2)}) collective-permute-start(f32[520,256]{1,0:T(8,128)S(1)} %shard_map.97.refs_0_.refs_2_), channel_id=1, source_target_pairs={{4,12},{12,20},{20,28},{8,0},{16,8},{24,16},{5,13},{13,21},{21,29}... | collective-permute-start | bytes 1597448 | tf_op jit(solution)/shard_map/ppermute | solution.py:500
  18.8 9.7 %collective-permute-start.7 = (f32[264,256]{1,0:T(8,128)S(1)}, f32[264,256]{1,0:T(8,128)S(1)}, u32[]{:S(2)}, u32[]{:S(2)}) collective-permute-start(f32[264,256]{1,0:T(8,128)S(1)} %collective-permute-done.6.crossed_ref), channel_id=1, source_target_pairs={{1,2},{2,1},{5,6},{6,5},{9,10},{10,9},{13,14},{14,13},{17,18},{18,... | collective-permute-start | bytes 811016 | tf_op jit(solution)/shard_map/ppermute | solution.py:504
  19.5 9.0 %collective-permute-start.8 = (f32[264,256]{1,0:T(8,128)S(1)}, f32[264,256]{1,0:T(8,128)S(1)}, u32[]{:S(2)}, u32[]{:S(2)}) collective-permute-start(f32[264,256]{1,0:T(8,128)S(1)} %collective-permute-done.6.crossed_ref), channel_id=1, source_target_pairs={{0,1},{1,0},{2,3},{3,2},{4,5},{5,4},{6,7},{7,6},{8,9},{9,8},{10,11... | collective-permute-start | bytes 811016 | tf_op jit(solution)/shard_map/ppermute | solution.py:504
  22.1 18.1 %collective-permute-start.5 = (f32[264,256]{1,0:T(8,128)S(1)}, f32[264,256]{1,0:T(8,128)S(1)}, u32[]{:S(2)}, u32[]{:S(2)}) collective-permute-start(f32[264,256]{1,0:T(8,128)S(1)} %shard_map.96.refs_0_.refs_1_), channel_id=1, source_target_pairs={{12,4},{20,12},{28,20},{0,8},{8,16},{16,24},{13,5},{21,13},{29,21}... | collective-permute-start | bytes 811016 | tf_op jit(solution)/shard_map/ppermute | solution.py:509
  28.8 6.4 %copy-start.1 = (s32[1,128,128]{2,1,0:T(8,128)S(1)}, s32[1,128,128]{2,1,0:T(8,128)}, u32[]{:S(2)}) copy-start(s32[1,128,128]{2,1,0:T(8,128)} %refs_7_.1) | copy-start | bytes 196612
  28.8 6.4 %copy-start.2 = (f32[1,128,128]{2,1,0:T(8,128)S(1)}, f32[1,128,128]{2,1,0:T(8,128)}, u32[]{:S(2)}) copy-start(f32[1,128,128]{2,1,0:T(8,128)} %refs_8_.1) | copy-start | bytes 196612
  28.8 11.4 %collective-permute-start.11 = (f32[256,256]{1,0:T(8,128)S(1)}, f32[256,256]{1,0:T(8,128)S(1)}, u32[]{:S(2)}, u32[]{:S(2)}) collective-permute-start(f32[256,256]{1,0:T(8,128)S(1)} %shard_map.99.refs_1_.refs_2_), channel_id=1, source_target_pairs={{12,4},{20,12},{28,20},{0,8},{8,16},{16,24},{13,5},{21,13},{29,21}... | collective-permute-start | bytes 786440 | tf_op jit(solution)/shard_map/ppermute | solution.py:509

commit v4 on v3

--- a/solution.py
+++ b/solution.py
@@ -16,7 +16,7 @@
 MAIN_DIAGONAL = 2.0 + 4.0 * ANISO + SCREEN
 LANES = 128
 SUBLANES = 8
-CROSS_ROWS = 8
+BELOW = (8, 0, 16, 16)
 VMEM_BYTES = 48 * 1024 * 1024
 
 f32 = jnp.float32
@@ -82,13 +82,24 @@
     )
 
 
-def invert(coupled, row, column):
+def invert(coupled, row, column, between=()):
+    given = None
+    steps = iter(between)
+
+    def beside():
+        nonlocal given
+        step = next(steps, None)
+        if step is not None:
+            given = step(given)
+
     b1 = scale(coupled, row)
     b1_factor = factor(b1)
     b2 = product(b1_factor, b1_factor)
+    beside()
     b2_factor = factor(b2)
     b4 = product(b2_factor, b2_factor)
     b3 = product(b1_factor, b2_factor)
+    beside()
     t = add(b1, b2, b3)
     rest = product(factor(t), factor(b4))
     size = b1[0].shape[0]
@@ -97,7 +108,7 @@
         == lax.broadcasted_iota(jnp.int32, (size, size), 1)
     ).astype(f32)
     total = add(t, b4, rest)
-    return scale((unit + total[0], total[1]), column)
+    return scale((unit + total[0], total[1]), column), given
 
 
 def halves(message_ref):
@@ -111,40 +122,64 @@
         parity = lax.rem(lax.axis_index("energy"), SHIFT)
         index = (SHIFT * chain + parity).astype(f32)
         energy = -2.0 + (4.0 / total_energies) * (index + 0.5)
-        real_ref, imag_ref = message_refs if len(message_refs) == 2 else halves(message_refs[0])
-        self.sigma = (real_ref[0:size, :], imag_ref[...])
-        damping = real_ref[size : size + 1, :]
-        self.occupation = real_ref[size + 1 : size + 2, :]
+        self.real_ref, self.imag_ref = (
+            message_refs if len(message_refs) == 2 else halves(message_refs[0])
+        )
+        damping = self.real_ref[size : size + 1, :]
+        self.occupation = self.real_ref[size + 1 : size + 2, :]
         onsite = onsite_ref[...]
         self.row = start_of(energy, onsite, damping)
         self.column = tuple(as_column(part) for part in self.row)
-        self.hopping = hopping_ref[0]
-
-    def lesser_source(self):
-        real, imag = self.sigma
+        self.hopping_ref = hopping_ref
+
+    def sigma(self):
+        size = self.hopping_ref.shape[-1]
+        return self.real_ref[0:size, :], self.imag_ref[0:size, :]
+
+    def coupled(self):
+        real, imag = self.sigma()
+        return self.hopping_ref[0] + real, imag
+
+    def source(self):
+        real, imag = self.sigma()
         return -self.occupation * (real - real.T), -self.occupation * (imag + imag.T)
 
-    def green(self, phonon=None):
-        coupled = (self.hopping + self.sigma[0], self.sigma[1])
-        if phonon is not None:
-            coupled = add(coupled, phonon)
-        return invert(coupled, self.row, self.column)
-
-    def green_and_lesser(self):
+    def green(self):
+        return invert(self.coupled(), self.row, self.column)[0]
+
+    def green_and_lesser(self, source):
         green = self.green()
-        mixed = product(factor(green), factor(self.lesser_source()))
+        mixed = product(factor(green), factor(source))
         return green, adjoint_product(factor(mixed), adjoint_factor(green))
 
-    def lesser_row(self, greens, lessers):
-        half = tuple(PHONON * part for part in add(*greens))
-        green = self.green(half)
-        source = add(self.lesser_source(), tuple(PHONON * part for part in add(*lessers)))
+    def lesser_row(self, coupled, source, beyond):
+        beyond_source = factor(beyond.source())
+        beyond_green = beyond.green()
+        steps = (
+            lambda _: product(factor(beyond_green), beyond_source),
+            lambda mixed: adjoint_product(factor(mixed), adjoint_factor(beyond_green)),
+        )
+        coupled = with_half(coupled, beyond_green)
+        green, lesser = invert(coupled, self.row, self.column, steps)
+        source = with_half(source, lesser)
         real, imag = parts(green[0]), parts(green[1])
         source_real, source_imag = parts(source[0]), parts(source[1])
         terms = green[0] * dot(real, source_imag) + green[1] * dot(imag, source_imag)
         terms = terms - 2.0 * green[1] * dot(real, source_real)
         column = jnp.sum(terms, axis=1, keepdims=True)
         return jnp.broadcast_to(column, (column.shape[0], LANES)).T[0:1, :]
+
+
+def with_half(matrix, phonon):
+    return tuple(a + PHONON * b for a, b in zip(matrix, phonon))
+
+
+def load(ref):
+    return ref[0], ref[1]
+
+
+def store(ref, matrix):
+    ref[0], ref[1] = matrix
 
 
 def chain_places():
@@ -184,7 +219,7 @@
             (block_ref.at[1, 0, 1 - parity], imag_ref.at[pl.ds(0, rows)]),
             (block_ref.at[0, 0, parity], own_refs[0].at[pl.ds(0, rows)]),
             (coupling_ref, own_refs[0].at[pl.ds(rows, 1)]),
-            (block_ref.at[1, 0, parity], own_refs[1]),
+            (block_ref.at[1, 0, parity], own_refs[1].at[pl.ds(0, rows)]),
         ]
         copies = [
             pltpu.make_async_copy(source, target, sems.at[at])
@@ -210,7 +245,7 @@
         [pl.BlockSpec(memory_space=pltpu.HBM)] * 4,
         [
             jax.ShapeDtypeStruct((height, columns), f32)
-            for height in (rows + CROSS_ROWS, rows + CROSS_ROWS, rows + SUBLANES, rows, SUBLANES)
+            for height in (*(rows + extra for extra in BELOW), SUBLANES)
         ],
         scratch_shapes=[
             pltpu.VMEM(damping.shape, f32),
@@ -266,23 +301,38 @@
     return call(kernel, operands, [vmem()] * 6, jax.ShapeDtypeStruct((height, columns), f32))
 
 
-def green_and_lesser(message, hopping, onsite, place, total_energies):
-    count = len(message)
-
-    def kernel(*refs):
-        hopping_ref, onsite_ref, green_ref, lesser_ref = refs[count:]
-        element = Element(
-            refs[:count], hopping_ref, onsite_ref, chain_places()[place], total_energies
-        )
-        green, lesser = element.green_and_lesser()
-        for plane in range(2):
-            green_ref[plane] = green[plane]
-            lesser_ref[plane] = lesser[plane]
+def own_first(message, hopping, onsite, total_energies):
+    def kernel(message_ref, hopping_ref, onsite_ref, green_ref, lesser_ref, source_ref):
+        place = chain_places()["own"]
+        element = Element([message_ref], hopping_ref, onsite_ref, place, total_energies)
+        source = element.source()
+        green, lesser = element.green_and_lesser(source)
+        for ref, matrix in ((green_ref, green), (lesser_ref, lesser), (source_ref, source)):
+            store(ref, matrix)
 
     size = hopping.shape[-1]
     shape = jax.ShapeDtypeStruct((2, size, size), f32)
-    operands = (*message, hopping, onsite)
-    return call(kernel, operands, [vmem()] * len(operands), [shape, shape])
+    return call(kernel, (message, hopping, onsite), [vmem()] * 3, [shape] * 3)
+
+
+def pair_first(paired, mine, green, lesser, source, hopping, onsite, total_energies):
+    def kernel(*refs):
+        paired_refs, mine_refs, (green_ref, lesser_ref, source_ref) = refs[:2], refs[2:3], refs[3:6]
+        hopping_ref, onsite_ref, *out_refs = refs[6:]
+        chains = chain_places()
+        pair = Element(paired_refs, hopping_ref, onsite_ref, chains["pair"], total_energies)
+        own = Element(mine_refs, hopping_ref, onsite_ref, chains["own"], total_energies)
+        pair_source = pair.source()
+        store(out_refs[0], with_half(pair.coupled(), load(green_ref)))
+        store(out_refs[1], with_half(pair_source, load(lesser_ref)))
+        pair_green, pair_lesser = pair.green_and_lesser(pair_source)
+        store(out_refs[2], with_half(own.coupled(), pair_green))
+        store(out_refs[3], with_half(load(source_ref), pair_lesser))
+
+    operands = (*paired, mine, green, lesser, source, hopping, onsite)
+    size = hopping.shape[-1]
+    shape = jax.ShapeDtypeStruct((2, size, size), f32)
+    return call(kernel, operands, [vmem()] * len(operands), [shape] * 4)
 
 
 def grid_share(rows_here, energy_devices):
@@ -290,7 +340,7 @@
     return needed, -(-2 * needed // energy_devices)
 
 
-def pair_pass(early, paired, green, lesser, hopping, onsite, tile_map, potential, total_energies):
+def pair_pass(early, paired, coupled, source, hopping, onsite, tile_map, potential, total_energies):
     size = hopping.shape[-1]
     energy_devices, slabs = lax.axis_size("energy"), lax.axis_size("slab")
     grid_total, columns = tile_map.shape[1:]
@@ -302,16 +352,12 @@
 
     def kernel(*refs):
         early_refs, paired_refs, refs = refs[:1], refs[1:3], refs[3:]
-        green_ref, lesser_ref, hopping_ref, onsite_ref, tile_ref, potential_ref = refs[:6]
+        coupled_ref, source_ref, hopping_ref, onsite_ref, tile_ref, potential_ref = refs[:6]
         parcel_ref, row_ref, local_ref, grid_ref = refs[6:]
         chains = chain_places()
         here = Element(paired_refs, hopping_ref, onsite_ref, chains["pair"], total_energies)
         beyond = Element(early_refs, hopping_ref, onsite_ref, chains["early"], total_energies)
-        beyond_green, beyond_lesser = beyond.green_and_lesser()
-        row = here.lesser_row(
-            [beyond_green, (green_ref[0], green_ref[1])],
-            [beyond_lesser, (lesser_ref[0], lesser_ref[1])],
-        )
+        row = here.lesser_row(load(coupled_ref), load(source_ref), beyond)
         row_ref[...] = row
         at_energy, at_slab = lax.axis_index("energy"), lax.axis_index("slab")
         border = jnp.zeros((SUBLANES, columns), f32)
@@ -344,7 +390,7 @@
             for slab in range(slabs):
                 parcel_ref[to * slabs + slab, :, size:] = jnp.where(at_slab == slab, same, other)
 
-    operands = [early, *paired, green, lesser, hopping, onsite, tile_map, potential]
+    operands = [early, *paired, coupled, source, hopping, onsite, tile_map, potential]
     return call(
         kernel,
         operands,
@@ -358,26 +404,22 @@
     )
 
 
-def own_pass(late, mine, green, lesser, hopping, onsite, parcels, other_row, total_energies):
+def own_pass(late, mine, coupled, source, hopping, onsite, parcels, other_row, total_energies):
     size = hopping.shape[-1]
 
     def kernel(*refs):
         late_refs, mine_refs, refs = refs[:2], refs[2:3], refs[3:]
-        green_ref, lesser_ref, hopping_ref, onsite_ref, other_ref, _, parcel_ref, row_ref = refs
+        coupled_ref, source_ref, hopping_ref, onsite_ref, other_ref, _, parcel_ref, row_ref = refs
         chains = chain_places()
         here = Element(mine_refs, hopping_ref, onsite_ref, chains["own"], total_energies)
         beyond = Element(late_refs, hopping_ref, onsite_ref, chains["late"], total_energies)
-        beyond_green, beyond_lesser = beyond.green_and_lesser()
-        row = here.lesser_row(
-            [beyond_green, (green_ref[0], green_ref[1])],
-            [beyond_lesser, (lesser_ref[0], lesser_ref[1])],
-        )
+        row = here.lesser_row(load(coupled_ref), load(source_ref), beyond)
         row_ref[...] = row
         both = row + other_ref[...]
         for to in range(parcel_ref.shape[0]):
             parcel_ref[to, :, 0:size] = both
 
-    operands = [*late, mine, green, lesser, hopping, onsite, other_row, parcels]
+    operands = [*late, mine, coupled, source, hopping, onsite, other_row, parcels]
     return call(
         kernel,
         operands,
@@ -498,7 +540,7 @@
     own_sides = [[lax.ppermute(part, "slab", way) for way in swaps] for part in blocks[2:4]]
     mine = own_self_energy(*own_sides, coupling, blocks[4])
     early = lax.ppermute(mine, "energy", far)
-    own_green, own_lesser = green_and_lesser([mine], *common, "own", total_energies)
+    own_green, own_lesser, own_source = own_first(mine, *common, total_energies)
     paired, late = [], []
     for plane, part in enumerate(crossed):
         sides = [lax.ppermute(part, "slab", way) for way in swaps]
@@ -507,12 +549,14 @@
         extra = 0 if plane else SUBLANES
         paired.append(pair_self_energy(sides, coupling, own_sides[0], part, extra))
         late.append(lax.ppermute(paired[-1], "energy", near))
-    pair_green, pair_lesser = green_and_lesser(paired, *common, "pair", total_energies)
+    *pair_parts, own_coupled, own_total = pair_first(
+        paired, mine, own_green, own_lesser, own_source, *common, total_energies
+    )
     parcels, pair_row, local = pair_pass(
-        early, paired, own_green, own_lesser, *common, tile_map, prev_potential, total_energies
+        early, paired, *pair_parts, *common, tile_map, prev_potential, total_energies
     )
     parcels, own_row = own_pass(
-        late, mine, pair_green, pair_lesser, *common, parcels, pair_row, total_energies
+        late, mine, own_coupled, own_total, *common, parcels, pair_row, total_energies
     )
     parcels = lax.all_to_all(parcels, DEVICES, 0, 0)
     parcels = parcels.reshape(energy_devices, slabs, *parcels.shape[1:])

time: 58.6 us -> 57.5 us (0.981)
  blocking collectives: 12.1 us -> 11 us
    ppermute x2, starting transfers between devices: 3.1 us -> 4.74 us  [per_device(): crossed = [lax.ppermute(part, 'energy', pair) for part in blocks[:2]]]
    all_to_all x1, blocking collectives: 12.1 us -> 11 us  [per_device(): parcels = lax.all_to_all(parcels, DEVICES, 0, 0)]
    ppermute x4, starting transfers between devices: 7.61 us -> 6.77 us  [per_device(): sides = [lax.ppermute(part, 'slab', way) for way in swaps]]
  transfers between devices with their start and end apart: 13 -> 13, of which waited for: 1 -> 2; matrix products, arithmetic and copies ran while one was open for 0% -> 0% of each run, Pallas kernels for 19% -> 19%
where the time goes in v4:
time: 57.5 us; the launch traced here: 57.2 us
  starting transfers between devices  24.4 us (42%)
  Pallas kernels  18 us (31%)
  blocking collectives  11 us (19%)
  waiting for transfers between devices  2.89 us (5%)
  between operations  0.86 us (1%)
    pallas_call x9, Pallas kernels, call(): pl.pallas_call(kernel, out_shape=shapes, in_specs=specs, out_specs=[vmem(...  18 us
    all_to_all x1, blocking collectives, per_device(): parcels = lax.all_to_all(parcels, DEVICES, 0, 0)  11 us
    ppermute x2, starting transfers between devices, per_device(): late.append(lax.ppermute(paired[-1], 'energy', near))  7.16 us
    ppermute x4, starting transfers between devices, per_device(): sides = [lax.ppermute(part, 'slab', way) for way in swaps]  6.77 us
    ppermute x2, starting transfers between devices, per_device(): crossed = [lax.ppermute(part, 'energy', pair) for part in blocks[:2]]  4.74 us
    ppermute x4, starting transfers between devices, per_device(): lax.ppermute(part, 'slab', way)  4.34 us
    ppermute x2, waiting for transfers between devices, per_device(): crossed = [lax.ppermute(part, 'energy', pair) for part in blocks[:2]]  2.86 us
    ppermute x1, starting transfers between devices, per_device(): early = lax.ppermute(mine, 'energy', far)  1.42 us
  transfers between devices with their start and end apart: 13, of which 2 were waited for; matrix products, arithmetic and copies ran while one was open for 0% of the time, Pallas kernels for 19%

profile of v4, /device:TPU:0, one launch (start us, length us, event | category | flops | bytes accessed | tf_op | source)
XLA Modules:
  0.0 57.2 jit_solution(12439749044784109126)
XLA Ops:
  0.6 1.4 %shard_map.95 = (f32[264,256]{1,0:T(8,128)S(1)}, f32[256,256]{1,0:T(8,128)S(1)}, f32[272,256]{1,0:T(8,128)S(1)}, f32[272,256]{1,0:T(8,128)S(1)}, f32[8,256]{1,0:T(8,128)S(1)}) custom-call(f32[2,1,2,256,256]{4,3,2,1,0:T(8,128)} %block_ref.1, f32[1,256]{1,0:T(1,128)} %coupling_ref.5, f32[1,2]{1,0:T(1,128)} %refs_0_.1, f32[1,2]{1,0:T(1,128)} %refs_1_.1), custom_call_target="tpu_custom_call" | custom-call | tf_op jit(solution)/shard_map/pallas_call | solution.py:198
  2.0 3.0 %collective-permute-start = (f32[264,256]{1,0:T(8,128)S(1)}, f32[264,256]{1,0:T(8,128)S(1)}, u32[]{:S(2)}, u32[]{:S(2)}) collective-permute-start(f32[264,256]{1,0:T(8,128)S(1)} %get-tuple-element.21), channel_id=1, source_target_pairs={{0,4},{4,0},{8,12},{12,8},{16,20},{20,16},{24,28},{28,24},{1,5},{5... | collective-permute-start | bytes 811016 | tf_op jit(solution)/shard_map/ppermute | solution.py:539
  5.0 0.7 %collective-permute-start.3 = (f32[272,256]{1,0:T(8,128)S(1)}, f32[272,256]{1,0:T(8,128)S(1)}, u32[]{:S(2)}, u32[]{:S(2)}) collective-permute-start(f32[272,256]{1,0:T(8,128)S(1)} %get-tuple-element.22), channel_id=1, source_target_pairs={{1,2},{2,1},{5,6},{6,5},{9,10},{10,9},{13,14},{14,13},{17,18},{18,... | collective-permute-start | bytes 835592 | tf_op jit(solution)/shard_map/ppermute | solution.py:540
  5.7 2.9 %collective-permute-start.4 = (f32[272,256]{1,0:T(8,128)S(1)}, f32[272,256]{1,0:T(8,128)S(1)}, u32[]{:S(2)}, u32[]{:S(2)}) collective-permute-start(f32[272,256]{1,0:T(8,128)S(1)} %get-tuple-element.22), channel_id=1, source_target_pairs={{0,1},{1,0},{2,3},{3,2},{4,5},{5,4},{6,7},{7,6},{8,9},{9,8},{10,11... | collective-permute-start | bytes 835592 | tf_op jit(solution)/shard_map/ppermute | solution.py:540
  8.6 0.1 collective-permute-start.10
  8.7 0.7 %collective-permute-start.9 = (f32[272,256]{1,0:T(8,128)S(1)}, f32[272,256]{1,0:T(8,128)S(1)}, u32[]{:S(2)}, u32[]{:S(2)}) collective-permute-start(f32[272,256]{1,0:T(8,128)S(1)} %get-tuple-element.24), channel_id=1, source_target_pairs={{1,2},{2,1},{5,6},{6,5},{9,10},{10,9},{13,14},{14,13},{17,18},{18,... | collective-permute-start | bytes 835592 | tf_op jit(solution)/shard_map/ppermute | solution.py:540
  9.4 2.1 %collective-permute-done.crossed_ref = f32[264,256]{1,0:T(8,128)S(1)} collective-permute-done((f32[264,256]{1,0:T(8,128)S(1)}, f32[264,256]{1,0:T(8,128)S(1)}, u32[]{:S(2)}, u32[]{:S(2)}) %collective-permute-start) | collective-permute-done | bytes 270368 | tf_op jit(solution)/shard_map/ppermute | solution.py:539
  11.5 0.0 copy-start.4
  11.5 1.7 %collective-permute-start.6 = (f32[256,256]{1,0:T(8,128)S(1)}, f32[256,256]{1,0:T(8,128)S(1)}, u32[]{:S(2)}, u32[]{:S(2)}) collective-permute-start(f32[256,256]{1,0:T(8,128)S(1)} %get-tuple-element.23), channel_id=1, source_target_pairs={{0,4},{4,0},{8,12},{12,8},{16,20},{20,16},{24,28},{28,24},{1,5},{5... | collective-permute-start | bytes 786440 | tf_op jit(solution)/shard_map/ppermute | solution.py:539
  13.2 0.0 collective-permute-done.3.own_outer_ref.refs_0_
  13.3 0.7 %collective-permute-start.1 = (f32[264,256]{1,0:T(8,128)S(1)}, f32[264,256]{1,0:T(8,128)S(1)}, u32[]{:S(2)}, u32[]{:S(2)}) collective-permute-start(f32[264,256]{1,0:T(8,128)S(1)} %collective-permute-done.crossed_ref), channel_id=1, source_target_pairs={{1,2},{2,1},{5,6},{6,5},{9,10},{10,9},{13,14},{14,13},{17,18},{18,... | collective-permute-start | bytes 811016 | tf_op jit(solution)/shard_map/ppermute | solution.py:546
  13.9 0.0 collective-permute-done.4.own_inner_ref.refs_1_
  13.9 2.9 %collective-permute-start.2 = (f32[264,256]{1,0:T(8,128)S(1)}, f32[264,256]{1,0:T(8,128)S(1)}, u32[]{:S(2)}, u32[]{:S(2)}) collective-permute-start(f32[264,256]{1,0:T(8,128)S(1)} %collective-permute-done.crossed_ref), channel_id=1, source_target_pairs={{0,1},{1,0},{2,3},{3,2},{4,5},{5,4},{6,7},{7,6},{8,9},{9,8},{10,11... | collective-permute-start | bytes 811016 | tf_op jit(solution)/shard_map/ppermute | solution.py:546
  16.9 0.0 collective-permute-done.10.refs_3_
  16.9 0.0 collective-permute-done.9.refs_2_
  16.9 0.0 copy-done.4
  16.9 0.3 shard_map.97.message_ref.refs_2_
  17.2 0.0 copy-start
  17.2 0.0 copy-start.3
  17.2 1.4 %collective-permute-start.12 = (f32[520,256]{1,0:T(8,128)S(1)}, f32[520,256]{1,0:T(8,128)S(1)}, u32[]{:S(2)}, u32[]{:S(2)}) collective-permute-start(f32[520,256]{1,0:T(8,128)S(1)} %shard_map.97.message_ref.refs_2_), channel_id=1, source_target_pairs={{4,12},{12,20},{20,28},{8,0},{16,8},{24,16},{5,13},{13,21},{21,29}... | collective-permute-start | bytes 1597448 | tf_op jit(solution)/shard_map/ppermute | solution.py:542
  18.6 0.7 %collective-permute-done.6.crossed_ref = f32[256,256]{1,0:T(8,128)S(1)} collective-permute-done((f32[256,256]{1,0:T(8,128)S(1)}, f32[256,256]{1,0:T(8,128)S(1)}, u32[]{:S(2)}, u32[]{:S(2)}) %collective-permute-start.6) | collective-permute-done | bytes 262176 | tf_op jit(solution)/shard_map/ppermute | solution.py:539
  19.4 0.7 %collective-permute-start.7 = (f32[256,256]{1,0:T(8,128)S(1)}, f32[256,256]{1,0:T(8,128)S(1)}, u32[]{:S(2)}, u32[]{:S(2)}) collective-permute-start(f32[256,256]{1,0:T(8,128)S(1)} %collective-permute-done.6.crossed_ref), channel_id=1, source_target_pairs={{1,2},{2,1},{5,6},{6,5},{9,10},{10,9},{13,14},{14,13},{17,18},{18,... | collective-permute-start | bytes 786440 | tf_op jit(solution)/shard_map/ppermute | solution.py:546
  20.0 2.5 %collective-permute-start.8 = (f32[256,256]{1,0:T(8,128)S(1)}, f32[256,256]{1,0:T(8,128)S(1)}, u32[]{:S(2)}, u32[]{:S(2)}) collective-permute-start(f32[256,256]{1,0:T(8,128)S(1)} %collective-permute-done.6.crossed_ref), channel_id=1, source_target_pairs={{0,1},{1,0},{2,3},{3,2},{4,5},{5,4},{6,7},{7,6},{8,9},{9,8},{10,11... | collective-permute-start | bytes 786440 | tf_op jit(solution)/shard_map/ppermute | solution.py:546
  22.5 0.0 collective-permute-done.1.outer_ref
  22.5 0.0 collective-permute-done.2.inner_ref
  22.5 0.3 shard_map.96.refs_0_.refs_1_
  22.8 3.5 %collective-permute-start.5 = (f32[264,256]{1,0:T(8,128)S(1)}, f32[264,256]{1,0:T(8,128)S(1)}, u32[]{:S(2)}, u32[]{:S(2)}) collective-permute-start(f32[264,256]{1,0:T(8,128)S(1)} %shard_map.96.refs_0_.refs_1_), channel_id=1, source_target_pairs={{12,4},{20,12},{28,20},{0,8},{8,16},{16,24},{13,5},{21,13},{29,21}... | collective-permute-start | bytes 811016 | tf_op jit(solution)/shard_map/ppermute | solution.py:551
  26.3 0.0 copy-done
  26.3 0.0 copy-done.3
  26.3 2.6 %shard_map.98 = (f32[2,256,256]{2,1,0:T(8,128)S(1)}, f32[2,256,256]{2,1,0:T(8,128)S(1)}, f32[2,256,256]{2,1,0:T(8,128)S(1)}) custom-call(f32[520,256]{1,0:T(8,128)S(1)} %shard_map.97.message_ref.refs_2_, f32[1,256,256]{2,1,0:T(8,128)S(1)} %copy-done, f32[1,256]{1,0:T(1,128)S(1)} %copy-done.3), custom_call_target="tpu_custom_call" | custom-call | tf_op jit(solution)/shard_map/pallas_call | solution.py:198
  28.9 0.0 collective-permute-done.7.outer_ref
  28.9 0.0 collective-permute-done.8.inner_ref
  29.0 0.3 shard_map.99.refs_1_.refs_2_
  29.2 3.7 %collective-permute-start.11 = (f32[256,256]{1,0:T(8,128)S(1)}, f32[256,256]{1,0:T(8,128)S(1)}, u32[]{:S(2)}, u32[]{:S(2)}) collective-permute-start(f32[256,256]{1,0:T(8,128)S(1)} %shard_map.99.refs_1_.refs_2_), channel_id=1, source_target_pairs={{12,4},{20,12},{28,20},{0,8},{8,16},{16,24},{13,5},{21,13},{29,21}... | collective-permute-start | bytes 786440 | tf_op jit(solution)/shard_map/ppermute | solution.py:551
  32.9 0.0 copy-start.1
  32.9 0.0 copy-start.2
  32.9 2.7 %shard_map.100 = (f32[2,256,256]{2,1,0:T(8,128)S(1)}, f32[2,256,256]{2,1,0:T(8,128)S(1)}, f32[2,256,256]{2,1,0:T(8,128)S(1)}, f32[2,256,256]{2,1,0:T(8,128)S(1)}) custom-call(f32[264,256]{1,0:T(8,128)S(1)} %shard_map.96.refs_0_.refs_1_, f32[256,256]{1,0:T(8,128)S(1)} %shard_map.99.refs_1_.refs_2_, f32[520,256]{1,0:T(8,128)S(1)} %shard_map.97.message_ref.refs_2_, ...), custom_call_target="tpu_custom_call" | custom-call | tf_op jit(solution)/shard_map/pallas_call | solution.py:198
  35.7 0.0 collective-permute-done.12.refs_0_
  35.7 0.0 copy-done.1
  35.7 0.0 copy-done.2
  35.7 4.8 %shard_map.101 = (f32[32,1,896]{2,1,0:T(1,128)S(1)}, f32[1,256]{1,0:T(1,128)S(1)}, f32[2,24,128]{2,1,0:T(8,128)S(1)}) custom-call(f32[520,256]{1,0:T(8,128)S(1)} %collective-permute-done.12.refs_0_, f32[264,256]{1,0:T(8,128)S(1)} %shard_map.96.refs_0_.refs_1_, f32[256,256]{1,0:T(8,128)S(1)} %shard_map.99.refs_1_.refs_2_, ...), custom_call_target="tpu_custom_call" | custom-call | tf_op jit(solution)/shard_map/pallas_call | solution.py:198
  40.5 0.0 collective-permute-done.11.refs_1_
  40.5 0.0 collective-permute-done.5.refs_0_
  40.5 4.7 %shard_map.102 = (f32[32,1,896]{2,1,0:T(1,128)S(1)}, f32[1,256]{1,0:T(1,128)S(1)}) custom-call(f32[264,256]{1,0:T(8,128)S(1)} %collective-permute-done.5.refs_0_, f32[256,256]{1,0:T(8,128)S(1)} %collective-permute-done.11.refs_1_, f32[520,256]{1,0:T(8,128)S(1)} %shard_map.97.message_ref.refs_2_, ...), custom_call_target="tpu_custom_call", output_to_operand_aliasing={{0}: (8, {})} | custom-call | tf_op jit(solution)/shard_map/pallas_call | solution.py:198
  45.3 11.0 %all_to_all.5 = f32[32,1,896]{2,1,0:T(1,128)S(1)} all-to-all(f32[32,1,896]{2,1,0:T(1,128)S(1)} %get-tuple-element.37), channel_id=1, replica_groups=mesh['energy'=8,'slab'=4] {'energy','slab'}, dimensions={0} | all-to-all | bytes 229376 | tf_op jit(solution)/shard_map/all_to_all | solution.py:561
  56.3 0.9 %shard_map.103 = (f32[1,2,256]{2,1,0:T(2,128)}, f32[1,16,128]{2,1,0:T(8,128)}) custom-call(f32[8,4,1,896]{3,2,1,0:T(1,128)S(1)} %bitcast.1, f32[1,256]{1,0:T(1,128)S(1)} %get-tuple-element.38.own_ref, f32[2,24,128]{2,1,0:T(8,128)S(1)} %get-tuple-element.39.local_ref), custom_call_target="tpu_custom_call" | custom-call | tf_op jit(solution)/shard_map/pallas_call | solution.py:198
Async XLA Ops:
  2.0 9.5 %collective-permute-start = (f32[264,256]{1,0:T(8,128)S(1)}, f32[264,256]{1,0:T(8,128)S(1)}, u32[]{:S(2)}, u32[]{:S(2)}) collective-permute-start(f32[264,256]{1,0:T(8,128)S(1)} %get-tuple-element.21), channel_id=1, source_target_pairs={{0,4},{4,0},{8,12},{12,8},{16,20},{20,16},{24,28},{28,24},{1,5},{5... | collective-permute-start | bytes 811016 | tf_op jit(solution)/shard_map/ppermute | solution.py:539
  5.0 8.2 %collective-permute-start.3 = (f32[272,256]{1,0:T(8,128)S(1)}, f32[272,256]{1,0:T(8,128)S(1)}, u32[]{:S(2)}, u32[]{:S(2)}) collective-permute-start(f32[272,256]{1,0:T(8,128)S(1)} %get-tuple-element.22), channel_id=1, source_target_pairs={{1,2},{2,1},{5,6},{6,5},{9,10},{10,9},{13,14},{14,13},{17,18},{18,... | collective-permute-start | bytes 835592 | tf_op jit(solution)/shard_map/ppermute | solution.py:540
  5.7 8.2 %collective-permute-start.4 = (f32[272,256]{1,0:T(8,128)S(1)}, f32[272,256]{1,0:T(8,128)S(1)}, u32[]{:S(2)}, u32[]{:S(2)}) collective-permute-start(f32[272,256]{1,0:T(8,128)S(1)} %get-tuple-element.22), channel_id=1, source_target_pairs={{0,1},{1,0},{2,3},{3,2},{4,5},{5,4},{6,7},{7,6},{8,9},{9,8},{10,11... | collective-permute-start | bytes 835592 | tf_op jit(solution)/shard_map/ppermute | solution.py:540
  8.6 8.2 %collective-permute-start.10 = (f32[272,256]{1,0:T(8,128)S(1)}, f32[272,256]{1,0:T(8,128)S(1)}, u32[]{:S(2)}, u32[]{:S(2)}) collective-permute-start(f32[272,256]{1,0:T(8,128)S(1)} %get-tuple-element.24), channel_id=1, source_target_pairs={{0,1},{1,0},{2,3},{3,2},{4,5},{5,4},{6,7},{7,6},{8,9},{9,8},{10,11... | collective-permute-start | bytes 835592 | tf_op jit(solution)/shard_map/ppermute | solution.py:540
  8.7 8.2 %collective-permute-start.9 = (f32[272,256]{1,0:T(8,128)S(1)}, f32[272,256]{1,0:T(8,128)S(1)}, u32[]{:S(2)}, u32[]{:S(2)}) collective-permute-start(f32[272,256]{1,0:T(8,128)S(1)} %get-tuple-element.24), channel_id=1, source_target_pairs={{1,2},{2,1},{5,6},{6,5},{9,10},{10,9},{13,14},{14,13},{17,18},{18,... | collective-permute-start | bytes 835592 | tf_op jit(solution)/shard_map/ppermute | solution.py:540
  11.5 5.4 %copy-start.4 = (f32[1,256]{1,0:T(1,128)S(1)}, f32[1,256]{1,0:T(1,128)}, u32[]{:S(2)}) copy-start(f32[1,256]{1,0:T(1,128)} %coupling_ref.5) | copy-start | bytes 3076
  11.5 7.8 %collective-permute-start.6 = (f32[256,256]{1,0:T(8,128)S(1)}, f32[256,256]{1,0:T(8,128)S(1)}, u32[]{:S(2)}, u32[]{:S(2)}) collective-permute-start(f32[256,256]{1,0:T(8,128)S(1)} %get-tuple-element.23), channel_id=1, source_target_pairs={{0,4},{4,0},{8,12},{12,8},{16,20},{20,16},{24,28},{28,24},{1,5},{5... | collective-permute-start | bytes 786440 | tf_op jit(solution)/shard_map/ppermute | solution.py:539
  13.3 9.3 %collective-permute-start.1 = (f32[264,256]{1,0:T(8,128)S(1)}, f32[264,256]{1,0:T(8,128)S(1)}, u32[]{:S(2)}, u32[]{:S(2)}) collective-permute-start(f32[264,256]{1,0:T(8,128)S(1)} %collective-permute-done.crossed_ref), channel_id=1, source_target_pairs={{1,2},{2,1},{5,6},{6,5},{9,10},{10,9},{13,14},{14,13},{17,18},{18,... | collective-permute-start | bytes 811016 | tf_op jit(solution)/shard_map/ppermute | solution.py:546
  13.9 8.6 %collective-permute-start.2 = (f32[264,256]{1,0:T(8,128)S(1)}, f32[264,256]{1,0:T(8,128)S(1)}, u32[]{:S(2)}, u32[]{:S(2)}) collective-permute-start(f32[264,256]{1,0:T(8,128)S(1)} %collective-permute-done.crossed_ref), channel_id=1, source_target_pairs={{0,1},{1,0},{2,3},{3,2},{4,5},{5,4},{6,7},{7,6},{8,9},{9,8},{10,11... | collective-permute-start | bytes 811016 | tf_op jit(solution)/shard_map/ppermute | solution.py:546
  17.2 9.2 %copy-start = (f32[1,256,256]{2,1,0:T(8,128)S(1)}, f32[1,256,256]{2,1,0:T(8,128)}, u32[]{:S(2)}) copy-start(f32[1,256,256]{2,1,0:T(8,128)} %refs_5_.3) | copy-start | bytes 786436
  17.2 9.2 %copy-start.3 = (f32[1,256]{1,0:T(1,128)S(1)}, f32[1,256]{1,0:T(1,128)}, u32[]{:S(2)}) copy-start(f32[1,256]{1,0:T(1,128)} %refs_6_.5) | copy-start | bytes 3076
  17.2 18.5 %collective-permute-start.12 = (f32[520,256]{1,0:T(8,128)S(1)}, f32[520,256]{1,0:T(8,128)S(1)}, u32[]{:S(2)}, u32[]{:S(2)}) collective-permute-start(f32[520,256]{1,0:T(8,128)S(1)} %shard_map.97.message_ref.refs_2_), channel_id=1, source_target_pairs={{4,12},{12,20},{20,28},{8,0},{16,8},{24,16},{5,13},{13,21},{21,29}... | collective-permute-start | bytes 1597448 | tf_op jit(solution)/shard_map/ppermute | solution.py:542
  19.4 9.6 %collective-permute-start.7 = (f32[256,256]{1,0:T(8,128)S(1)}, f32[256,256]{1,0:T(8,128)S(1)}, u32[]{:S(2)}, u32[]{:S(2)}) collective-permute-start(f32[256,256]{1,0:T(8,128)S(1)} %collective-permute-done.6.crossed_ref), channel_id=1, source_target_pairs={{1,2},{2,1},{5,6},{6,5},{9,10},{10,9},{13,14},{14,13},{17,18},{18,... | collective-permute-start | bytes 786440 | tf_op jit(solution)/shard_map/ppermute | solution.py:546
  20.0 8.9 %collective-permute-start.8 = (f32[256,256]{1,0:T(8,128)S(1)}, f32[256,256]{1,0:T(8,128)S(1)}, u32[]{:S(2)}, u32[]{:S(2)}) collective-permute-start(f32[256,256]{1,0:T(8,128)S(1)} %collective-permute-done.6.crossed_ref), channel_id=1, source_target_pairs={{0,1},{1,0},{2,3},{3,2},{4,5},{5,4},{6,7},{7,6},{8,9},{9,8},{10,11... | collective-permute-start | bytes 786440 | tf_op jit(solution)/shard_map/ppermute | solution.py:546
  22.8 17.7 %collective-permute-start.5 = (f32[264,256]{1,0:T(8,128)S(1)}, f32[264,256]{1,0:T(8,128)S(1)}, u32[]{:S(2)}, u32[]{:S(2)}) collective-permute-start(f32[264,256]{1,0:T(8,128)S(1)} %shard_map.96.refs_0_.refs_1_), channel_id=1, source_target_pairs={{12,4},{20,12},{28,20},{0,8},{8,16},{16,24},{13,5},{21,13},{29,21}... | collective-permute-start | bytes 811016 | tf_op jit(solution)/shard_map/ppermute | solution.py:551
  29.2 11.3 %collective-permute-start.11 = (f32[256,256]{1,0:T(8,128)S(1)}, f32[256,256]{1,0:T(8,128)S(1)}, u32[]{:S(2)}, u32[]{:S(2)}) collective-permute-start(f32[256,256]{1,0:T(8,128)S(1)} %shard_map.99.refs_1_.refs_2_), channel_id=1, source_target_pairs={{12,4},{20,12},{28,20},{0,8},{8,16},{16,24},{13,5},{21,13},{29,21}... | collective-permute-start | bytes 786440 | tf_op jit(solution)/shard_map/ppermute | solution.py:551
  32.9 2.8 %copy-start.1 = (s32[1,128,128]{2,1,0:T(8,128)S(1)}, s32[1,128,128]{2,1,0:T(8,128)}, u32[]{:S(2)}) copy-start(s32[1,128,128]{2,1,0:T(8,128)} %refs_7_.3) | copy-start | bytes 196612
  32.9 2.8 %copy-start.2 = (f32[1,128,128]{2,1,0:T(8,128)S(1)}, f32[1,128,128]{2,1,0:T(8,128)}, u32[]{:S(2)}) copy-start(f32[1,128,128]{2,1,0:T(8,128)} %refs_8_.1) | copy-start | bytes 196612

commit v5 on v4

--- a/solution.py
+++ b/solution.py
@@ -214,8 +214,8 @@
         own_levels_ref, held_refs, sems = refs[6], refs[7:9], refs[9]
         parity = lax.rem(lax.axis_index("energy"), SHIFT)
         moves = [
+            *zip(level_refs, held_refs),
             (block_ref.at[0, 0, 1 - parity], real_ref.at[pl.ds(0, rows)]),
-            *zip(level_refs, held_refs),
             (block_ref.at[1, 0, 1 - parity], imag_ref.at[pl.ds(0, rows)]),
             (block_ref.at[0, 0, parity], own_refs[0].at[pl.ds(0, rows)]),
             (coupling_ref, own_refs[0].at[pl.ds(rows, 1)]),
@@ -227,7 +227,7 @@
         ]
         for copy in copies:
             copy.start()
-        for copy in copies:
+        for copy in copies[:2]:
             copy.wait()
         damping_here, occupation_here = (held_ref[...] for held_ref in held_refs)
         which = lax.broadcasted_iota(jnp.int32, (SUBLANES, columns), 0)
@@ -237,6 +237,8 @@
         ]
         real_ref[rows : rows + SUBLANES, :] = jnp.where(parity == 0, levels[1], levels[0])
         own_levels_ref[...] = jnp.where(parity == 0, levels[0], levels[1])
+        for copy in copies[2:]:
+            copy.wait()
 
     operands = (boundary_green, coupling, damping, occupation)
     return call(

time: 57.5 us -> 57.5 us (level)
  no operation moved by 1% of the time
where the time goes in v5:
time: 57.5 us; the launch traced here: 57.2 us
  starting transfers between devices  24.4 us (42%)
  Pallas kernels  17.9 us (31%)
  blocking collectives  11 us (19%)
  waiting for transfers between devices  2.89 us (5%)
  between operations  0.86 us (1%)
    pallas_call x9, Pallas kernels, call(): pl.pallas_call(kernel, out_shape=shapes, in_specs=specs, out_specs=[vmem(...  17.9 us
    all_to_all x1, blocking collectives, per_device(): parcels = lax.all_to_all(parcels, DEVICES, 0, 0)  11 us
    ppermute x2, starting transfers between devices, per_device(): late.append(lax.ppermute(paired[-1], 'energy', near))  7.16 us
    ppermute x4, starting transfers between devices, per_device(): sides = [lax.ppermute(part, 'slab', way) for way in swaps]  6.77 us
    ppermute x2, starting transfers between devices, per_device(): crossed = [lax.ppermute(part, 'energy', pair) for part in blocks[:2]]  4.74 us
    ppermute x4, starting transfers between devices, per_device(): lax.ppermute(part, 'slab', way)  4.34 us
    ppermute x2, waiting for transfers between devices, per_device(): crossed = [lax.ppermute(part, 'energy', pair) for part in blocks[:2]]  2.86 us
    ppermute x1, starting transfers between devices, per_device(): early = lax.ppermute(mine, 'energy', far)  1.42 us
  transfers between devices with their start and end apart: 13, of which 2 were waited for; matrix products, arithmetic and copies ran while one was open for 0% of the time, Pallas kernels for 19%

profile of v5, /device:TPU:0, one launch (start us, length us, event | category | flops | bytes accessed | tf_op | source)
XLA Modules:
  0.0 57.2 jit_solution(2546706661686668858)
XLA Ops:
  0.6 1.3 %shard_map.95 = (f32[264,256]{1,0:T(8,128)S(1)}, f32[256,256]{1,0:T(8,128)S(1)}, f32[272,256]{1,0:T(8,128)S(1)}, f32[272,256]{1,0:T(8,128)S(1)}, f32[8,256]{1,0:T(8,128)S(1)}) custom-call(f32[2,1,2,256,256]{4,3,2,1,0:T(8,128)} %block_ref.1, f32[1,256]{1,0:T(1,128)} %coupling_ref.5, f32[1,2]{1,0:T(1,128)} %refs_0_.1, f32[1,2]{1,0:T(1,128)} %refs_1_.1), custom_call_target="tpu_custom_call" | custom-call | tf_op jit(solution)/shard_map/pallas_call | solution.py:198
  1.9 3.0 %collective-permute-start = (f32[264,256]{1,0:T(8,128)S(1)}, f32[264,256]{1,0:T(8,128)S(1)}, u32[]{:S(2)}, u32[]{:S(2)}) collective-permute-start(f32[264,256]{1,0:T(8,128)S(1)} %get-tuple-element.21), channel_id=1, source_target_pairs={{0,4},{4,0},{8,12},{12,8},{16,20},{20,16},{24,28},{28,24},{1,5},{5... | collective-permute-start | bytes 811016 | tf_op jit(solution)/shard_map/ppermute | solution.py:541
  4.9 0.7 %collective-permute-start.3 = (f32[272,256]{1,0:T(8,128)S(1)}, f32[272,256]{1,0:T(8,128)S(1)}, u32[]{:S(2)}, u32[]{:S(2)}) collective-permute-start(f32[272,256]{1,0:T(8,128)S(1)} %get-tuple-element.22), channel_id=1, source_target_pairs={{1,2},{2,1},{5,6},{6,5},{9,10},{10,9},{13,14},{14,13},{17,18},{18,... | collective-permute-start | bytes 835592 | tf_op jit(solution)/shard_map/ppermute | solution.py:542
  5.6 2.9 %collective-permute-start.4 = (f32[272,256]{1,0:T(8,128)S(1)}, f32[272,256]{1,0:T(8,128)S(1)}, u32[]{:S(2)}, u32[]{:S(2)}) collective-permute-start(f32[272,256]{1,0:T(8,128)S(1)} %get-tuple-element.22), channel_id=1, source_target_pairs={{0,1},{1,0},{2,3},{3,2},{4,5},{5,4},{6,7},{7,6},{8,9},{9,8},{10,11... | collective-permute-start | bytes 835592 | tf_op jit(solution)/shard_map/ppermute | solution.py:542
  8.5 0.1 collective-permute-start.10
  8.6 0.7 %collective-permute-start.9 = (f32[272,256]{1,0:T(8,128)S(1)}, f32[272,256]{1,0:T(8,128)S(1)}, u32[]{:S(2)}, u32[]{:S(2)}) collective-permute-start(f32[272,256]{1,0:T(8,128)S(1)} %get-tuple-element.24), channel_id=1, source_target_pairs={{1,2},{2,1},{5,6},{6,5},{9,10},{10,9},{13,14},{14,13},{17,18},{18,... | collective-permute-start | bytes 835592 | tf_op jit(solution)/shard_map/ppermute | solution.py:542
  9.3 2.1 %collective-permute-done.crossed_ref = f32[264,256]{1,0:T(8,128)S(1)} collective-permute-done((f32[264,256]{1,0:T(8,128)S(1)}, f32[264,256]{1,0:T(8,128)S(1)}, u32[]{:S(2)}, u32[]{:S(2)}) %collective-permute-start) | collective-permute-done | bytes 270368 | tf_op jit(solution)/shard_map/ppermute | solution.py:541
  11.4 0.0 copy-start.4
  11.4 1.7 %collective-permute-start.6 = (f32[256,256]{1,0:T(8,128)S(1)}, f32[256,256]{1,0:T(8,128)S(1)}, u32[]{:S(2)}, u32[]{:S(2)}) collective-permute-start(f32[256,256]{1,0:T(8,128)S(1)} %get-tuple-element.23), channel_id=1, source_target_pairs={{0,4},{4,0},{8,12},{12,8},{16,20},{20,16},{24,28},{28,24},{1,5},{5... | collective-permute-start | bytes 786440 | tf_op jit(solution)/shard_map/ppermute | solution.py:541
  13.2 0.0 collective-permute-done.3.own_outer_ref.refs_0_
  13.2 0.7 %collective-permute-start.1 = (f32[264,256]{1,0:T(8,128)S(1)}, f32[264,256]{1,0:T(8,128)S(1)}, u32[]{:S(2)}, u32[]{:S(2)}) collective-permute-start(f32[264,256]{1,0:T(8,128)S(1)} %collective-permute-done.crossed_ref), channel_id=1, source_target_pairs={{1,2},{2,1},{5,6},{6,5},{9,10},{10,9},{13,14},{14,13},{17,18},{18,... | collective-permute-start | bytes 811016 | tf_op jit(solution)/shard_map/ppermute | solution.py:548
  13.8 0.0 collective-permute-done.4.own_inner_ref.refs_1_
  13.9 2.9 %collective-permute-start.2 = (f32[264,256]{1,0:T(8,128)S(1)}, f32[264,256]{1,0:T(8,128)S(1)}, u32[]{:S(2)}, u32[]{:S(2)}) collective-permute-start(f32[264,256]{1,0:T(8,128)S(1)} %collective-permute-done.crossed_ref), channel_id=1, source_target_pairs={{0,1},{1,0},{2,3},{3,2},{4,5},{5,4},{6,7},{7,6},{8,9},{9,8},{10,11... | collective-permute-start | bytes 811016 | tf_op jit(solution)/shard_map/ppermute | solution.py:548
  16.8 0.0 collective-permute-done.10.refs_3_
  16.8 0.0 collective-permute-done.9.refs_2_
  16.8 0.0 copy-done.4
  16.8 0.3 shard_map.97.message_ref.refs_2_
  17.1 0.0 copy-start
  17.1 0.0 copy-start.3
  17.1 1.4 %collective-permute-start.12 = (f32[520,256]{1,0:T(8,128)S(1)}, f32[520,256]{1,0:T(8,128)S(1)}, u32[]{:S(2)}, u32[]{:S(2)}) collective-permute-start(f32[520,256]{1,0:T(8,128)S(1)} %shard_map.97.message_ref.refs_2_), channel_id=1, source_target_pairs={{4,12},{12,20},{20,28},{8,0},{16,8},{24,16},{5,13},{13,21},{21,29}... | collective-permute-start | bytes 1597448 | tf_op jit(solution)/shard_map/ppermute | solution.py:544
  18.5 0.7 %collective-permute-done.6.crossed_ref = f32[256,256]{1,0:T(8,128)S(1)} collective-permute-done((f32[256,256]{1,0:T(8,128)S(1)}, f32[256,256]{1,0:T(8,128)S(1)}, u32[]{:S(2)}, u32[]{:S(2)}) %collective-permute-start.6) | collective-permute-done | bytes 262176 | tf_op jit(solution)/shard_map/ppermute | solution.py:541
  19.3 0.7 %collective-permute-start.7 = (f32[256,256]{1,0:T(8,128)S(1)}, f32[256,256]{1,0:T(8,128)S(1)}, u32[]{:S(2)}, u32[]{:S(2)}) collective-permute-start(f32[256,256]{1,0:T(8,128)S(1)} %collective-permute-done.6.crossed_ref), channel_id=1, source_target_pairs={{1,2},{2,1},{5,6},{6,5},{9,10},{10,9},{13,14},{14,13},{17,18},{18,... | collective-permute-start | bytes 786440 | tf_op jit(solution)/shard_map/ppermute | solution.py:548
  19.9 2.5 %collective-permute-start.8 = (f32[256,256]{1,0:T(8,128)S(1)}, f32[256,256]{1,0:T(8,128)S(1)}, u32[]{:S(2)}, u32[]{:S(2)}) collective-permute-start(f32[256,256]{1,0:T(8,128)S(1)} %collective-permute-done.6.crossed_ref), channel_id=1, source_target_pairs={{0,1},{1,0},{2,3},{3,2},{4,5},{5,4},{6,7},{7,6},{8,9},{9,8},{10,11... | collective-permute-start | bytes 786440 | tf_op jit(solution)/shard_map/ppermute | solution.py:548
  22.5 0.0 collective-permute-done.1.outer_ref
  22.5 0.0 collective-permute-done.2.inner_ref
  22.5 0.3 shard_map.96.refs_0_.refs_1_
  22.7 3.5 %collective-permute-start.5 = (f32[264,256]{1,0:T(8,128)S(1)}, f32[264,256]{1,0:T(8,128)S(1)}, u32[]{:S(2)}, u32[]{:S(2)}) collective-permute-start(f32[264,256]{1,0:T(8,128)S(1)} %shard_map.96.refs_0_.refs_1_), channel_id=1, source_target_pairs={{12,4},{20,12},{28,20},{0,8},{8,16},{16,24},{13,5},{21,13},{29,21}... | collective-permute-start | bytes 811016 | tf_op jit(solution)/shard_map/ppermute | solution.py:553
  26.2 0.0 copy-done
  26.2 0.0 copy-done.3
  26.3 2.6 %shard_map.98 = (f32[2,256,256]{2,1,0:T(8,128)S(1)}, f32[2,256,256]{2,1,0:T(8,128)S(1)}, f32[2,256,256]{2,1,0:T(8,128)S(1)}) custom-call(f32[520,256]{1,0:T(8,128)S(1)} %shard_map.97.message_ref.refs_2_, f32[1,256,256]{2,1,0:T(8,128)S(1)} %copy-done, f32[1,256]{1,0:T(1,128)S(1)} %copy-done.3), custom_call_target="tpu_custom_call" | custom-call | tf_op jit(solution)/shard_map/pallas_call | solution.py:198
  28.9 0.0 collective-permute-done.7.outer_ref
  28.9 0.0 collective-permute-done.8.inner_ref
  28.9 0.3 shard_map.99.refs_1_.refs_2_
  29.2 3.7 %collective-permute-start.11 = (f32[256,256]{1,0:T(8,128)S(1)}, f32[256,256]{1,0:T(8,128)S(1)}, u32[]{:S(2)}, u32[]{:S(2)}) collective-permute-start(f32[256,256]{1,0:T(8,128)S(1)} %shard_map.99.refs_1_.refs_2_), channel_id=1, source_target_pairs={{12,4},{20,12},{28,20},{0,8},{8,16},{16,24},{13,5},{21,13},{29,21}... | collective-permute-start | bytes 786440 | tf_op jit(solution)/shard_map/ppermute | solution.py:553
  32.8 0.0 copy-start.1
  32.8 0.0 copy-start.2
  32.8 2.7 %shard_map.100 = (f32[2,256,256]{2,1,0:T(8,128)S(1)}, f32[2,256,256]{2,1,0:T(8,128)S(1)}, f32[2,256,256]{2,1,0:T(8,128)S(1)}, f32[2,256,256]{2,1,0:T(8,128)S(1)}) custom-call(f32[264,256]{1,0:T(8,128)S(1)} %shard_map.96.refs_0_.refs_1_, f32[256,256]{1,0:T(8,128)S(1)} %shard_map.99.refs_1_.refs_2_, f32[520,256]{1,0:T(8,128)S(1)} %shard_map.97.message_ref.refs_2_, ...), custom_call_target="tpu_custom_call" | custom-call | tf_op jit(solution)/shard_map/pallas_call | solution.py:198
  35.6 0.0 collective-permute-done.12.refs_0_
  35.6 0.0 copy-done.1
  35.6 0.0 copy-done.2
  35.6 4.8 %shard_map.101 = (f32[32,1,896]{2,1,0:T(1,128)S(1)}, f32[1,256]{1,0:T(1,128)S(1)}, f32[2,24,128]{2,1,0:T(8,128)S(1)}) custom-call(f32[520,256]{1,0:T(8,128)S(1)} %collective-permute-done.12.refs_0_, f32[264,256]{1,0:T(8,128)S(1)} %shard_map.96.refs_0_.refs_1_, f32[256,256]{1,0:T(8,128)S(1)} %shard_map.99.refs_1_.refs_2_, ...), custom_call_target="tpu_custom_call" | custom-call | tf_op jit(solution)/shard_map/pallas_call | solution.py:198
  40.4 0.0 collective-permute-done.11.refs_1_
  40.5 0.0 collective-permute-done.5.refs_0_
  40.5 4.7 %shard_map.102 = (f32[32,1,896]{2,1,0:T(1,128)S(1)}, f32[1,256]{1,0:T(1,128)S(1)}) custom-call(f32[264,256]{1,0:T(8,128)S(1)} %collective-permute-done.5.refs_0_, f32[256,256]{1,0:T(8,128)S(1)} %collective-permute-done.11.refs_1_, f32[520,256]{1,0:T(8,128)S(1)} %shard_map.97.message_ref.refs_2_, ...), custom_call_target="tpu_custom_call", output_to_operand_aliasing={{0}: (8, {})} | custom-call | tf_op jit(solution)/shard_map/pallas_call | solution.py:198
  45.2 11.0 %all_to_all.5 = f32[32,1,896]{2,1,0:T(1,128)S(1)} all-to-all(f32[32,1,896]{2,1,0:T(1,128)S(1)} %get-tuple-element.37), channel_id=1, replica_groups=mesh['energy'=8,'slab'=4] {'energy','slab'}, dimensions={0} | all-to-all | bytes 229376 | tf_op jit(solution)/shard_map/all_to_all | solution.py:563
  56.2 0.9 %shard_map.103 = (f32[1,2,256]{2,1,0:T(2,128)}, f32[1,16,128]{2,1,0:T(8,128)}) custom-call(f32[8,4,1,896]{3,2,1,0:T(1,128)S(1)} %bitcast.1, f32[1,256]{1,0:T(1,128)S(1)} %get-tuple-element.38.own_ref, f32[2,24,128]{2,1,0:T(8,128)S(1)} %get-tuple-element.39.local_ref), custom_call_target="tpu_custom_call" | custom-call | tf_op jit(solution)/shard_map/pallas_call | solution.py:198
Async XLA Ops:
  1.9 9.5 %collective-permute-start = (f32[264,256]{1,0:T(8,128)S(1)}, f32[264,256]{1,0:T(8,128)S(1)}, u32[]{:S(2)}, u32[]{:S(2)}) collective-permute-start(f32[264,256]{1,0:T(8,128)S(1)} %get-tuple-element.21), channel_id=1, source_target_pairs={{0,4},{4,0},{8,12},{12,8},{16,20},{20,16},{24,28},{28,24},{1,5},{5... | collective-permute-start | bytes 811016 | tf_op jit(solution)/shard_map/ppermute | solution.py:541
  4.9 8.2 %collective-permute-start.3 = (f32[272,256]{1,0:T(8,128)S(1)}, f32[272,256]{1,0:T(8,128)S(1)}, u32[]{:S(2)}, u32[]{:S(2)}) collective-permute-start(f32[272,256]{1,0:T(8,128)S(1)} %get-tuple-element.22), channel_id=1, source_target_pairs={{1,2},{2,1},{5,6},{6,5},{9,10},{10,9},{13,14},{14,13},{17,18},{18,... | collective-permute-start | bytes 835592 | tf_op jit(solution)/shard_map/ppermute | solution.py:542
  5.6 8.2 %collective-permute-start.4 = (f32[272,256]{1,0:T(8,128)S(1)}, f32[272,256]{1,0:T(8,128)S(1)}, u32[]{:S(2)}, u32[]{:S(2)}) collective-permute-start(f32[272,256]{1,0:T(8,128)S(1)} %get-tuple-element.22), channel_id=1, source_target_pairs={{0,1},{1,0},{2,3},{3,2},{4,5},{5,4},{6,7},{7,6},{8,9},{9,8},{10,11... | collective-permute-start | bytes 835592 | tf_op jit(solution)/shard_map/ppermute | solution.py:542
  8.5 8.2 %collective-permute-start.10 = (f32[272,256]{1,0:T(8,128)S(1)}, f32[272,256]{1,0:T(8,128)S(1)}, u32[]{:S(2)}, u32[]{:S(2)}) collective-permute-start(f32[272,256]{1,0:T(8,128)S(1)} %get-tuple-element.24), channel_id=1, source_target_pairs={{0,1},{1,0},{2,3},{3,2},{4,5},{5,4},{6,7},{7,6},{8,9},{9,8},{10,11... | collective-permute-start | bytes 835592 | tf_op jit(solution)/shard_map/ppermute | solution.py:542
  8.6 8.2 %collective-permute-start.9 = (f32[272,256]{1,0:T(8,128)S(1)}, f32[272,256]{1,0:T(8,128)S(1)}, u32[]{:S(2)}, u32[]{:S(2)}) collective-permute-start(f32[272,256]{1,0:T(8,128)S(1)} %get-tuple-element.24), channel_id=1, source_target_pairs={{1,2},{2,1},{5,6},{6,5},{9,10},{10,9},{13,14},{14,13},{17,18},{18,... | collective-permute-start | bytes 835592 | tf_op jit(solution)/shard_map/ppermute | solution.py:542
  11.4 5.4 %copy-start.4 = (f32[1,256]{1,0:T(1,128)S(1)}, f32[1,256]{1,0:T(1,128)}, u32[]{:S(2)}) copy-start(f32[1,256]{1,0:T(1,128)} %coupling_ref.5) | copy-start | bytes 3076
  11.4 7.8 %collective-permute-start.6 = (f32[256,256]{1,0:T(8,128)S(1)}, f32[256,256]{1,0:T(8,128)S(1)}, u32[]{:S(2)}, u32[]{:S(2)}) collective-permute-start(f32[256,256]{1,0:T(8,128)S(1)} %get-tuple-element.23), channel_id=1, source_target_pairs={{0,4},{4,0},{8,12},{12,8},{16,20},{20,16},{24,28},{28,24},{1,5},{5... | collective-permute-start | bytes 786440 | tf_op jit(solution)/shard_map/ppermute | solution.py:541
  13.2 9.3 %collective-permute-start.1 = (f32[264,256]{1,0:T(8,128)S(1)}, f32[264,256]{1,0:T(8,128)S(1)}, u32[]{:S(2)}, u32[]{:S(2)}) collective-permute-start(f32[264,256]{1,0:T(8,128)S(1)} %collective-permute-done.crossed_ref), channel_id=1, source_target_pairs={{1,2},{2,1},{5,6},{6,5},{9,10},{10,9},{13,14},{14,13},{17,18},{18,... | collective-permute-start | bytes 811016 | tf_op jit(solution)/shard_map/ppermute | solution.py:548
  13.9 8.6 %collective-permute-start.2 = (f32[264,256]{1,0:T(8,128)S(1)}, f32[264,256]{1,0:T(8,128)S(1)}, u32[]{:S(2)}, u32[]{:S(2)}) collective-permute-start(f32[264,256]{1,0:T(8,128)S(1)} %collective-permute-done.crossed_ref), channel_id=1, source_target_pairs={{0,1},{1,0},{2,3},{3,2},{4,5},{5,4},{6,7},{7,6},{8,9},{9,8},{10,11... | collective-permute-start | bytes 811016 | tf_op jit(solution)/shard_map/ppermute | solution.py:548
  17.1 9.2 %copy-start = (f32[1,256,256]{2,1,0:T(8,128)S(1)}, f32[1,256,256]{2,1,0:T(8,128)}, u32[]{:S(2)}) copy-start(f32[1,256,256]{2,1,0:T(8,128)} %refs_5_.3) | copy-start | bytes 786436
  17.1 9.2 %copy-start.3 = (f32[1,256]{1,0:T(1,128)S(1)}, f32[1,256]{1,0:T(1,128)}, u32[]{:S(2)}) copy-start(f32[1,256]{1,0:T(1,128)} %refs_6_.5) | copy-start | bytes 3076
  17.1 18.5 %collective-permute-start.12 = (f32[520,256]{1,0:T(8,128)S(1)}, f32[520,256]{1,0:T(8,128)S(1)}, u32[]{:S(2)}, u32[]{:S(2)}) collective-permute-start(f32[520,256]{1,0:T(8,128)S(1)} %shard_map.97.message_ref.refs_2_), channel_id=1, source_target_pairs={{4,12},{12,20},{20,28},{8,0},{16,8},{24,16},{5,13},{13,21},{21,29}... | collective-permute-start | bytes 1597448 | tf_op jit(solution)/shard_map/ppermute | solution.py:544
  19.3 9.6 %collective-permute-start.7 = (f32[256,256]{1,0:T(8,128)S(1)}, f32[256,256]{1,0:T(8,128)S(1)}, u32[]{:S(2)}, u32[]{:S(2)}) collective-permute-start(f32[256,256]{1,0:T(8,128)S(1)} %collective-permute-done.6.crossed_ref), channel_id=1, source_target_pairs={{1,2},{2,1},{5,6},{6,5},{9,10},{10,9},{13,14},{14,13},{17,18},{18,... | collective-permute-start | bytes 786440 | tf_op jit(solution)/shard_map/ppermute | solution.py:548
  19.9 8.9 %collective-permute-start.8 = (f32[256,256]{1,0:T(8,128)S(1)}, f32[256,256]{1,0:T(8,128)S(1)}, u32[]{:S(2)}, u32[]{:S(2)}) collective-permute-start(f32[256,256]{1,0:T(8,128)S(1)} %collective-permute-done.6.crossed_ref), channel_id=1, source_target_pairs={{0,1},{1,0},{2,3},{3,2},{4,5},{5,4},{6,7},{7,6},{8,9},{9,8},{10,11... | collective-permute-start | bytes 786440 | tf_op jit(solution)/shard_map/ppermute | solution.py:548
  22.7 17.7 %collective-permute-start.5 = (f32[264,256]{1,0:T(8,128)S(1)}, f32[264,256]{1,0:T(8,128)S(1)}, u32[]{:S(2)}, u32[]{:S(2)}) collective-permute-start(f32[264,256]{1,0:T(8,128)S(1)} %shard_map.96.refs_0_.refs_1_), channel_id=1, source_target_pairs={{12,4},{20,12},{28,20},{0,8},{8,16},{16,24},{13,5},{21,13},{29,21}... | collective-permute-start | bytes 811016 | tf_op jit(solution)/shard_map/ppermute | solution.py:553
  29.2 11.3 %collective-permute-start.11 = (f32[256,256]{1,0:T(8,128)S(1)}, f32[256,256]{1,0:T(8,128)S(1)}, u32[]{:S(2)}, u32[]{:S(2)}) collective-permute-start(f32[256,256]{1,0:T(8,128)S(1)} %shard_map.99.refs_1_.refs_2_), channel_id=1, source_target_pairs={{12,4},{20,12},{28,20},{0,8},{8,16},{16,24},{13,5},{21,13},{29,21}... | collective-permute-start | bytes 786440 | tf_op jit(solution)/shard_map/ppermute | solution.py:553
  32.8 2.8 %copy-start.1 = (s32[1,128,128]{2,1,0:T(8,128)S(1)}, s32[1,128,128]{2,1,0:T(8,128)}, u32[]{:S(2)}) copy-start(s32[1,128,128]{2,1,0:T(8,128)} %refs_7_.3) | copy-start | bytes 196612
  32.8 2.8 %copy-start.2 = (f32[1,128,128]{2,1,0:T(8,128)S(1)}, f32[1,128,128]{2,1,0:T(8,128)}, u32[]{:S(2)}) copy-start(f32[1,128,128]{2,1,0:T(8,128)} %refs_8_.1) | copy-start | bytes 196612

commit v6 on v5

--- a/solution.py
+++ b/solution.py
@@ -16,7 +16,7 @@
 MAIN_DIAGONAL = 2.0 + 4.0 * ANISO + SCREEN
 LANES = 128
 SUBLANES = 8
-BELOW = (8, 0, 16, 16)
+BELOW = (8, 0, 24, 16)
 VMEM_BYTES = 48 * 1024 * 1024
 
 f32 = jnp.float32

time: 57.5 us -> 57.5 us (level)
  no operation moved by 1% of the time
where the time goes in v6:
time: 57.5 us; the launch traced here: 57.1 us
  starting transfers between devices  24.9 us (43%)
  Pallas kernels  17.9 us (31%)
  blocking collectives  11 us (19%)
  waiting for transfers between devices  2.46 us (4%)
  between operations  0.86 us (1%)
    pallas_call x9, Pallas kernels, call(): pl.pallas_call(kernel, out_shape=shapes, in_specs=specs, out_specs=[vmem(...  17.9 us
    all_to_all x1, blocking collectives, per_device(): parcels = lax.all_to_all(parcels, DEVICES, 0, 0)  11 us
    ppermute x4, starting transfers between devices, per_device(): sides = [lax.ppermute(part, 'slab', way) for way in swaps]  7.19 us
    ppermute x2, starting transfers between devices, per_device(): late.append(lax.ppermute(paired[-1], 'energy', near))  7.16 us
    ppermute x2, starting transfers between devices, per_device(): crossed = [lax.ppermute(part, 'energy', pair) for part in blocks[:2]]  4.74 us
    ppermute x4, starting transfers between devices, per_device(): lax.ppermute(part, 'slab', way)  4.34 us
    ppermute x2, waiting for transfers between devices, per_device(): crossed = [lax.ppermute(part, 'energy', pair) for part in blocks[:2]]  2.43 us
    ppermute x1, starting transfers between devices, per_device(): early = lax.ppermute(mine, 'energy', far)  1.42 us
  transfers between devices with their start and end apart: 13, of which 2 were waited for; matrix products, arithmetic and copies ran while one was open for 0% of the time, Pallas kernels for 19%

profile of v6, /device:TPU:0, one launch (start us, length us, event | category | flops | bytes accessed | tf_op | source)
XLA Modules:
  0.0 57.1 jit_solution(10408547629083006914)
XLA Ops:
  0.6 1.3 %shard_map.95 = (f32[264,256]{1,0:T(8,128)S(1)}, f32[256,256]{1,0:T(8,128)S(1)}, f32[280,256]{1,0:T(8,128)S(1)}, f32[272,256]{1,0:T(8,128)S(1)}, f32[8,256]{1,0:T(8,128)S(1)}) custom-call(f32[2,1,2,256,256]{4,3,2,1,0:T(8,128)} %block_ref.1, f32[1,256]{1,0:T(1,128)} %coupling_ref.5, f32[1,2]{1,0:T(1,128)} %refs_0_.1, f32[1,2]{1,0:T(1,128)} %refs_1_.1), custom_call_target="tpu_custom_call" | custom-call | tf_op jit(solution)/shard_map/pallas_call | solution.py:198
  1.9 3.0 %collective-permute-start = (f32[264,256]{1,0:T(8,128)S(1)}, f32[264,256]{1,0:T(8,128)S(1)}, u32[]{:S(2)}, u32[]{:S(2)}) collective-permute-start(f32[264,256]{1,0:T(8,128)S(1)} %get-tuple-element.21), channel_id=1, source_target_pairs={{0,4},{4,0},{8,12},{12,8},{16,20},{20,16},{24,28},{28,24},{1,5},{5... | collective-permute-start | bytes 811016 | tf_op jit(solution)/shard_map/ppermute | solution.py:541
  4.9 0.7 %collective-permute-start.3 = (f32[280,256]{1,0:T(8,128)S(1)}, f32[280,256]{1,0:T(8,128)S(1)}, u32[]{:S(2)}, u32[]{:S(2)}) collective-permute-start(f32[280,256]{1,0:T(8,128)S(1)} %get-tuple-element.22), channel_id=1, source_target_pairs={{1,2},{2,1},{5,6},{6,5},{9,10},{10,9},{13,14},{14,13},{17,18},{18,... | collective-permute-start | bytes 860168 | tf_op jit(solution)/shard_map/ppermute | solution.py:542
  5.6 2.9 %collective-permute-start.4 = (f32[280,256]{1,0:T(8,128)S(1)}, f32[280,256]{1,0:T(8,128)S(1)}, u32[]{:S(2)}, u32[]{:S(2)}) collective-permute-start(f32[280,256]{1,0:T(8,128)S(1)} %get-tuple-element.22), channel_id=1, source_target_pairs={{0,1},{1,0},{2,3},{3,2},{4,5},{5,4},{6,7},{7,6},{8,9},{9,8},{10,11... | collective-permute-start | bytes 860168 | tf_op jit(solution)/shard_map/ppermute | solution.py:542
  8.5 0.1 collective-permute-start.10
  8.6 0.7 %collective-permute-start.9 = (f32[272,256]{1,0:T(8,128)S(1)}, f32[272,256]{1,0:T(8,128)S(1)}, u32[]{:S(2)}, u32[]{:S(2)}) collective-permute-start(f32[272,256]{1,0:T(8,128)S(1)} %get-tuple-element.24), channel_id=1, source_target_pairs={{1,2},{2,1},{5,6},{6,5},{9,10},{10,9},{13,14},{14,13},{17,18},{18,... | collective-permute-start | bytes 835592 | tf_op jit(solution)/shard_map/ppermute | solution.py:542
  9.3 2.1 %collective-permute-done.crossed_ref = f32[264,256]{1,0:T(8,128)S(1)} collective-permute-done((f32[264,256]{1,0:T(8,128)S(1)}, f32[264,256]{1,0:T(8,128)S(1)}, u32[]{:S(2)}, u32[]{:S(2)}) %collective-permute-start) | collective-permute-done | bytes 270368 | tf_op jit(solution)/shard_map/ppermute | solution.py:541
  11.4 0.0 copy-start.4
  11.4 1.7 %collective-permute-start.6 = (f32[256,256]{1,0:T(8,128)S(1)}, f32[256,256]{1,0:T(8,128)S(1)}, u32[]{:S(2)}, u32[]{:S(2)}) collective-permute-start(f32[256,256]{1,0:T(8,128)S(1)} %get-tuple-element.23), channel_id=1, source_target_pairs={{0,4},{4,0},{8,12},{12,8},{16,20},{20,16},{24,28},{28,24},{1,5},{5... | collective-permute-start | bytes 786440 | tf_op jit(solution)/shard_map/ppermute | solution.py:541
  13.2 0.0 collective-permute-done.10.refs_3_
  13.2 0.7 %collective-permute-start.1 = (f32[264,256]{1,0:T(8,128)S(1)}, f32[264,256]{1,0:T(8,128)S(1)}, u32[]{:S(2)}, u32[]{:S(2)}) collective-permute-start(f32[264,256]{1,0:T(8,128)S(1)} %collective-permute-done.crossed_ref), channel_id=1, source_target_pairs={{1,2},{2,1},{5,6},{6,5},{9,10},{10,9},{13,14},{14,13},{17,18},{18,... | collective-permute-start | bytes 811016 | tf_op jit(solution)/shard_map/ppermute | solution.py:548
  13.8 0.0 collective-permute-done.9.refs_2_
  13.9 3.4 %collective-permute-start.2 = (f32[264,256]{1,0:T(8,128)S(1)}, f32[264,256]{1,0:T(8,128)S(1)}, u32[]{:S(2)}, u32[]{:S(2)}) collective-permute-start(f32[264,256]{1,0:T(8,128)S(1)} %collective-permute-done.crossed_ref), channel_id=1, source_target_pairs={{0,1},{1,0},{2,3},{3,2},{4,5},{5,4},{6,7},{7,6},{8,9},{9,8},{10,11... | collective-permute-start | bytes 811016 | tf_op jit(solution)/shard_map/ppermute | solution.py:548
  17.2 0.0 collective-permute-done.3.own_outer_ref.refs_0_
  17.2 0.0 collective-permute-done.4.own_inner_ref.refs_1_
  17.2 0.0 copy-done.4
  17.2 0.3 shard_map.97.message_ref.refs_2_
  17.5 0.0 copy-start
  17.5 0.0 copy-start.3
  17.5 1.4 %collective-permute-start.12 = (f32[520,256]{1,0:T(8,128)S(1)}, f32[520,256]{1,0:T(8,128)S(1)}, u32[]{:S(2)}, u32[]{:S(2)}) collective-permute-start(f32[520,256]{1,0:T(8,128)S(1)} %shard_map.97.message_ref.refs_2_), channel_id=1, source_target_pairs={{4,12},{12,20},{20,28},{8,0},{16,8},{24,16},{5,13},{13,21},{21,29}... | collective-permute-start | bytes 1597448 | tf_op jit(solution)/shard_map/ppermute | solution.py:544
  19.0 0.3 collective-permute-done.6.crossed_ref
  19.3 0.7 %collective-permute-start.7 = (f32[256,256]{1,0:T(8,128)S(1)}, f32[256,256]{1,0:T(8,128)S(1)}, u32[]{:S(2)}, u32[]{:S(2)}) collective-permute-start(f32[256,256]{1,0:T(8,128)S(1)} %collective-permute-done.6.crossed_ref), channel_id=1, source_target_pairs={{1,2},{2,1},{5,6},{6,5},{9,10},{10,9},{13,14},{14,13},{17,18},{18,... | collective-permute-start | bytes 786440 | tf_op jit(solution)/shard_map/ppermute | solution.py:548
  19.9 2.5 %collective-permute-start.8 = (f32[256,256]{1,0:T(8,128)S(1)}, f32[256,256]{1,0:T(8,128)S(1)}, u32[]{:S(2)}, u32[]{:S(2)}) collective-permute-start(f32[256,256]{1,0:T(8,128)S(1)} %collective-permute-done.6.crossed_ref), channel_id=1, source_target_pairs={{0,1},{1,0},{2,3},{3,2},{4,5},{5,4},{6,7},{7,6},{8,9},{9,8},{10,11... | collective-permute-start | bytes 786440 | tf_op jit(solution)/shard_map/ppermute | solution.py:548
  22.5 0.0 collective-permute-done.1.outer_ref
  22.5 0.0 collective-permute-done.2.inner_ref
  22.5 0.3 shard_map.96.refs_0_.refs_1_
  22.7 3.5 %collective-permute-start.5 = (f32[264,256]{1,0:T(8,128)S(1)}, f32[264,256]{1,0:T(8,128)S(1)}, u32[]{:S(2)}, u32[]{:S(2)}) collective-permute-start(f32[264,256]{1,0:T(8,128)S(1)} %shard_map.96.refs_0_.refs_1_), channel_id=1, source_target_pairs={{12,4},{20,12},{28,20},{0,8},{8,16},{16,24},{13,5},{21,13},{29,21}... | collective-permute-start | bytes 811016 | tf_op jit(solution)/shard_map/ppermute | solution.py:553
  26.2 0.0 copy-done
  26.2 0.0 copy-done.3
  26.3 2.6 %shard_map.98 = (f32[2,256,256]{2,1,0:T(8,128)S(1)}, f32[2,256,256]{2,1,0:T(8,128)S(1)}, f32[2,256,256]{2,1,0:T(8,128)S(1)}) custom-call(f32[520,256]{1,0:T(8,128)S(1)} %shard_map.97.message_ref.refs_2_, f32[1,256,256]{2,1,0:T(8,128)S(1)} %copy-done, f32[1,256]{1,0:T(1,128)S(1)} %copy-done.3), custom_call_target="tpu_custom_call" | custom-call | tf_op jit(solution)/shard_map/pallas_call | solution.py:198
  28.9 0.0 collective-permute-done.7.outer_ref
  28.9 0.0 collective-permute-done.8.inner_ref
  28.9 0.3 shard_map.99.refs_1_.refs_2_
  29.2 3.7 %collective-permute-start.11 = (f32[256,256]{1,0:T(8,128)S(1)}, f32[256,256]{1,0:T(8,128)S(1)}, u32[]{:S(2)}, u32[]{:S(2)}) collective-permute-start(f32[256,256]{1,0:T(8,128)S(1)} %shard_map.99.refs_1_.refs_2_), channel_id=1, source_target_pairs={{12,4},{20,12},{28,20},{0,8},{8,16},{16,24},{13,5},{21,13},{29,21}... | collective-permute-start | bytes 786440 | tf_op jit(solution)/shard_map/ppermute | solution.py:553
  32.8 0.0 copy-start.1
  32.8 0.0 copy-start.2
  32.8 2.7 %shard_map.100 = (f32[2,256,256]{2,1,0:T(8,128)S(1)}, f32[2,256,256]{2,1,0:T(8,128)S(1)}, f32[2,256,256]{2,1,0:T(8,128)S(1)}, f32[2,256,256]{2,1,0:T(8,128)S(1)}) custom-call(f32[264,256]{1,0:T(8,128)S(1)} %shard_map.96.refs_0_.refs_1_, f32[256,256]{1,0:T(8,128)S(1)} %shard_map.99.refs_1_.refs_2_, f32[520,256]{1,0:T(8,128)S(1)} %shard_map.97.message_ref.refs_2_, ...), custom_call_target="tpu_custom_call" | custom-call | tf_op jit(solution)/shard_map/pallas_call | solution.py:198
  35.6 0.0 collective-permute-done.12.refs_0_
  35.6 0.0 copy-done.1
  35.6 0.0 copy-done.2
  35.6 4.8 %shard_map.101 = (f32[32,1,896]{2,1,0:T(1,128)S(1)}, f32[1,256]{1,0:T(1,128)S(1)}, f32[2,24,128]{2,1,0:T(8,128)S(1)}) custom-call(f32[520,256]{1,0:T(8,128)S(1)} %collective-permute-done.12.refs_0_, f32[264,256]{1,0:T(8,128)S(1)} %shard_map.96.refs_0_.refs_1_, f32[256,256]{1,0:T(8,128)S(1)} %shard_map.99.refs_1_.refs_2_, ...), custom_call_target="tpu_custom_call" | custom-call | tf_op jit(solution)/shard_map/pallas_call | solution.py:198
  40.4 0.0 collective-permute-done.11.refs_1_
  40.5 0.0 collective-permute-done.5.refs_0_
  40.5 4.7 %shard_map.102 = (f32[32,1,896]{2,1,0:T(1,128)S(1)}, f32[1,256]{1,0:T(1,128)S(1)}) custom-call(f32[264,256]{1,0:T(8,128)S(1)} %collective-permute-done.5.refs_0_, f32[256,256]{1,0:T(8,128)S(1)} %collective-permute-done.11.refs_1_, f32[520,256]{1,0:T(8,128)S(1)} %shard_map.97.message_ref.refs_2_, ...), custom_call_target="tpu_custom_call", output_to_operand_aliasing={{0}: (8, {})} | custom-call | tf_op jit(solution)/shard_map/pallas_call | solution.py:198
  45.2 11.0 %all_to_all.5 = f32[32,1,896]{2,1,0:T(1,128)S(1)} all-to-all(f32[32,1,896]{2,1,0:T(1,128)S(1)} %get-tuple-element.37), channel_id=1, replica_groups=mesh['energy'=8,'slab'=4] {'energy','slab'}, dimensions={0} | all-to-all | bytes 229376 | tf_op jit(solution)/shard_map/all_to_all | solution.py:563
  56.2 0.9 %shard_map.103 = (f32[1,2,256]{2,1,0:T(2,128)}, f32[1,16,128]{2,1,0:T(8,128)}) custom-call(f32[8,4,1,896]{3,2,1,0:T(1,128)S(1)} %bitcast.1, f32[1,256]{1,0:T(1,128)S(1)} %get-tuple-element.38.own_ref, f32[2,24,128]{2,1,0:T(8,128)S(1)} %get-tuple-element.39.local_ref), custom_call_target="tpu_custom_call" | custom-call | tf_op jit(solution)/shard_map/pallas_call | solution.py:198
Async XLA Ops:
  1.9 9.5 %collective-permute-start = (f32[264,256]{1,0:T(8,128)S(1)}, f32[264,256]{1,0:T(8,128)S(1)}, u32[]{:S(2)}, u32[]{:S(2)}) collective-permute-start(f32[264,256]{1,0:T(8,128)S(1)} %get-tuple-element.21), channel_id=1, source_target_pairs={{0,4},{4,0},{8,12},{12,8},{16,20},{20,16},{24,28},{28,24},{1,5},{5... | collective-permute-start | bytes 811016 | tf_op jit(solution)/shard_map/ppermute | solution.py:541
  4.9 12.3 %collective-permute-start.3 = (f32[280,256]{1,0:T(8,128)S(1)}, f32[280,256]{1,0:T(8,128)S(1)}, u32[]{:S(2)}, u32[]{:S(2)}) collective-permute-start(f32[280,256]{1,0:T(8,128)S(1)} %get-tuple-element.22), channel_id=1, source_target_pairs={{1,2},{2,1},{5,6},{6,5},{9,10},{10,9},{13,14},{14,13},{17,18},{18,... | collective-permute-start | bytes 860168 | tf_op jit(solution)/shard_map/ppermute | solution.py:542
  5.6 11.6 %collective-permute-start.4 = (f32[280,256]{1,0:T(8,128)S(1)}, f32[280,256]{1,0:T(8,128)S(1)}, u32[]{:S(2)}, u32[]{:S(2)}) collective-permute-start(f32[280,256]{1,0:T(8,128)S(1)} %get-tuple-element.22), channel_id=1, source_target_pairs={{0,1},{1,0},{2,3},{3,2},{4,5},{5,4},{6,7},{7,6},{8,9},{9,8},{10,11... | collective-permute-start | bytes 860168 | tf_op jit(solution)/shard_map/ppermute | solution.py:542
  8.5 4.6 %collective-permute-start.10 = (f32[272,256]{1,0:T(8,128)S(1)}, f32[272,256]{1,0:T(8,128)S(1)}, u32[]{:S(2)}, u32[]{:S(2)}) collective-permute-start(f32[272,256]{1,0:T(8,128)S(1)} %get-tuple-element.24), channel_id=1, source_target_pairs={{0,1},{1,0},{2,3},{3,2},{4,5},{5,4},{6,7},{7,6},{8,9},{9,8},{10,11... | collective-permute-start | bytes 835592 | tf_op jit(solution)/shard_map/ppermute | solution.py:542
  8.6 5.2 %collective-permute-start.9 = (f32[272,256]{1,0:T(8,128)S(1)}, f32[272,256]{1,0:T(8,128)S(1)}, u32[]{:S(2)}, u32[]{:S(2)}) collective-permute-start(f32[272,256]{1,0:T(8,128)S(1)} %get-tuple-element.24), channel_id=1, source_target_pairs={{1,2},{2,1},{5,6},{6,5},{9,10},{10,9},{13,14},{14,13},{17,18},{18,... | collective-permute-start | bytes 835592 | tf_op jit(solution)/shard_map/ppermute | solution.py:542
  11.4 5.8 %copy-start.4 = (f32[1,256]{1,0:T(1,128)S(1)}, f32[1,256]{1,0:T(1,128)}, u32[]{:S(2)}) copy-start(f32[1,256]{1,0:T(1,128)} %coupling_ref.5) | copy-start | bytes 3076
  11.4 7.8 %collective-permute-start.6 = (f32[256,256]{1,0:T(8,128)S(1)}, f32[256,256]{1,0:T(8,128)S(1)}, u32[]{:S(2)}, u32[]{:S(2)}) collective-permute-start(f32[256,256]{1,0:T(8,128)S(1)} %get-tuple-element.23), channel_id=1, source_target_pairs={{0,4},{4,0},{8,12},{12,8},{16,20},{20,16},{24,28},{28,24},{1,5},{5... | collective-permute-start | bytes 786440 | tf_op jit(solution)/shard_map/ppermute | solution.py:541
  13.2 9.3 %collective-permute-start.1 = (f32[264,256]{1,0:T(8,128)S(1)}, f32[264,256]{1,0:T(8,128)S(1)}, u32[]{:S(2)}, u32[]{:S(2)}) collective-permute-start(f32[264,256]{1,0:T(8,128)S(1)} %collective-permute-done.crossed_ref), channel_id=1, source_target_pairs={{1,2},{2,1},{5,6},{6,5},{9,10},{10,9},{13,14},{14,13},{17,18},{18,... | collective-permute-start | bytes 811016 | tf_op jit(solution)/shard_map/ppermute | solution.py:548
  13.9 8.6 %collective-permute-start.2 = (f32[264,256]{1,0:T(8,128)S(1)}, f32[264,256]{1,0:T(8,128)S(1)}, u32[]{:S(2)}, u32[]{:S(2)}) collective-permute-start(f32[264,256]{1,0:T(8,128)S(1)} %collective-permute-done.crossed_ref), channel_id=1, source_target_pairs={{0,1},{1,0},{2,3},{3,2},{4,5},{5,4},{6,7},{7,6},{8,9},{9,8},{10,11... | collective-permute-start | bytes 811016 | tf_op jit(solution)/shard_map/ppermute | solution.py:548
  17.5 8.7 %copy-start = (f32[1,256,256]{2,1,0:T(8,128)S(1)}, f32[1,256,256]{2,1,0:T(8,128)}, u32[]{:S(2)}) copy-start(f32[1,256,256]{2,1,0:T(8,128)} %refs_5_.3) | copy-start | bytes 786436
  17.5 8.7 %copy-start.3 = (f32[1,256]{1,0:T(1,128)S(1)}, f32[1,256]{1,0:T(1,128)}, u32[]{:S(2)}) copy-start(f32[1,256]{1,0:T(1,128)} %refs_6_.5) | copy-start | bytes 3076
  17.5 18.1 %collective-permute-start.12 = (f32[520,256]{1,0:T(8,128)S(1)}, f32[520,256]{1,0:T(8,128)S(1)}, u32[]{:S(2)}, u32[]{:S(2)}) collective-permute-start(f32[520,256]{1,0:T(8,128)S(1)} %shard_map.97.message_ref.refs_2_), channel_id=1, source_target_pairs={{4,12},{12,20},{20,28},{8,0},{16,8},{24,16},{5,13},{13,21},{21,29}... | collective-permute-start | bytes 1597448 | tf_op jit(solution)/shard_map/ppermute | solution.py:544
  19.3 9.6 %collective-permute-start.7 = (f32[256,256]{1,0:T(8,128)S(1)}, f32[256,256]{1,0:T(8,128)S(1)}, u32[]{:S(2)}, u32[]{:S(2)}) collective-permute-start(f32[256,256]{1,0:T(8,128)S(1)} %collective-permute-done.6.crossed_ref), channel_id=1, source_target_pairs={{1,2},{2,1},{5,6},{6,5},{9,10},{10,9},{13,14},{14,13},{17,18},{18,... | collective-permute-start | bytes 786440 | tf_op jit(solution)/shard_map/ppermute | solution.py:548
  19.9 8.9 %collective-permute-start.8 = (f32[256,256]{1,0:T(8,128)S(1)}, f32[256,256]{1,0:T(8,128)S(1)}, u32[]{:S(2)}, u32[]{:S(2)}) collective-permute-start(f32[256,256]{1,0:T(8,128)S(1)} %collective-permute-done.6.crossed_ref), channel_id=1, source_target_pairs={{0,1},{1,0},{2,3},{3,2},{4,5},{5,4},{6,7},{7,6},{8,9},{9,8},{10,11... | collective-permute-start | bytes 786440 | tf_op jit(solution)/shard_map/ppermute | solution.py:548
  22.7 17.7 %collective-permute-start.5 = (f32[264,256]{1,0:T(8,128)S(1)}, f32[264,256]{1,0:T(8,128)S(1)}, u32[]{:S(2)}, u32[]{:S(2)}) collective-permute-start(f32[264,256]{1,0:T(8,128)S(1)} %shard_map.96.refs_0_.refs_1_), channel_id=1, source_target_pairs={{12,4},{20,12},{28,20},{0,8},{8,16},{16,24},{13,5},{21,13},{29,21}... | collective-permute-start | bytes 811016 | tf_op jit(solution)/shard_map/ppermute | solution.py:553
  29.2 11.3 %collective-permute-start.11 = (f32[256,256]{1,0:T(8,128)S(1)}, f32[256,256]{1,0:T(8,128)S(1)}, u32[]{:S(2)}, u32[]{:S(2)}) collective-permute-start(f32[256,256]{1,0:T(8,128)S(1)} %shard_map.99.refs_1_.refs_2_), channel_id=1, source_target_pairs={{12,4},{20,12},{28,20},{0,8},{8,16},{16,24},{13,5},{21,13},{29,21}... | collective-permute-start | bytes 786440 | tf_op jit(solution)/shard_map/ppermute | solution.py:553
  32.8 2.8 %copy-start.1 = (s32[1,128,128]{2,1,0:T(8,128)S(1)}, s32[1,128,128]{2,1,0:T(8,128)}, u32[]{:S(2)}) copy-start(s32[1,128,128]{2,1,0:T(8,128)} %refs_7_.3) | copy-start | bytes 196612
  32.8 2.8 %copy-start.2 = (f32[1,128,128]{2,1,0:T(8,128)S(1)}, f32[1,128,128]{2,1,0:T(8,128)}, u32[]{:S(2)}) copy-start(f32[1,128,128]{2,1,0:T(8,128)} %refs_8_.1) | copy-start | bytes 196612
